TPU v7x, 128 devices: a whole 4x4x4 slice. The times are simulated.
128 devices in a mesh: row: 16 (over y, z_hi, core), col: 8 (over x, z_lo).
Axes of the slice: x: 4, y: 4, z: 4 (z_hi: 2, z_lo: 2; z = z_hi * 2 + z_lo), core: 2. Of those that a mesh axis runs over, the one named last changes fastest.
Arguments:
- tokens: bfloat16 [6144, 4096], P('row', 'col'), may hold values from -6 to 6
- cotangent: bfloat16 [6144, 4096], P('row', 'col'), may hold values from -6 to 6
- gate_blocks: bfloat16 [32, 32, 128, 128], P('row', 'col'), may hold values from -0.1875 to 0.1875
- up_blocks: bfloat16 [32, 32, 128, 128], P('row', 'col'), may hold values from -0.1875 to 0.1875
- down_blocks: bfloat16 [32, 32, 128, 128], P('row', 'col'), may hold values from -0.09375 to 0.09375
- gate_cols: int32 [32, 32], P('row', 'col'), may hold values from 0 to 127, as said below
- up_cols: int32 [32, 32], P('row', 'col'), may hold values from 0 to 127, as said below
- down_cols: int32 [32, 32], P('row', 'col'), may hold values from 0 to 127, as said below
Outputs:
- output: bfloat16 [6144, 4096], P('row', 'col')
- tokens_grad: bfloat16 [6144, 4096], P('row', 'col')
- gate_grad: bfloat16 [32, 32, 128, 128], P('row', 'col')
- up_grad: bfloat16 [32, 32, 128, 128], P('row', 'col')
- down_grad: bfloat16 [32, 32, 128, 128], P('row', 'col')
Inputs may be any that keep to these rules, and one draw needn't show every extreme that they name: In every block row of gate_cols, slots c * 4 to c * 4 + 3 hold 4 different block columns, all in c * 16 to c * 16 + 15. In every block row of up_cols, slots c * 4 to c * 4 + 3 hold 4 different block columns, all in c * 16 to c * 16 + 15. In every block row of down_cols, slots c * 4 to c * 4 + 3 hold 4 different block columns, all in c * 16 to c * 16 + 15.
All inputs are finite; a program needn't handle non-finite values.
Results may differ from a plain program's by a relative error of at most 0.022.
Values may be sent and summed in bfloat16 or wider, within the bound.
No kernel may reach another device: no remote copies, remote signals or barrier semaphores. Data moves between devices by JAX's collectives and lax.ppermute only.
A program may use at most 256 MiB of HBM per device.

v0:
```python
import jax
import jax.numpy as jnp
from jax import lax
from jax.sharding import PartitionSpec as P


def spread_columns(products, columns, local_width):
    tok_rows = products.shape[0]
    flat = products.reshape(tok_rows, -1, products.shape[3])
    empty = jnp.zeros((tok_rows, local_width, products.shape[3]), jnp.float32)
    return empty.at[:, columns.reshape(-1)].add(flat)


def body(tokens, cotangent, gate_blocks, up_blocks, down_blocks, gate_cols, up_cols, down_cols):
    local_rows = gate_blocks.shape[0]
    local_slots = gate_blocks.shape[1]
    block_size = gate_blocks.shape[2]
    local_width = 4 * local_slots
    offset = lax.axis_index("col") * local_width
    tok_rows = tokens.shape[0]
    features, cot_features = (
        lax.all_gather(tokens, "col", axis=1, tiled=True),
        lax.all_gather(cotangent, "col", axis=1, tiled=True),
    )
    blocks_all = features.shape[1] // block_size
    feature_blocks = features.reshape(tok_rows, blocks_all, block_size)
    cotangent_blocks = cot_features.reshape(tok_rows, blocks_all, block_size)
    gate_vals = lax.all_gather(gate_blocks, "row", axis=0, tiled=True)
    up_vals = lax.all_gather(up_blocks, "row", axis=0, tiled=True)
    gate_piece = lax.all_gather(gate_cols.astype(jnp.bfloat16), "row", axis=0, tiled=True)
    up_piece = lax.all_gather(up_cols.astype(jnp.bfloat16), "row", axis=0, tiled=True)
    inputs = feature_blocks
    gate_local = gate_piece.astype(jnp.int32) - offset
    up_local = up_piece.astype(jnp.int32) - offset
    gate_products = jnp.einsum(
        "tkd,kjde->tkje", inputs, gate_vals, preferred_element_type=jnp.float32
    )
    up_products = jnp.einsum("tkd,kjde->tkje", inputs, up_vals, preferred_element_type=jnp.float32)
    gate_acc = spread_columns(gate_products, gate_local, local_width)
    up_acc = spread_columns(up_products, up_local, local_width)
    gate_gate_idx = gate_local
    gate_up_idx = up_local
    gate_acc, up_acc, gate_idx, up_idx = (gate_acc, up_acc, gate_gate_idx, gate_up_idx)
    silu_gate = jax.nn.silu(gate_acc)
    hidden_blocks = (silu_gate * up_acc).astype(jnp.bfloat16)
    down_vals = lax.all_gather(down_blocks, "row", axis=0, tiled=True)
    down_piece = lax.all_gather(down_cols.astype(jnp.bfloat16), "row", axis=0, tiled=True)
    down_local = down_piece.astype(jnp.int32) - offset
    chosen = jnp.take(hidden_blocks, down_local, axis=1)
    partial_value = jnp.einsum(
        "tkje,kjde->tkd", chosen, down_vals, preferred_element_type=jnp.float32
    )
    out_acc = partial_value
    down_down_idx = down_local
    out_acc, down_idx = (out_acc, down_down_idx)
    output = lax.psum_scatter(
        out_acc.reshape(tok_rows, -1).astype(jnp.bfloat16), "col", scatter_dimension=1, tiled=True
    )
    inputs = cotangent_blocks
    products = jnp.einsum(
        "tkd,kjde->tkje",
        inputs,
        lax.all_gather(down_blocks, "row", axis=0, tiled=True),
        preferred_element_type=jnp.float32,
    )
    hidden_grad = spread_columns(products, down_idx, local_width)
    sigmoid_gate = jax.nn.sigmoid(gate_acc)
    up_delta = (hidden_grad * silu_gate).astype(jnp.bfloat16)
    gate_delta = (
        hidden_grad * up_acc * sigmoid_gate * (1.0 + gate_acc * (1.0 - sigmoid_gate))
    ).astype(jnp.bfloat16)
    gate_vals = lax.all_gather(gate_blocks, "row", axis=0, tiled=True)
    up_vals = lax.all_gather(up_blocks, "row", axis=0, tiled=True)
    gate_local = gate_idx
    up_local = up_idx
    partial_value = jnp.einsum(
        "tkje,kjde->tkd",
        jnp.take(gate_delta, gate_local, axis=1),
        gate_vals,
        preferred_element_type=jnp.float32,
    )
    partial_value = partial_value + jnp.einsum(
        "tkje,kjde->tkd",
        jnp.take(up_delta, up_local, axis=1),
        up_vals,
        preferred_element_type=jnp.float32,
    )
    tokens_grad = lax.psum_scatter(
        partial_value.reshape(tok_rows, -1).astype(jnp.bfloat16),
        "col",
        scatter_dimension=1,
        tiled=True,
    )
    grad_scale = float(tok_rows * lax.axis_size("row")) ** (-0.5)
    groups = local_rows * lax.axis_size("row") // local_rows

    def one_group(group_index):
        group_first = group_index * local_rows
        inputs = lax.dynamic_slice_in_dim(feature_blocks, group_first, local_rows, 1)
        cot_inputs = lax.dynamic_slice_in_dim(cotangent_blocks, group_first, local_rows, 1)
        gate_local = lax.dynamic_slice_in_dim(gate_idx, group_first, local_rows, 0)
        up_local = lax.dynamic_slice_in_dim(up_idx, group_first, local_rows, 0)
        down_local = lax.dynamic_slice_in_dim(down_idx, group_first, local_rows, 0)
        gate_term = jnp.einsum(
            "tkd,tkje->kjde",
            inputs,
            jnp.take(gate_delta, gate_local, axis=1),
            preferred_element_type=jnp.float32,
        )
        up_term = jnp.einsum(
            "tkd,tkje->kjde",
            inputs,
            jnp.take(up_delta, up_local, axis=1),
            preferred_element_type=jnp.float32,
        )
        down_term = jnp.einsum(
            "tkd,tkje->kjde",
            cot_inputs,
            jnp.take(hidden_blocks, down_local, axis=1),
            preferred_element_type=jnp.float32,
        )
        return jnp.stack([gate_term, up_term, down_term], axis=1) * grad_scale

    stacked = lax.map(one_group, jnp.arange(groups, dtype=jnp.int32))
    weight_grads = lax.psum_scatter(
        stacked.reshape((local_rows * lax.axis_size("row"),) + stacked.shape[2:]).astype(
            jnp.bfloat16
        ),
        "row",
        scatter_dimension=0,
        tiled=True,
    ).astype(jnp.float32)
    gate_grad = weight_grads[:, 0].astype(jnp.bfloat16)
    up_grad = weight_grads[:, 1].astype(jnp.bfloat16)
    down_grad = weight_grads[:, 2].astype(jnp.bfloat16)
    return (output, tokens_grad, gate_grad, up_grad, down_grad)


def solution(mesh):
    in_specs = (
        P("row", "col"),
        P("row", "col"),
        P("row", "col", None, None),
        P("row", "col", None, None),
        P("row", "col", None, None),
        P("row", "col"),
        P("row", "col"),
        P("row", "col"),
    )
    out_specs = (
        P("row", "col"),
        P("row", "col"),
        P("row", "col", None, None),
        P("row", "col", None, None),
        P("row", "col", None, None),
    )
    return jax.shard_map(body, mesh=mesh, in_specs=in_specs, out_specs=out_specs, check_vma=False)
```

profile of v0, /device:TPU:0, one launch (start us, length us, event | category | flops | bytes accessed | tf_op | source)
XLA Modules:
  0.0 1249.0 jit_solution(13534747205828137103)
XLA Ops:
  14.0 28.1 %all-gather = bf16[16,2,4]{2,1,0:T(2,128)(2,1)S(1)} all-gather(bf16[1,2,4]{2,1,0:T(2,128)(2,1)S(1)} %convert_bitcast_fusion.2), channel_id=1, replica_groups=mesh['row'=16,'col'=8] {'row'}, dimensions={0}, use_global_device_ids=true | all-gather | bytes 272 | tf_op jit(solution)/shard_map/all_gather | solution.py:30
  42.9 19.3 %all-gather.1 = bf16[16,2,4]{2,1,0:T(2,128)(2,1)S(1)} all-gather(bf16[1,2,4]{2,1,0:T(2,128)(2,1)S(1)} %convert_bitcast_fusion.1), channel_id=1, replica_groups=mesh['row'=16,'col'=8] {'row'}, dimensions={0}, use_global_device_ids=true | all-gather | bytes 272 | tf_op jit(solution)/shard_map/all_gather | solution.py:31
  63.0 22.3 %all-gather.2 = bf16[16,2,4]{2,1,0:T(2,128)(2,1)S(1)} all-gather(bf16[1,2,4]{2,1,0:T(2,128)(2,1)S(1)} %convert_bitcast_fusion), channel_id=1, replica_groups=mesh['row'=16,'col'=8] {'row'}, dimensions={0}, use_global_device_ids=true | all-gather | bytes 272 | tf_op jit(solution)/shard_map/all_gather | solution.py:47
  85.4 57.2 %all-gather.9.cloned.1.call-done = bf16[32,4,128,128]{3,2,1,0:T(8,128)(2,1)} async-done(((bf16[2,4,128,128]{3,2,1,0:T(8,128)(2,1)}), bf16[32,4,128,128]{3,2,1,0:T(8,128)(2,1)}) %all-gather.9.cloned.1.call-update) | async-done | bytes 4194320 | tf_op jit(solution)/shard_map/all_gather | solution.py:28
  142.6 15.2 %fusion.52 = f32[32,4,128,384]{3,2,1,0:T(8,128)} fusion(bf16[32,4,128,128]{3,2,1,0:T(8,128)(2,1)} %all-gather.9.cloned.1.call-done, bf16[384,32,128,1]{0,2,3,1:T(8,128)(2,1)} %bitcast.176), kind=kOutput, calls=%fused_computation.100 | convolution fusion | flops 1610612736 | bytes 32505856 | tf_op jit(solution)/shard_map/tkd,kjde->tkje/dot_general | solution.py:35
  157.8 25.0 %copy.57 = f32[384,128,128]{2,0,1:T(8,128)} copy(f32[384,128,128]{0,2,1:T(8,128)} %bitcast.166) | data formatting | bytes 50331648 | tf_op jit(solution)/shard_map/reshape | solution.py:9
  182.8 16.9 %all-gather.13.cloned.1.call-done = bf16[32,4,128,128]{3,2,1,0:T(8,128)(2,1)} async-done(((bf16[2,4,128,128]{3,2,1,0:T(8,128)(2,1)}), bf16[32,4,128,128]{3,2,1,0:T(8,128)(2,1)}) %all-gather.13.cloned.1.call-update) | async-done | bytes 4194320 | tf_op jit(solution)/shard_map/all_gather | solution.py:29
  199.7 14.1 %fusion.53 = f32[32,4,128,384]{3,2,1,0:T(8,128)} fusion(bf16[32,4,128,128]{3,2,1,0:T(8,128)(2,1)} %all-gather.13.cloned.1.call-done, bf16[384,32,128,1]{0,2,3,1:T(8,128)(2,1)S(1)} %bitcast.178), kind=kOutput, calls=%fused_computation.101 | convolution fusion | flops 1610612736 | bytes 32505856 | tf_op jit(solution)/shard_map/tkd,kjde->tkje/dot_general | solution.py:38
  213.8 24.8 %copy.60 = f32[384,128,128]{2,0,1:T(8,128)} copy(f32[384,128,128]{0,2,1:T(8,128)} %bitcast.167) | data formatting | bytes 50331648 | tf_op jit(solution)/shard_map/reshape | solution.py:9
  238.6 32.0 %all-gather.17.cloned.1.call-done = bf16[384,4096]{0,1:T(8,128)(2,1)} async-done(((bf16[384,512]{0,1:T(8,128)(2,1)}), bf16[384,4096]{0,1:T(8,128)(2,1)}) %all-gather.17.cloned.1.call-update) | async-done | bytes 3145744 | tf_op jit(solution)/shard_map/all_gather | solution.py:23
  270.6 59.5 %all-gather.15.cloned.1.call-done = bf16[32,4,128,128]{3,2,1,0:T(8,128)(2,1)} async-done(((bf16[2,4,128,128]{3,2,1,0:T(8,128)(2,1)}), bf16[32,4,128,128]{3,2,1,0:T(8,128)(2,1)}) %all-gather.15.cloned.1.call-update) | async-done | bytes 4194320 | tf_op jit(solution)/shard_map/all_gather | solution.py:46
  330.0 14.9 %fusion.54 = f32[32,4,128,384]{3,2,1,0:T(8,128)} fusion(bf16[32,4,128,128]{3,2,1,0:T(8,128)(2,1)} %all-gather.15.cloned.1.call-done, bf16[384,32,128,1]{0,2,3,1:T(8,128)(2,1)} %bitcast.182), kind=kOutput, calls=%fused_computation.102 | convolution fusion | flops 1610612736 | bytes 32505856 | tf_op jit(solution)/shard_map/tkd,kjde->tkje/dot_general | solution.py:60
  345.0 24.7 %copy.65 = f32[384,128,128]{2,0,1:T(8,128)} copy(f32[384,128,128]{0,2,1:T(8,128)} %bitcast.168) | data formatting | bytes 50331648 | tf_op jit(solution)/shard_map/reshape | solution.py:9
  370.0 38.7 %scatter_fusion = f32[384,16,128]{2,0,1:T(8,128)S(1)} fusion(f32[384,16,128]{2,0,1:T(8,128)S(1)} %broadcast.80.clone, s32[128]{0:T(128)S(1)} %fusion.46, f32[128,384,128]{2,1,0:T(8,128)} %bitcast.169), kind=kCustom, calls=%fused_computation.6 | custom fusion | flops 6291456 | bytes 75497984 | tf_op jit(solution)/shard_map/scatter-add | solution.py:11
  410.9 62.6 %scatter_fusion.1 = f32[384,16,128]{2,0,1:T(8,128)} fusion(f32[384,16,128]{2,0,1:T(8,128)} %broadcast.80.clone.2, s32[128]{0:T(128)S(1)} %fusion.47, f32[128,384,128]{2,1,0:T(8,128)} %bitcast.170), kind=kCustom, calls=%fused_computation.7 | custom fusion | flops 6291456 | bytes 75497984 | tf_op jit(solution)/shard_map/scatter-add | solution.py:11
  473.8 38.7 %scatter_fusion.2 = f32[384,16,128]{2,0,1:T(8,128)S(1)} fusion(f32[384,16,128]{2,0,1:T(8,128)S(1)} %broadcast.80.clone.1, s32[128]{0:T(128)S(1)} %fusion.48, f32[128,384,128]{2,1,0:T(8,128)} %bitcast.171), kind=kCustom, calls=%fused_computation.8 | custom fusion | flops 6291456 | bytes 75497984 | tf_op jit(solution)/shard_map/scatter-add | solution.py:11
  518.3 278.2 %while.10 = (s32[]{:T(128)}, bf16[16,2,3,4,128,128]{4,5,3,1,2,0:T(8,128)(2,1)}, s32[16]{0:T(128)S(1)}, s32[32,4]{1,0:T(8,128)S(1)}, bf16[384,16,128]{2,0,1:T(8,1...) while((s32[]{:T(128)}, ...), condition=%wide.region_6.9_spmd, body=%wide.region_5.8_spmd.sunk | while | flops 304352384 | bytes 31798688 | solution.py:124
  796.5 16.6 %copy.69 = bf16[16,2,3,4,128,128]{5,4,3,1,0,2:T(8,128)(2,1)} copy(bf16[16,2,3,4,128,128]{4,5,3,1,2,0:T(8,128)(2,1)} %get-tuple-element.64) | data formatting | bytes 25165824 | tf_op jit(solution)/shard_map/convert_element_type | solution.py:126
  814.5 8.5 gather_fusion.5
  823.1 8.6 gather_fusion.4
  853.0 8.8 gather_fusion.3
  874.2 216.5 %all-reduce.3.cloned.1.call-done = bf16[32,3,4,128,128]{4,3,2,0,1:T(8,128)(2,1)} async-done(((bf16[32,3,4,128,128]{4,3,2,0,1:T(8,128)(2,1)}), bf16[32,3,4,128,128]{4,3,2,0,1:T(8,128)(2,1)}) %all-reduce.3.cloned.1.call-update) | async-done | bytes 12582928
  1092.7 75.0 %reduce-scatter.8.cloned.1.call-done = bf16[384,512]{1,0:T(8,128)(2,1)} async-done(((bf16[384,4096]{1,0:T(8,128)(2,1)}), bf16[384,512]{1,0:T(8,128)(2,1)}) %reduce-scatter.8.cloned.1.call-update) | async-done | bytes 393232 | tf_op jit(solution)/shard_map/reduce_scatter | solution.py:88
  1167.7 74.5 %reduce-scatter.6.cloned.1.call-done = bf16[384,512]{1,0:T(8,128)(2,1)} async-done(((bf16[384,4096]{1,0:T(8,128)(2,1)}), bf16[384,512]{1,0:T(8,128)(2,1)}) %reduce-scatter.6.cloned.1.call-update) | async-done | bytes 393232 | tf_op jit(solution)/shard_map/reduce_scatter | solution.py:56
  (482 shorter events, 320.1 us)
Async XLA Ops:
  7.2 78.2 %all-gather.11.cloned.1.call-start = ((), (), s32[]{:S(2)}) async-start(), calls=%async_computation.3 | async-start | bytes 3538944 | tf_op jit(solution)/shard_map/all_gather | solution.py:22
  9.1 133.4 %all-gather.9.cloned.1.call-start = ((), (), s32[]{:S(2)}) async-start(), calls=%async_computation.2 | async-start | bytes 4456448 | tf_op jit(solution)/shard_map/all_gather | solution.py:28
  9.9 189.8 %all-gather.13.cloned.1.call-start = ((), (), s32[]{:S(2)}) async-start(), calls=%async_computation.4 | async-start | bytes 4456448 | tf_op jit(solution)/shard_map/all_gather | solution.py:29
  10.6 259.9 %all-gather.17.cloned.1.call-start = ((), (), s32[]{:S(2)}) async-start(), calls=%async_computation.7 | async-start | bytes 3538944 | tf_op jit(solution)/shard_map/all_gather | solution.py:23
  12.6 317.4 %all-gather.15.cloned.1.call-start = ((), (), s32[]{:S(2)}) async-start(), calls=%async_computation.5 | async-start | bytes 4456448 | tf_op jit(solution)/shard_map/all_gather | solution.py:46
  13.2 1077.5 %all-reduce.3.cloned.1.call-start = ((), (), s32[]{:S(2)}) async-start(), calls=%async_computation.9 | async-start | bytes 25165824
  42.1 43.1 %copy-start.11 = (s32[4,8,4]{2,1,0:T(8,128)}, s32[4,8,4]{2,1,0:T(8,128)S(1)}, u32[]{:S(2)}) copy-start(s32[4,8,4]{2,1,0:T(8,128)S(1)} %convert_subtract_fusion.2) | copy-start | bytes 1540
  62.2 95.6 %copy-start.13 = (s32[4,8,4]{2,1,0:T(8,128)}, s32[4,8,4]{2,1,0:T(8,128)S(1)}, u32[]{:S(2)}) copy-start(s32[4,8,4]{2,1,0:T(8,128)S(1)} %convert_subtract_fusion.1) | copy-start | bytes 1540
  85.2 72.6 %copy-start.9 = (s32[4,8,4]{2,1,0:T(8,128)}, s32[4,8,4]{2,1,0:T(8,128)S(1)}, u32[]{:S(2)}) copy-start(s32[4,8,4]{2,1,0:T(8,128)S(1)} %convert_subtract_fusion) | copy-start | bytes 1540
  157.8 41.9 %copy-start.6 = (bf16[384,4096]{0,1:T(8,128)(2,1)S(1)}, bf16[384,4096]{0,1:T(8,128)(2,1)}, u32[]{:S(2)}) copy-start(bf16[384,4096]{0,1:T(8,128)(2,1)} %all-gather.11.cloned.1.call-done) | copy-start | bytes 9437188
  408.6 64.9 %copy-start = (f32[384,16,128]{2,0,1:T(8,128)}, f32[384,16,128]{2,0,1:T(8,128)S(1)}, u32[]{:S(2)}) copy-start(f32[384,16,128]{2,0,1:T(8,128)S(1)} %scatter_fusion) | copy-start | bytes 9437188
  522.6 9.5 copy-start.1
  540.0 9.5 copy-start.1
  557.4 9.5 copy-start.1
  574.8 9.5 copy-start.1
  609.5 9.5 copy-start.1
  626.9 9.5 copy-start.1
  661.6 9.5 copy-start.1
  696.4 9.5 copy-start.1
  713.8 9.5 copy-start.1
  731.2 9.5 copy-start.1
  748.6 9.5 copy-start.1
  813.2 354.5 %reduce-scatter.8.cloned.1.call-start = ((), (), s32[]{:S(2)}) async-start(), calls=%async_computation.8 | async-start | bytes 3538944 | tf_op jit(solution)/shard_map/reduce_scatter | solution.py:88
  852.8 389.4 %reduce-scatter.6.cloned.1.call-start = ((), (), s32[]{:S(2)}) async-start(), calls=%async_computation.6 | async-start | bytes 3538944 | tf_op jit(solution)/shard_map/reduce_scatter | solution.py:56
  (45 other events, 326.0 us)
Sparse Core Ops, SparseCore 0:
  10.2 72.7 all-gather.10
  85.4 57.0 all-gather.8
  145.0 54.6 all-gather.12
  201.8 68.7 all-gather.16
  272.8 57.1 all-gather.14
  813.3 277.3 all-reduce.2
  1093.7 73.9 reduce-scatter.7
  1170.6 71.5 reduce-scatter.5
where the time goes:
time: 1260 us; the launch traced here: 1250 us
  waiting for transfers between devices  534 us (42%)
  local copies, waits for them, and re-layouts  302 us (24%)
  other arithmetic  167 us (13%)
  matrix products  150 us (12%)
  blocking collectives  69.6 us (6%)
  between operations  15.1 us (1%)
    unnamed x9, waiting for transfers between devices  219 us
    scatter-add x3, other arithmetic, spread_columns(): return empty.at[:, columns.reshape(-1)].add(flat)  140 us
    gather x32, local copies, waits for them, and re-layouts, one_group(): jnp.take(up_delta, up_local, axis=1)  86.3 us
    reduce_scatter x1, waiting for transfers between devices, body(): lax.psum_scatter(partial_value.reshape(tok_rows, -1).astype(jnp.bfloat16)...  75 us
    reduce_scatter x1, waiting for transfers between devices, body(): lax.psum_scatter(out_acc.reshape(tok_rows, -1).astype(jnp.bfloat16), 'col...  74.5 us
    reshape x3, local copies, waits for them, and re-layouts, spread_columns(): flat = products.reshape(tok_rows, -1, products.shape[3])  74.5 us
    all_gather x1, waiting for transfers between devices, body(): down_vals = lax.all_gather(down_blocks, 'row', axis=0, tiled=True)  59.5 us
    all_gather x1, waiting for transfers between devices, body(): gate_vals = lax.all_gather(gate_blocks, 'row', axis=0, tiled=True)  57.2 us
  transfers between devices with their start and end apart: 8, of which 7 were waited for; matrix products, arithmetic and copies ran while one was open for 12% of the time, Pallas kernels for 0%

commit v1 on v0

v1 whole, which is shorter than its diff:
```python
import functools

import jax
import jax.numpy as jnp
from jax import lax
from jax.experimental import pallas as pl
from jax.experimental.pallas import tpu as pltpu
from jax.sharding import PartitionSpec as P

BLK = 128
NZ = 4
FB_DEV = 16
X_SIZE = 4
VMEM_BYTES = 56 * 1024 * 1024
NT = (((1,), (1,)), ((), ()))
TN = (((0,), (0,)), ((), ()))


def lanes(values):
    return jnp.concatenate(values, axis=1)


def sums_kernel(order, cols, x_ref, w_ref, hidden_ref, gate_delta_ref, up_delta_ref, acc):
    step = pl.program_id(0)
    tok_rows = hidden_ref.shape[1]

    @pl.when(step == 0)
    def _():
        acc[...] = jnp.zeros_like(acc)

    for i in range(4):
        owner = order[step] * 2 + i // 2
        feat = x_ref[0, :tok_rows, i * BLK : (i + 1) * BLK]
        cot = x_ref[0, tok_rows:, i * BLK : (i + 1) * BLK]
        for t in range(3):
            left = cot if t == 2 else feat
            for pair in range(0, NZ, 2):
                row = (t * 2 + i % 2) * NZ * BLK + pair * BLK
                right = lanes(
                    [w_ref[i // 2, row : row + BLK, :], w_ref[i // 2, row + BLK : row + 2 * BLK, :]]
                )
                prod = jnp.dot(left, right, preferred_element_type=jnp.float32)
                for h in range(2):
                    col = cols[owner * 24 + t * 8 + (i % 2) * NZ + pair + h]
                    acc[t, col] += prod[:, h * BLK : (h + 1) * BLK]

    @pl.when(step == pl.num_programs(0) - 1)
    def _():
        @pl.loop(0, FB_DEV)
        def _(f):
            gate = acc[0, f]
            up = acc[1, f]
            grad = acc[2, f]
            sig = jax.nn.sigmoid(gate)
            silu = gate * sig
            hidden_ref[f] = (silu * up).astype(jnp.bfloat16)
            up_delta_ref[f] = (grad * silu).astype(jnp.bfloat16)
            gate_delta_ref[f] = (grad * up * sig * (1.0 + gate * (1.0 - sig))).astype(jnp.bfloat16)


def weight_grads_kernel(scale, order, cols, x_ref, hidden_ref, gate_delta_ref, up_delta_ref, o_ref):
    step = pl.program_id(0)
    tok_rows = hidden_ref.shape[1]
    for i in range(4):
        owner = order[step] * 2 + i // 2
        feat = x_ref[0, :tok_rows, i * BLK : (i + 1) * BLK]
        cot = x_ref[0, tok_rows:, i * BLK : (i + 1) * BLK]
        for t, source in enumerate((gate_delta_ref, up_delta_ref, hidden_ref)):
            left = cot if t == 2 else feat
            base = owner * 24 + t * 8 + (i % 2) * NZ
            right = lanes([source[cols[base + s]] for s in range(NZ)])
            prod = lax.dot_general(left, right, TN, preferred_element_type=jnp.float32) * scale
            row = (t * 2 + i % 2) * NZ * BLK
            for s in range(NZ):
                o_ref[i // 2, row + s * BLK : row + (s + 1) * BLK, :] = prod[
                    :, s * BLK : (s + 1) * BLK
                ].astype(jnp.bfloat16)


def product_kernel(tensors, cols, w_ref, *refs):
    step = pl.program_id(0)
    sources, o_ref = refs[:-1], refs[-1]
    for i in range(4):
        owner = step * 2 + i // 2
        left, right = [], []
        for n, t in enumerate(tensors):
            base = owner * 24 + t * 8 + (i % 2) * NZ
            row = (n * 2 + i % 2) * NZ * BLK
            for s in range(NZ):
                left.append(sources[n][cols[base + s]])
                right.append(w_ref[i // 2, row + s * BLK : row + (s + 1) * BLK, :])
        prod = lax.dot_general(lanes(left), lanes(right), NT, preferred_element_type=jnp.float32)
        o_ref[0, :, i * BLK : (i + 1) * BLK] = prod.astype(jnp.bfloat16)


def cost(flops, moved):
    return pl.CostEstimate(flops=flops, bytes_accessed=moved, transcendentals=0)


def params():
    return pltpu.CompilerParams(
        dimension_semantics=("arbitrary",), vmem_limit_bytes=VMEM_BYTES
    )


def whole(shape):
    return pl.BlockSpec(shape, lambda j, *_: (0,) * len(shape))


def local_sums(order, cols, feats, weights):
    steps, rows2, width = feats.shape
    tok_rows = rows2 // 2
    shape = (FB_DEV, tok_rows, BLK)
    per = weights.shape[1]
    out = jax.ShapeDtypeStruct(shape, jnp.bfloat16)
    return pl.pallas_call(
        sums_kernel,
        out_shape=(out, out, out),
        grid_spec=pltpu.PrefetchScalarGridSpec(
            num_scalar_prefetch=2,
            grid=(steps,),
            in_specs=[
                pl.BlockSpec((1, rows2, width), lambda j, order, cols: (j, 0, 0)),
                pl.BlockSpec((2, per, BLK), lambda j, order, cols: (order[j], 0, 0)),
            ],
            out_specs=[whole(shape)] * 3,
            scratch_shapes=[pltpu.VMEM((3,) + shape, jnp.float32)],
        ),
        compiler_params=params(),
        cost_estimate=cost(10**10, 30 * 10**6),
        name="local_sums",
    )(order, cols, feats, weights)


def weight_grads(order, cols, feats, hidden, gate_delta, up_delta, scale):
    steps, rows2, width = feats.shape
    rows = 3 * 2 * NZ * BLK
    return pl.pallas_call(
        functools.partial(weight_grads_kernel, scale),
        out_shape=jax.ShapeDtypeStruct((2 * steps, rows, BLK), jnp.bfloat16),
        grid_spec=pltpu.PrefetchScalarGridSpec(
            num_scalar_prefetch=2,
            grid=(steps,),
            in_specs=[pl.BlockSpec((1, rows2, width), lambda j, order, cols: (j, 0, 0))]
            + [whole(hidden.shape)] * 3,
            out_specs=pl.BlockSpec((2, rows, BLK), lambda j, order, cols: (order[j], 0, 0)),
        ),
        compiler_params=params(),
        cost_estimate=cost(10**10, 25 * 10**6),
        name="weight_grads",
    )(order, cols, feats, hidden, gate_delta, up_delta)


def block_product(tensors, cols, weights, sources):
    tok_rows = sources[0].shape[1]
    steps = weights.shape[0] // 2
    rows = len(tensors) * 2 * NZ * BLK
    at = tensors[0] * 2 * NZ * BLK // rows
    return pl.pallas_call(
        functools.partial(product_kernel, tensors),
        out_shape=jax.ShapeDtypeStruct((steps, tok_rows, 4 * BLK), jnp.bfloat16),
        grid_spec=pltpu.PrefetchScalarGridSpec(
            num_scalar_prefetch=1,
            grid=(steps,),
            in_specs=[pl.BlockSpec((2, rows, BLK), lambda j, cols: (j, at, 0))]
            + [whole(sources[0].shape)] * len(sources),
            out_specs=pl.BlockSpec((1, tok_rows, 4 * BLK), lambda j, cols: (j, 0, 0)),
        ),
        compiler_params=params(),
        cost_estimate=cost(len(tensors) * 3 * 10**9, len(tensors) * 7 * 10**6),
        name="block_product",
    )(cols, weights, *sources)


def over_x(value, shift, cols):
    pairs = [(c, ((c // 2 + shift) % X_SIZE) * 2 + c % 2) for c in range(cols)]
    return lax.ppermute(value, "col", pairs)


def gather_features(own, cols):
    me = lax.axis_index("col")
    x, z = me // 2, me % 2
    near = lax.ppermute(own, "col", [(c, c ^ 1) for c in range(cols)])
    own_w, own_e = over_x(own, 1, cols), over_x(own, -1, cols)
    near_w, near_e = over_x(near, 1, cols), over_x(near, -1, cols)
    own_far, near_far = over_x(own_w, 1, cols), over_x(near_e, -1, cols)
    pieces = [own, near, own_w, own_e, near_w, near_e, own_far, near_far]
    shifts = [(0, 0), (0, 1), (-1, 0), (1, 0), (-1, 1), (1, 1), (2, 0), (2, 1)]
    order = [((x + dx) % X_SIZE) * 2 + (z + dz) % 2 for dx, dz in shifts]
    return jnp.stack(pieces), jnp.stack(order).astype(jnp.int32)


def body(tokens, cotangent, gate_blocks, up_blocks, down_blocks, gate_cols, up_cols, down_cols):
    n_row, n_col = lax.axis_size("row"), lax.axis_size("col")
    tok_rows = tokens.shape[0]
    tables = jnp.concatenate(
        [jnp.bitwise_and(t, FB_DEV - 1).reshape(1, -1) for t in (gate_cols, up_cols, down_cols)], 1
    ).astype(jnp.bfloat16)
    tables = jnp.pad(tables, ((0, 15), (0, BLK - tables.shape[1])))
    packed = jnp.concatenate(
        [b.reshape(-1, BLK) for b in (gate_blocks, up_blocks, down_blocks)] + [tables], 0
    )
    weights = lax.all_gather(packed, "row", axis=0, tiled=True).reshape(n_row, -1, BLK)
    feats, order = gather_features(jnp.concatenate([tokens, cotangent], 0), n_col)
    at = packed.shape[0] - 16
    cols = weights[:, at, : 3 * 2 * NZ].astype(jnp.int32).reshape(-1)
    hidden, gate_delta, up_delta = local_sums(order, cols, feats, weights)
    scale = float(tok_rows * n_row) ** (-0.5)
    terms = weight_grads(order, cols, feats, hidden, gate_delta, up_delta, scale)
    grads = lax.psum_scatter(terms.reshape(-1, BLK), "row", scatter_dimension=0, tiled=True)
    gate_grad, up_grad, down_grad = (
        g.reshape(gate_blocks.shape) for g in jnp.split(grads, 3, axis=0)
    )

    def reduce_features(partial_value):
        parts = lax.all_to_all(partial_value, "col", 0, 0, tiled=True)
        return jnp.sum(parts.astype(jnp.float32), axis=0).astype(jnp.bfloat16)

    output = reduce_features(block_product((2,), cols, weights, (hidden,)))
    tokens_grad = reduce_features(block_product((0, 1), cols, weights, (gate_delta, up_delta)))
    return (output, tokens_grad, gate_grad, up_grad, down_grad)


def solution(mesh):
    flat, blocks = P("row", "col"), P("row", "col", None, None)
    in_specs = (flat, flat, blocks, blocks, blocks, flat, flat, flat)
    out_specs = (flat, flat, blocks, blocks, blocks)
    return jax.shard_map(body, mesh=mesh, in_specs=in_specs, out_specs=out_specs, check_vma=False)
```

time: 1260 us -> 314 us (0.25)
  waiting for transfers between devices: 534 us -> 196 us
  local copies, waits for them, and re-layouts: 302 us -> 13.2 us
  other arithmetic: 167 us -> 9.5 us
  matrix products: 150 us -> 0 us
  blocking collectives: 69.6 us -> 0 us
  Pallas kernels: 0 us -> 59.5 us
  starting transfers between devices: 0.32 us -> 19.6 us
    unnamed x9 -> x2, waiting for transfers between devices: 219 us -> 0.03 us
    gather x99 -> x0, local copies, waits for them, and re-layouts: 179 us -> none  [the longest x32 86.3 us: one_group(): jnp.take(up_delta, up_local, axis=1)]
    dot_general x54 -> x0, matrix products: 150 us -> none  [the longest x16 38.3 us: one_group(): jnp.einsum('tkd,tkje->kjde', inputs, jnp.take(up_delta, up_local, axis=1)...]
    scatter-add x3 -> x0, other arithmetic: 140 us -> none  [spread_columns(): return empty.at[:, columns.reshape(-1)].add(flat)]
    all_gather x5 -> x1, waiting for transfers between devices: 166 us -> 35.9 us  [body(): lax.all_gather(packed, 'row', axis=0, tiled=True).reshape(n_row, -1, BLK)]
    reduce_scatter x2 -> x1, waiting for transfers between devices: 150 us -> 40.2 us  [body(): lax.psum_scatter(terms.reshape(-1, BLK), 'row', scatter_dimension=0, tile...]
    all_to_all x0 -> x2, waiting for transfers between devices: none -> 75.9 us  [reduce_features(): parts = lax.all_to_all(partial_value, 'col', 0, 0, tiled=True)]
    reshape x6 -> x0, local copies, waits for them, and re-layouts: 74.8 us -> none  [the longest x3 74.5 us: spread_columns(): flat = products.reshape(tok_rows, -1, products.shape[3])]
  transfers between devices with their start and end apart: 8 -> 11, of which waited for: 7 -> 8; matrix products, arithmetic and copies ran while one was open for 12% -> 5% of each run, Pallas kernels for 0% -> 8%
where the time goes in v1:
time: 314 us; the launch traced here: 312 us
  waiting for transfers between devices  196 us (62%)
  Pallas kernels  59.5 us (19%)
  starting transfers between devices  19.6 us (6%)
  between operations  14.1 us (4%)
  local copies, waits for them, and re-layouts  13.2 us (4%)
  other arithmetic  9.5 us (3%)
    all_to_all x2, waiting for transfers between devices, reduce_features(): parts = lax.all_to_all(partial_value, 'col', 0, 0, tiled=True)  75.9 us
    reduce_scatter x1, waiting for transfers between devices, body(): lax.psum_scatter(terms.reshape(-1, BLK), 'row', scatter_dimension=0, tile...  40.2 us
    all_gather x1, waiting for transfers between devices, body(): lax.all_gather(packed, 'row', axis=0, tiled=True).reshape(n_row, -1, BLK)  35.9 us
    ppermute x6, waiting for transfers between devices, over_x(): return lax.ppermute(value, 'col', pairs)  24.1 us
    pallas_call x2, Pallas kernels, block_product(): pl.pallas_call(functools.partial(product_kernel, tensors), out_shape=jax....  23.8 us
    pallas_call x1, Pallas kernels, local_sums(): pl.pallas_call(sums_kernel, out_shape=(out, out, out), grid_spec=pltpu.Pr...  20.8 us
    ppermute x1, waiting for transfers between devices, gather_features(): near = lax.ppermute(own, 'col', [(c, c ^ 1) for c in range(cols)])  20.2 us
    pallas_call x1, Pallas kernels, weight_grads(): pl.pallas_call(functools.partial(weight_grads_kernel, scale), out_shape=j...  14.9 us
  transfers between devices with their start and end apart: 11, of which 8 were waited for; matrix products, arithmetic and copies ran while one was open for 5% of the time, Pallas kernels for 8%

profile of v1, /device:TPU:0, one launch (start us, length us, event | category | flops | bytes accessed | tf_op | source)
XLA Modules:
  0.0 312.2 jit_solution(1294054733294146860)
XLA Ops:
  9.6 2.1 pad_maximum_fusion
  12.8 1.0 constant_dynamic-update-slice_fusion
  13.8 2.1 collective-permute-start
  15.9 1.5 collective-permute-start.1
  17.4 1.7 collective-permute-start.2
  20.8 20.2 %collective-permute-done = bf16[768,512]{1,0:T(8,128)(2,1)S(1)} collective-permute-done((bf16[768,512]{1,0:T(8,128)(2,1)S(1)}, bf16[768,512]{1,0:T(8,128)(2,1)S(1)}, u32[]{:S(2)}, u32[]{:S(2)}) %collective-permute-start) | collective-permute-done | bytes 786464 | tf_op jit(solution)/shard_map/ppermute | solution.py:183
  41.0 1.3 collective-permute-start.3
  42.3 2.0 collective-permute-start.4
  47.1 12.7 %collective-permute-done.4 = bf16[768,512]{1,0:T(8,128)(2,1)S(1)} collective-permute-done((bf16[768,512]{1,0:T(8,128)(2,1)S(1)}, bf16[768,512]{1,0:T(8,128)(2,1)S(1)}, u32[]{:S(2)}, u32[]{:S(2)}) %collective-permute-start.4) | collective-permute-done | bytes 786464 | tf_op jit(solution)/shard_map/ppermute | solution.py:177
  59.9 2.1 collective-permute-start.6
  64.6 10.6 %collective-permute-done.5 = bf16[768,512]{1,0:T(8,128)(2,1)S(1)} collective-permute-done((bf16[768,512]{1,0:T(8,128)(2,1)S(1)}, bf16[768,512]{1,0:T(8,128)(2,1)S(1)}, u32[]{:S(2)}, u32[]{:S(2)}) %collective-permute-start.5) | collective-permute-done | bytes 786464 | tf_op jit(solution)/shard_map/ppermute | solution.py:177
  77.1 35.9 %all-gather.2.cloned.1.call-done = bf16[49408,128]{1,0:T(8,128)(2,1)} async-done(((bf16[3088,128]{1,0:T(8,128)(2,1)}), bf16[49408,128]{1,0:T(8,128)(2,1)}) %all-gather.2.cloned.1.call-update) | async-done | bytes 12648464 | tf_op jit(solution)/shard_map/all_gather | solution.py:203
  114.4 20.8 %local_sums.1 = (bf16[16,384,128]{2,1,0:T(8,128)(2,1)}, bf16[16,384,128]{2,1,0:T(8,128)(2,1)}, bf16[16,384,128]{2,1,0:T(8,128)(2,1)}) custom-call(s32[8]{0:T(128)} %stack.62.order, s32[384]{0:T(512)} %reshape.104.cols, bf16[8,768,512]{2,1,0:T(8,128)(2,1)} %bitcast_dynamic-update-slice_fusion.x_ref, bf16[16,3088,128]{2,1,0:T(8,128)(2,1)} %bitcast.33), custom_call_target="tpu_custom_call" | custom-call | flops 10000000000 | bytes 30000000 | tf_op jit(solution)/shard_map/local_sums/pallas_call | solution.py:116
  135.2 14.9 %weight_grads.1 = bf16[16,3072,128]{2,1,0:T(8,128)(2,1)} custom-call(s32[8]{0:T(128)} %stack.62.order, s32[384]{0:T(512)} %reshape.104.cols, bf16[8,768,512]{2,1,0:T(8,128)(2,1)} %bitcast_dynamic-update-slice_fusion.x_ref, bf16[16,384,128]{2,1,0:T(8,128)(2,1)} %get-tuple-element.8.refs_0_.hidden_ref, ...), custom_call_target="tpu_custom_call" | custom-call | flops 10000000000 | bytes 25000000 | tf_op jit(solution)/shard_map/weight_grads/pallas_call | solution.py:138
  150.2 9.8 %block_product.2 = bf16[8,384,512]{2,1,0:T(8,128)(2,1)} custom-call(s32[384]{0:T(512)} %reshape.104.cols, bf16[16,3088,128]{2,1,0:T(8,128)(2,1)} %bitcast.34, bf16[16,384,128]{2,1,0:T(8,128)(2,1)} %get-tuple-element.8.refs_0_.hidden_ref), custom_call_target="tpu_custom_call" | custom-call | flops 3000000000 | bytes 7000000 | tf_op jit(solution)/shard_map/block_product/pallas_call | solution.py:159
  160.0 4.4 %all-to-all-start = ((bf16[8,384,512]{2,1,0:T(8,128)(2,1)}), bf16[8,384,512]{2,1,0:T(8,128)(2,1)S(1)}, u32[]{:S(2)}, u32[]{:S(2)}) async-start(bf16[8,384,512]{2,1,0:T(8,128)(2,1)} %block_product.2), calls=%async_computation | async-start | bytes 6291456 | tf_op jit(solution)/shard_map/all_to_all | solution.py:216
  164.4 13.9 %block_product.3 = bf16[8,384,512]{2,1,0:T(8,128)(2,1)} custom-call(s32[384]{0:T(512)} %reshape.104.cols, bf16[16,3088,128]{2,1,0:T(8,128)(2,1)} %bitcast.35, bf16[16,384,128]{2,1,0:T(8,128)(2,1)} %get-tuple-element.9.refs_0_.gate_delta_ref, bf16[16,384,128]{2,1,0:T(8,128)(2,1)} %get-tuple-element.10.refs_1_.up_delta_ref), custom_call_target="tpu_custom_call" | custom-call | flops 6000000000 | bytes 14000000 | tf_op jit(solution)/shard_map/block_product/pallas_call | solution.py:159
  178.3 32.0 %all-to-all-done = bf16[8,384,512]{2,1,0:T(8,128)(2,1)S(1)} async-done(((bf16[8,384,512]{2,1,0:T(8,128)(2,1)}), bf16[8,384,512]{2,1,0:T(8,128)(2,1)S(1)}, u32[]{:S(2)}, u32[]{:S(2)}) %all-to-all-start) | async-done | bytes 3145760 | tf_op jit(solution)/shard_map/all_to_all | solution.py:216
  210.3 4.5 %all-to-all-start.1 = ((bf16[8,384,512]{2,1,0:T(8,128)(2,1)}), bf16[8,384,512]{2,1,0:T(8,128)(2,1)}, u32[]{:S(2)}, u32[]{:S(2)}) async-start(bf16[8,384,512]{2,1,0:T(8,128)(2,1)} %block_product.3), calls=%async_computation.1 | async-start | bytes 6291456 | tf_op jit(solution)/shard_map/all_to_all | solution.py:216
  214.8 1.3 reduce_sum.24
  216.1 43.9 %all-to-all-done.1 = bf16[8,384,512]{2,1,0:T(8,128)(2,1)} async-done(((bf16[8,384,512]{2,1,0:T(8,128)(2,1)}), bf16[8,384,512]{2,1,0:T(8,128)(2,1)}, u32[]{:S(2)}, u32[]{:S(2)}) %all-to-all-start.1) | async-done | bytes 3145760 | tf_op jit(solution)/shard_map/all_to_all | solution.py:216
  259.9 3.2 %reduce_sum.25 = bf16[384,512]{1,0:T(8,128)(2,1)} reduce(bf16[8,384,512]{2,1,0:T(8,128)(2,1)} %all-to-all-done.1, bf16[]{:T(256)} %constant.80.clone.1), dimensions={0}, to_apply=%region_1.2 | reduce | flops 1376256 | bytes 3538946 | tf_op jit(solution)/shard_map/reduce_sum | solution.py:217
  263.1 40.2 %reduce-scatter.2.cloned.1.call-done = bf16[3072,128]{1,0:T(8,128)(2,1)} async-done(((bf16[49152,128]{1,0:T(8,128)(2,1)}), bf16[3072,128]{1,0:T(8,128)(2,1)}) %reduce-scatter.2.cloned.1.call-update) | async-done | bytes 786448 | tf_op jit(solution)/shard_map/reduce_scatter | solution.py:210
  303.4 2.0 fusion.10
  (28 shorter events, 14.1 us)
Async XLA Ops:
  7.2 105.8 %all-gather.2.cloned.1.call-start = ((), (), s32[]{:S(2)}) async-start(), calls=%async_computation.3 | async-start | bytes 13438976 | tf_op jit(solution)/shard_map/all_gather | solution.py:203
  11.7 291.6 %reduce-scatter.2.cloned.1.call-start = ((), (), s32[]{:S(2)}) async-start(), calls=%async_computation.4 | async-start | bytes 13369344 | tf_op jit(solution)/shard_map/reduce_scatter | solution.py:210
  13.8 27.2 %collective-permute-start = (bf16[768,512]{1,0:T(8,128)(2,1)S(1)}, bf16[768,512]{1,0:T(8,128)(2,1)S(1)}, u32[]{:S(2)}, u32[]{:S(2)}) collective-permute-start(bf16[768,512]{1,0:T(8,128)(2,1)S(1)} %constant_dynamic-update-slice_fusion), channel_id=1, source_target_pairs={{0,1},{1,0},{2,3},{3,2},{4,5},{5,4},{6,7},{7,6},{8,9},{9,8},{10,11... | collective-permute-start | bytes 2359304 | tf_op jit(solution)/shard_map/ppermute | solution.py:183
  15.9 28.3 %collective-permute-start.1 = (bf16[768,512]{1,0:T(8,128)(2,1)S(1)}, bf16[768,512]{1,0:T(8,128)(2,1)S(1)}, u32[]{:S(2)}, u32[]{:S(2)}) collective-permute-start(bf16[768,512]{1,0:T(8,128)(2,1)S(1)} %constant_dynamic-update-slice_fusion), channel_id=1, source_target_pairs={{0,2},{1,3},{2,4},{3,5},{4,6},{5,7},{6,0},{7,1},{8,10},{9,11},{10,... | collective-permute-start | bytes 2359304 | tf_op jit(solution)/shard_map/ppermute | solution.py:177
  17.4 28.8 %collective-permute-start.2 = (bf16[768,512]{1,0:T(8,128)(2,1)S(1)}, bf16[768,512]{1,0:T(8,128)(2,1)S(1)}, u32[]{:S(2)}, u32[]{:S(2)}) collective-permute-start(bf16[768,512]{1,0:T(8,128)(2,1)S(1)} %constant_dynamic-update-slice_fusion), channel_id=1, source_target_pairs={{0,6},{1,7},{2,0},{3,1},{4,2},{5,3},{6,4},{7,5},{8,14},{9,15},{10,... | collective-permute-start | bytes 2359304 | tf_op jit(solution)/shard_map/ppermute | solution.py:177
  41.0 21.7 %collective-permute-start.3 = (bf16[768,512]{1,0:T(8,128)(2,1)S(1)}, bf16[768,512]{1,0:T(8,128)(2,1)S(1)}, u32[]{:S(2)}, u32[]{:S(2)}) collective-permute-start(bf16[768,512]{1,0:T(8,128)(2,1)S(1)} %collective-permute-done), channel_id=1, source_target_pairs={{0,2},{1,3},{2,4},{3,5},{4,6},{5,7},{6,0},{7,1},{8,10},{9,11},{10,... | collective-permute-start | bytes 2359304 | tf_op jit(solution)/shard_map/ppermute | solution.py:177
  42.3 17.6 %collective-permute-start.4 = (bf16[768,512]{1,0:T(8,128)(2,1)S(1)}, bf16[768,512]{1,0:T(8,128)(2,1)S(1)}, u32[]{:S(2)}, u32[]{:S(2)}) collective-permute-start(bf16[768,512]{1,0:T(8,128)(2,1)S(1)} %collective-permute-done), channel_id=1, source_target_pairs={{0,6},{1,7},{2,0},{3,1},{4,2},{5,3},{6,4},{7,5},{8,14},{9,15},{10,... | collective-permute-start | bytes 2359304 | tf_op jit(solution)/shard_map/ppermute | solution.py:177
  44.2 30.9 %collective-permute-start.5 = (bf16[768,512]{1,0:T(8,128)(2,1)S(1)}, bf16[768,512]{1,0:T(8,128)(2,1)S(1)}, u32[]{:S(2)}, u32[]{:S(2)}) collective-permute-start(bf16[768,512]{1,0:T(8,128)(2,1)S(1)} %collective-permute-done.1), channel_id=1, source_target_pairs={{0,2},{1,3},{2,4},{3,5},{4,6},{5,7},{6,0},{7,1},{8,10},{9,11},{10,... | collective-permute-start | bytes 2359304 | tf_op jit(solution)/shard_map/ppermute | solution.py:177
  59.9 16.3 %collective-permute-start.6 = (bf16[768,512]{1,0:T(8,128)(2,1)S(1)}, bf16[768,512]{1,0:T(8,128)(2,1)S(1)}, u32[]{:S(2)}, u32[]{:S(2)}) collective-permute-start(bf16[768,512]{1,0:T(8,128)(2,1)S(1)} %collective-permute-done.4), channel_id=1, source_target_pairs={{0,6},{1,7},{2,0},{3,1},{4,2},{5,3},{6,4},{7,5},{8,14},{9,15},{10,... | collective-permute-start | bytes 2359304 | tf_op jit(solution)/shard_map/ppermute | solution.py:177
  160.0 50.3 %all-to-all-start = ((bf16[8,384,512]{2,1,0:T(8,128)(2,1)}), bf16[8,384,512]{2,1,0:T(8,128)(2,1)S(1)}, u32[]{:S(2)}, u32[]{:S(2)}) async-start(bf16[8,384,512]{2,1,0:T(8,128)(2,1)} %block_product.2), calls=%async_computation | async-start | bytes 6291456 | tf_op jit(solution)/shard_map/all_to_all | solution.py:216
  210.3 49.6 %all-to-all-start.1 = ((bf16[8,384,512]{2,1,0:T(8,128)(2,1)}), bf16[8,384,512]{2,1,0:T(8,128)(2,1)}, u32[]{:S(2)}, u32[]{:S(2)}) async-start(bf16[8,384,512]{2,1,0:T(8,128)(2,1)} %block_product.3), calls=%async_computation.1 | async-start | bytes 6291456 | tf_op jit(solution)/shard_map/all_to_all | solution.py:216
Sparse Core Ops, SparseCore 0:
  11.8 101.0 all-gather.1
  150.3 153.0 reduce-scatter.1

commit v2 on v1

v2 whole, which is shorter than its diff:
```python
import functools

import jax
import jax.numpy as jnp
from jax import lax
from jax.experimental import pallas as pl
from jax.experimental.pallas import tpu as pltpu
from jax.sharding import PartitionSpec as P

BLK = 128
NZ = 4
FB_DEV = 16
RING = 4
VMEM_BYTES = 56 * 1024 * 1024
NT = (((1,), (1,)), ((), ()))
TN = (((0,), (0,)), ((), ()))


def lanes(values):
    return jnp.concatenate(values, axis=1)


def read_piece(sources, slots, held, sems):
    return [
        pltpu.make_async_copy(source, held.at[slot], sems.at[n])
        for n, (source, slot) in enumerate(zip(sources, slots))
    ]


def sums_kernel(n_feat, n_w, chips, owners, cols, *refs):
    feats, weights = refs[:n_feat], refs[n_feat : n_feat + n_w]
    hidden_ref, gate_delta_ref, up_delta_ref = refs[n_feat + n_w : n_feat + n_w + 3]
    acc, held_x, held_w, sem_x, sem_w = refs[n_feat + n_w + 3 :]
    tok_rows = hidden_ref.shape[1]
    copies_x = read_piece(feats, [chips[n] for n in range(n_feat)], held_x, sem_x)
    copies_w = read_piece(weights, range(n_w), held_w, sem_w)
    for copy in copies_x + copies_w:
        copy.start()
    acc[...] = jnp.zeros_like(acc)
    for copy in copies_x:
        copy.wait()

    def piece(p, carry):
        pltpu.make_async_copy(weights[0], held_w.at[p], sem_w.at[p]).wait()
        owner = owners[p]
        for i in range(2):
            at = pl.ds(pl.multiple_of((owner % 2) * 2 * BLK + i * BLK, BLK), BLK)
            feat = held_x[owner // 2, :tok_rows, at]
            cot = held_x[owner // 2, tok_rows:, at]
            for t in range(3):
                left = cot if t == 2 else feat
                for pair in range(0, NZ, 2):
                    row = (t * 2 + i) * NZ * BLK + pair * BLK
                    right = lanes(
                        [held_w[p, row : row + BLK, :], held_w[p, row + BLK : row + 2 * BLK, :]]
                    )
                    prod = jnp.dot(left, right, preferred_element_type=jnp.float32)
                    for h in range(2):
                        col = cols[p * 24 + t * 8 + i * NZ + pair + h]
                        acc[t, col] += prod[:, h * BLK : (h + 1) * BLK]
        return carry

    lax.fori_loop(0, n_w, piece, 0)

    @pl.loop(0, FB_DEV)
    def _(f):
        gate = acc[0, f]
        up = acc[1, f]
        grad = acc[2, f]
        sig = jax.nn.sigmoid(gate)
        silu = gate * sig
        hidden_ref[f] = (silu * up).astype(jnp.bfloat16)
        up_delta_ref[f] = (grad * silu).astype(jnp.bfloat16)
        gate_delta_ref[f] = (grad * up * sig * (1.0 + gate * (1.0 - sig))).astype(jnp.bfloat16)


def weight_grads_kernel(n_feat, tensors, half, scale, chips, owners, cols, *refs):
    feats, sources = refs[:n_feat], refs[n_feat : n_feat + len(tensors)]
    o_ref, held_x, sem_x = refs[n_feat + len(tensors) :]
    tok_rows = held_x.shape[1]
    first = tok_rows if tensors[0] == 2 else 0
    copies = read_piece(
        [f.at[pl.ds(first, tok_rows)] for f in feats], [chips[n] for n in range(n_feat)], held_x, sem_x
    )
    for copy in copies:
        copy.start()
    for copy in copies:
        copy.wait()

    def slot(p, carry):
        owner = owners[half * 8 + p]
        for i in range(2):
            at = pl.ds(pl.multiple_of((owner % 2) * 2 * BLK + i * BLK, BLK), BLK)
            left = held_x[owner // 2, :, at]
            right = []
            for n, t in enumerate(tensors):
                base = (half * 8 + p) * 24 + t * 8 + i * NZ
                right += [sources[n][cols[base + s]] for s in range(NZ)]
            prod = lax.dot_general(left, lanes(right), TN, preferred_element_type=jnp.float32) * scale
            for n in range(len(tensors)):
                for s in range(NZ):
                    row = (n * 2 + i) * NZ * BLK + s * BLK
                    at_col = (n * NZ + s) * BLK
                    o_ref[p, row : row + BLK, :] = prod[:, at_col : at_col + BLK].astype(jnp.bfloat16)
        return carry

    lax.fori_loop(0, 8, slot, 0)


def product_kernel(n_w, tensors, owners, cols, *refs):
    weights, sources = refs[:n_w], refs[n_w : n_w + len(tensors)]
    o_ref, held_w, sem_w = refs[n_w + len(tensors) :]
    rows = held_w.shape[1]
    views = [w.at[pl.ds(tensors[0] * 2 * NZ * BLK, rows)] for w in weights]
    for copy in read_piece(views, range(n_w), held_w, sem_w):
        copy.start()

    def piece(p, carry):
        pltpu.make_async_copy(views[0], held_w.at[p], sem_w.at[p]).wait()
        owner = owners[p]
        for i in range(2):
            left, right = [], []
            for n, t in enumerate(tensors):
                base = p * 24 + t * 8 + i * NZ
                row = (n * 2 + i) * NZ * BLK
                for s in range(NZ):
                    left.append(sources[n][cols[base + s]])
                    right.append(held_w[p, row + s * BLK : row + (s + 1) * BLK, :])
            prod = lax.dot_general(lanes(left), lanes(right), NT, preferred_element_type=jnp.float32)
            at = pl.ds(pl.multiple_of((owner % 2) * 2 * BLK + i * BLK, BLK), BLK)
            o_ref[owner // 2, :, at] = prod.astype(jnp.bfloat16)
        return carry

    lax.fori_loop(0, n_w, piece, 0)


def cost(flops, moved):
    return pl.CostEstimate(flops=flops, bytes_accessed=moved, transcendentals=0)


PARAMS = pltpu.CompilerParams(vmem_limit_bytes=VMEM_BYTES)
SMEM = pl.BlockSpec(memory_space=pltpu.SMEM)
VMEM = pl.BlockSpec(memory_space=pltpu.VMEM)
ANY = pl.BlockSpec(memory_space=pl.ANY)


def local_sums(chips, owners, cols, feats, weights):
    rows2, width = feats[0].shape
    shape = (FB_DEV, rows2 // 2, BLK)
    out = jax.ShapeDtypeStruct(shape, jnp.bfloat16)
    return pl.pallas_call(
        functools.partial(sums_kernel, len(feats), len(weights)),
        out_shape=(out, out, out),
        in_specs=[SMEM] * 3 + [ANY] * (len(feats) + len(weights)),
        out_specs=(VMEM, VMEM, VMEM),
        scratch_shapes=[
            pltpu.VMEM((3,) + shape, jnp.float32),
            pltpu.VMEM((len(feats), rows2, width), jnp.bfloat16),
            pltpu.VMEM((len(weights),) + weights[0].shape, jnp.bfloat16),
            pltpu.SemaphoreType.DMA((len(feats),)),
            pltpu.SemaphoreType.DMA((len(weights),)),
        ],
        compiler_params=PARAMS,
        cost_estimate=cost(10**10, 30 * 10**6),
        name="local_sums",
    )(chips, owners, cols, *feats, *weights)


def weight_grads(tensors, half, chips, owners, cols, feats, sources, scale):
    rows2, width = feats[0].shape
    rows = len(tensors) * 2 * NZ * BLK
    return pl.pallas_call(
        functools.partial(weight_grads_kernel, len(feats), tensors, half, scale),
        out_shape=jax.ShapeDtypeStruct((8, rows, BLK), jnp.bfloat16),
        in_specs=[SMEM] * 3 + [ANY] * len(feats) + [VMEM] * len(sources),
        out_specs=VMEM,
        scratch_shapes=[
            pltpu.VMEM((len(feats), rows2 // 2, width), jnp.bfloat16),
            pltpu.SemaphoreType.DMA((len(feats),)),
        ],
        compiler_params=PARAMS,
        cost_estimate=cost(len(tensors) * 2 * 10**9, len(tensors) * 6 * 10**6),
        name="weight_grads",
    )(chips, owners, cols, *feats, *sources)


def block_product(tensors, owners, cols, weights, sources):
    tok_rows = sources[0].shape[1]
    rows = len(tensors) * 2 * NZ * BLK
    return pl.pallas_call(
        functools.partial(product_kernel, len(weights), tensors),
        out_shape=jax.ShapeDtypeStruct((len(weights) // 2, tok_rows, 4 * BLK), jnp.bfloat16),
        in_specs=[SMEM] * 2 + [ANY] * len(weights) + [VMEM] * len(sources),
        out_specs=VMEM,
        scratch_shapes=[
            pltpu.VMEM((len(weights), rows, BLK), jnp.bfloat16),
            pltpu.SemaphoreType.DMA((len(weights),)),
        ],
        compiler_params=PARAMS,
        cost_estimate=cost(len(tensors) * 3 * 10**9, len(tensors) * 7 * 10**6),
        name="block_product",
    )(owners, cols, *weights, *sources)


SHIFTS = ((0, 0), (0, 1), (-1, 0), (1, 0), (-1, 1), (1, 1), (2, 0), (2, 1))


def permute(value, axis, target):
    return lax.ppermute(value, axis, [(i, target(i)) for i in range(lax.axis_size(axis))])


def over_x(value, shift):
    return permute(value, "col", lambda c: ((c // 2 + shift) % RING) * 2 + c % 2)


def over_y(value, shift):
    return permute(value, "row", lambda r: ((r // 4 + shift) % RING) * 4 + r % 4)


def ring_gather(own, near, ring):
    own_m, own_p = ring(own, 1), ring(own, -1)
    near_m, near_p = ring(near, 1), ring(near, -1)
    return [own, near, own_m, own_p, near_m, near_p, ring(own_m, 1), ring(near_p, -1)]


def gather_features(own):
    near = permute(own, "col", lambda c: c ^ 1)
    me = lax.axis_index("col")
    chips = [((me // 2 + d) % RING) * 2 + (me % 2 + e) % 2 for d, e in SHIFTS]
    return ring_gather(own, near, over_x), jnp.stack(chips).astype(jnp.int32)


def other_core(value):
    return permute(value, "row", lambda r: r ^ 1)


def gather_weights(own):
    near = permute(own, "row", lambda r: r ^ 2)
    same = ring_gather(own, near, over_y)
    me = lax.axis_index("row")
    chip = me // 2
    chips = [((chip // 2 + d) % RING) * 2 + (chip % 2 + e) % 2 for d, e in SHIFTS]
    owners = [c * 2 + me % 2 for c in chips]
    owners += [c * 2 + 1 - me % 2 for c in chips]
    return same + [other_core(p) for p in same], jnp.stack(owners).astype(jnp.int32)


def reduce_slots(mine, theirs):
    got = other_core(theirs)

    def slot(k):
        return mine[k].astype(jnp.float32) + got[k].astype(jnp.float32)

    def wire(*values):
        return jnp.concatenate([v.astype(jnp.bfloat16) for v in values], 0)

    far_p = over_y(wire(slot(6)), 1).astype(jnp.float32)
    far_m = over_y(wire(slot(7)), -1).astype(jnp.float32)
    from_m = over_y(wire(slot(3) + far_p, slot(5)), 1).astype(jnp.float32)
    from_p = over_y(wire(slot(2), slot(4) + far_m), -1).astype(jnp.float32)
    rows = mine.shape[1]
    keep = slot(0) + from_m[:rows] + from_p[:rows]
    give = slot(1) + from_m[rows:] + from_p[rows:]
    last = permute(wire(give), "row", lambda r: r ^ 2)
    return (keep + last.astype(jnp.float32)).astype(jnp.bfloat16)


def body(tokens, cotangent, gate_blocks, up_blocks, down_blocks, gate_cols, up_cols, down_cols):
    tok_rows = tokens.shape[0]
    tables = jnp.concatenate(
        [jnp.bitwise_and(t, FB_DEV - 1).reshape(1, -1) for t in (gate_cols, up_cols, down_cols)], 1
    ).astype(jnp.bfloat16)
    tables = jnp.pad(tables, ((0, 15), (0, BLK - tables.shape[1])))
    packed = jnp.concatenate(
        [b.reshape(-1, BLK) for b in (gate_blocks, up_blocks, down_blocks)] + [tables], 0
    )
    at = packed.shape[0] - 16
    weights, owners = gather_weights(packed)
    feats, chips = gather_features(jnp.concatenate([tokens, cotangent], 0))
    cols = jnp.concatenate([w[at, : 3 * 2 * NZ] for w in weights]).astype(jnp.int32)
    hidden, gate_delta, up_delta = local_sums(chips, owners, cols, feats, weights)
    scale = float(tok_rows * lax.axis_size("row")) ** (-0.5)

    def grads(tensors, sources):
        theirs = weight_grads(tensors, 1, chips, owners, cols, feats, sources, scale)
        mine = weight_grads(tensors, 0, chips, owners, cols, feats, sources, scale)
        return reduce_slots(mine, theirs)

    def reduce_features(partial_value):
        parts = lax.all_to_all(partial_value, "col", 0, 0, tiled=True)
        return jnp.sum(parts.astype(jnp.float32), axis=0).astype(jnp.bfloat16)

    down_grad = grads((2,), (hidden,)).reshape(down_blocks.shape)
    output = reduce_features(block_product((2,), owners, cols, weights, (hidden,)))
    both = grads((0, 1), (gate_delta, up_delta))
    gate_grad, up_grad = (g.reshape(gate_blocks.shape) for g in jnp.split(both, 2, axis=0))
    tokens_grad = reduce_features(
        block_product((0, 1), owners, cols, weights, (gate_delta, up_delta))
    )
    return (output, tokens_grad, gate_grad, up_grad, down_grad)


def solution(mesh):
    flat, blocks = P("row", "col"), P("row", "col", None, None)
    in_specs = (flat, flat, blocks, blocks, blocks, flat, flat, flat)
    out_specs = (flat, flat, blocks, blocks, blocks)
    return jax.shard_map(body, mesh=mesh, in_specs=in_specs, out_specs=out_specs, check_vma=False)
```

time: 314 us -> 297 us (0.946)
  waiting for transfers between devices: 196 us -> 121 us
  starting transfers between devices: 19.6 us -> 49.6 us
  Pallas kernels: 59.5 us -> 85.2 us
  other arithmetic: 9.5 us -> 29.1 us
  between operations: 14.1 us -> 1.13 us
    ppermute x7 -> x34, waiting for transfers between devices: 44.3 us -> 121 us  [permute(): lax.ppermute(value, axis, [(i, target(i)) for i in range(lax.axis_size(ax...]
    all_to_all x2, waiting for transfers between devices: 75.9 us -> 0.01 us  [reduce_features(): parts = lax.all_to_all(partial_value, 'col', 0, 0, tiled=True)]
    reduce_scatter x1 -> x0, waiting for transfers between devices: 40.2 us -> none  [body(): lax.psum_scatter(terms.reshape(-1, BLK), 'row', scatter_dimension=0, tile...]
    all_gather x1 -> x0, waiting for transfers between devices: 35.9 us -> none  [body(): lax.all_gather(packed, 'row', axis=0, tiled=True).reshape(n_row, -1, BLK)]
    ppermute x7 -> x34, starting transfers between devices: 10.7 us -> 40.3 us  [permute(): lax.ppermute(value, axis, [(i, target(i)) for i in range(lax.axis_size(ax...]
    pallas_call x4 -> x7, Pallas kernels: 59.5 us -> 85.2 us  [the longest x4 34.3 us: weight_grads(): pl.pallas_call(functools.partial(weight_grads_kernel, len(feats), tensors...]
    convert_element_type x1 -> x13, other arithmetic: 0.79 us -> 19.6 us  [the longest x6 14.6 us: wire(): return jnp.concatenate([v.astype(jnp.bfloat16) for v in values], 0)]
    unnamed x8 -> x57, local copies, waits for them, and re-layouts: 7.72 us -> 4.03 us
  transfers between devices with their start and end apart: 11 -> 36, of which waited for: 8 -> 12; matrix products, arithmetic and copies ran while one was open for 5% -> 10% of each run, Pallas kernels for 8% -> 16%
where the time goes in v2:
time: 297 us; the launch traced here: 296 us
  waiting for transfers between devices  121 us (41%)
  Pallas kernels  85.2 us (29%)
  starting transfers between devices  49.6 us (17%)
  other arithmetic  29.1 us (10%)
  local copies, waits for them, and re-layouts  10.1 us (3%)
    ppermute x34, waiting for transfers between devices, permute(): lax.ppermute(value, axis, [(i, target(i)) for i in range(lax.axis_size(ax...  121 us
    ppermute x34, starting transfers between devices, permute(): lax.ppermute(value, axis, [(i, target(i)) for i in range(lax.axis_size(ax...  40.3 us
    pallas_call x4, Pallas kernels, weight_grads(): pl.pallas_call(functools.partial(weight_grads_kernel, len(feats), tensors...  34.3 us
    pallas_call x1, Pallas kernels, local_sums(): pl.pallas_call(functools.partial(sums_kernel, len(feats), len(weights)),...  26.7 us
    pallas_call x2, Pallas kernels, block_product(): pl.pallas_call(functools.partial(product_kernel, len(weights), tensors),...  24.2 us
    convert_element_type x6, other arithmetic, wire(): return jnp.concatenate([v.astype(jnp.bfloat16) for v in values], 0)  14.6 us
    all_to_all x2, starting transfers between devices, reduce_features(): parts = lax.all_to_all(partial_value, 'col', 0, 0, tiled=True)  9.3 us
  transfers between devices with their start and end apart: 36, of which 12 were waited for; matrix products, arithmetic and copies ran while one was open for 10% of the time, Pallas kernels for 16%

profile of v2, /device:TPU:0, one launch (start us, length us, event | category | flops | bytes accessed | tf_op | source)
XLA Modules:
  0.0 296.5 jit_solution(10327965977199266728)
XLA Ops:
  4.2 4.0 %collective-permute-start = (bf16[3088,128]{1,0:T(8,128)(2,1)S(1)}, bf16[3088,128]{1,0:T(8,128)(2,1)}, u32[]{:S(2)}, u32[]{:S(2)}) collective-permute-start(bf16[3088,128]{1,0:T(8,128)(2,1)S(1)} %pad_maximum_fusion.2.refs_8_.refs_0_), channel_id=1, source_target_pairs={{0,16},{8,24},{16,0},{24,8},{32,48},{40,56},{48,32},{56,40},{64,80... | collective-permute-start | bytes 2371592 | tf_op jit(solution)/shard_map/ppermute | solution.py:209
  12.6 13.5 %collective-permute-done.refs_9_.refs_1_ = bf16[3088,128]{1,0:T(8,128)(2,1)} collective-permute-done((bf16[3088,128]{1,0:T(8,128)(2,1)S(1)}, bf16[3088,128]{1,0:T(8,128)(2,1)}, u32[]{:S(2)}, u32[]{:S(2)}) %collective-permute-start) | collective-permute-done | bytes 790560 | tf_op jit(solution)/shard_map/ppermute | solution.py:209
  34.5 13.2 %collective-permute-done.15.refs_1_ = bf16[768,512]{1,0:T(8,128)(2,1)S(1)} collective-permute-done((bf16[768,512]{1,0:T(8,128)(2,1)S(1)}, bf16[768,512]{1,0:T(8,128)(2,1)S(1)}, u32[]{:S(2)}, u32[]{:S(2)}) %collective-permute-start.15) | collective-permute-done | bytes 786464 | tf_op jit(solution)/shard_map/ppermute | solution.py:209
  51.7 11.6 %collective-permute-done.5.refs_14_.refs_6_ = bf16[3088,128]{1,0:T(8,128)(2,1)S(1)} collective-permute-done((bf16[3088,128]{1,0:T(8,128)(2,1)}, bf16[3088,128]{1,0:T(8,128)(2,1)S(1)}, u32[]{:S(2)}, u32[]{:S(2)}) %collective-permute-start.5) | collective-permute-done | bytes 790560 | tf_op jit(solution)/shard_map/ppermute | solution.py:209
  68.4 13.0 %collective-permute-done.6.refs_15_.refs_7_ = bf16[3088,128]{1,0:T(8,128)(2,1)S(1)} collective-permute-done((bf16[3088,128]{1,0:T(8,128)(2,1)}, bf16[3088,128]{1,0:T(8,128)(2,1)S(1)}, u32[]{:S(2)}, u32[]{:S(2)}) %collective-permute-start.6) | collective-permute-done | bytes 790560 | tf_op jit(solution)/shard_map/ppermute | solution.py:209
  82.8 3.8 %collective-permute-start.17 = (bf16[768,512]{1,0:T(8,128)(2,1)S(1)}, bf16[768,512]{1,0:T(8,128)(2,1)}, u32[]{:S(2)}, u32[]{:S(2)}) collective-permute-start(bf16[768,512]{1,0:T(8,128)(2,1)S(1)} %constant_dynamic-update-slice_fusion.refs_0_), channel_id=1, source_target_pairs={{0,6},{1,7},{2,0},{3,1},{4,2},{5,3},{6,4},{7,5},{8,14},{9,15},{10,... | collective-permute-start | bytes 2359304 | tf_op jit(solution)/shard_map/ppermute | solution.py:209
  86.8 3.3 %collective-permute-start.21 = (bf16[768,512]{1,0:T(8,128)(2,1)}, bf16[768,512]{1,0:T(8,128)(2,1)}, u32[]{:S(2)}, u32[]{:S(2)}) collective-permute-start(bf16[768,512]{1,0:T(8,128)(2,1)} %collective-permute-done.19.refs_5_), channel_id=1, source_target_pairs={{0,6},{1,7},{2,0},{3,1},{4,2},{5,3},{6,4},{7,5},{8,14},{9,15},{10,... | collective-permute-start | bytes 2359304 | tf_op jit(solution)/shard_map/ppermute | solution.py:209
  91.7 12.9 %collective-permute-done.17.refs_3_ = bf16[768,512]{1,0:T(8,128)(2,1)} collective-permute-done((bf16[768,512]{1,0:T(8,128)(2,1)S(1)}, bf16[768,512]{1,0:T(8,128)(2,1)}, u32[]{:S(2)}, u32[]{:S(2)}) %collective-permute-start.17) | collective-permute-done | bytes 786464 | tf_op jit(solution)/shard_map/ppermute | solution.py:209
  104.6 3.8 %collective-permute-done.18.refs_4_ = bf16[768,512]{1,0:T(8,128)(2,1)} collective-permute-done((bf16[768,512]{1,0:T(8,128)(2,1)S(1)}, bf16[768,512]{1,0:T(8,128)(2,1)}, u32[]{:S(2)}, u32[]{:S(2)}) %collective-permute-start.18) | collective-permute-done | bytes 786464 | tf_op jit(solution)/shard_map/ppermute | solution.py:209
  108.4 13.6 %collective-permute-done.20.refs_6_ = bf16[768,512]{1,0:T(8,128)(2,1)} collective-permute-done((bf16[768,512]{1,0:T(8,128)(2,1)S(1)}, bf16[768,512]{1,0:T(8,128)(2,1)}, u32[]{:S(2)}, u32[]{:S(2)}) %collective-permute-start.20) | collective-permute-done | bytes 786464 | tf_op jit(solution)/shard_map/ppermute | solution.py:209
  122.1 26.7 %local_sums.1 = (bf16[16,384,128]{2,1,0:T(8,128)(2,1)}, bf16[16,384,128]{2,1,0:T(8,128)(2,1)}, bf16[16,384,128]{2,1,0:T(8,128)(2,1)}) custom-call(s32[8]{0:T(128)} %stack.103.chips, s32[16]{0:T(128)} %stack.94.owners, s32[384]{0:T(512)} %convert_element_type.249.cols, bf16[768,512]{1,0:T(8,128)(2,1)} %copy-done.5, bf16[768,512]{1,0:T(8,128)(2,1)} %copy-done.10, ...), custom_call_target="tpu_custom_call" | custom-call | flops 10000000000 | bytes 30000000 | tf_op jit(solution)/shard_map/local_sums/pallas_call | solution.py:151
  148.8 9.9 %weight_grads.5 = bf16[8,2048,128]{2,1,0:T(8,128)(2,1)} custom-call(s32[8]{0:T(128)} %stack.103.chips, s32[16]{0:T(128)} %stack.94.owners, s32[384]{0:T(512)} %convert_element_type.249.cols, bf16[768,512]{1,0:T(8,128)(2,1)} %copy-done.5, bf16[768,512]{1,0:T(8,128)(2,1)} %copy-done.10, bf16[768,512]{1,0:T(8,128)(2,1)} %copy-done.11, ...), custom_call_target="tpu_custom_call" | custom-call | flops 4000000000 | bytes 12000000 | tf_op jit(solution)/shard_map/weight_grads/pallas_call | solution.py:172
  158.8 7.4 %weight_grads.7 = bf16[8,1024,128]{2,1,0:T(8,128)(2,1)} custom-call(s32[8]{0:T(128)} %stack.103.chips, s32[16]{0:T(128)} %stack.94.owners, s32[384]{0:T(512)} %convert_element_type.249.cols, bf16[768,512]{1,0:T(8,128)(2,1)} %copy-done.5, bf16[768,512]{1,0:T(8,128)(2,1)} %copy-done.10, bf16[768,512]{1,0:T(8,128)(2,1)} %copy-done.11, ...), custom_call_target="tpu_custom_call" | custom-call | flops 2000000000 | bytes 6000000 | tf_op jit(solution)/shard_map/weight_grads/pallas_call | solution.py:172
  166.7 10.2 %block_product.2 = bf16[8,384,512]{2,1,0:T(8,128)(2,1)} custom-call(s32[16]{0:T(128)} %stack.94.owners, s32[384]{0:T(512)} %convert_element_type.249.cols, bf16[3088,128]{1,0:T(8,128)(2,1)} %copy-done.9, bf16[3088,128]{1,0:T(8,128)(2,1)} %collective-permute-done.refs_9_.refs_1_, bf16[3088,128]{1,0:T(8,128)(2,1)} %collective-permute-done.1.refs_10_.refs_2_, ...), custom_call_target="tpu_custom_call" | custom-call | flops 3000000000 | bytes 7000000 | tf_op jit(solution)/shard_map/block_product/pallas_call | solution.py:190
  176.9 3.8 %all-to-all-start = ((bf16[8,384,512]{2,1,0:T(8,128)(2,1)}), bf16[8,384,512]{2,1,0:T(8,128)(2,1)S(1)}, u32[]{:S(2)}, u32[]{:S(2)}) async-start(bf16[8,384,512]{2,1,0:T(8,128)(2,1)} %block_product.2), calls=%async_computation | async-start | bytes 6291456 | tf_op jit(solution)/shard_map/all_to_all | solution.py:290
  180.7 7.3 %weight_grads.6 = bf16[8,1024,128]{2,1,0:T(8,128)(2,1)} custom-call(s32[8]{0:T(128)} %stack.103.chips, s32[16]{0:T(128)} %stack.94.owners, s32[384]{0:T(512)} %convert_element_type.249.cols, bf16[768,512]{1,0:T(8,128)(2,1)} %copy-done.5, bf16[768,512]{1,0:T(8,128)(2,1)} %copy-done.10, bf16[768,512]{1,0:T(8,128)(2,1)} %copy-done.11, ...), custom_call_target="tpu_custom_call" | custom-call | flops 2000000000 | bytes 6000000 | tf_op jit(solution)/shard_map/weight_grads/pallas_call | solution.py:172
  188.1 9.7 %weight_grads.4 = bf16[8,2048,128]{2,1,0:T(8,128)(2,1)} custom-call(s32[8]{0:T(128)} %stack.103.chips, s32[16]{0:T(128)} %stack.94.owners, s32[384]{0:T(512)} %convert_element_type.249.cols, bf16[768,512]{1,0:T(8,128)(2,1)} %copy-done.5, bf16[768,512]{1,0:T(8,128)(2,1)} %copy-done.10, bf16[768,512]{1,0:T(8,128)(2,1)} %copy-done.11, ...), custom_call_target="tpu_custom_call" | custom-call | flops 4000000000 | bytes 12000000 | tf_op jit(solution)/shard_map/weight_grads/pallas_call | solution.py:172
  203.2 3.7 %fusion.5 = (bf16[2048,128]{1,0:T(8,128)(2,1)S(1)}, bf16[2048,128]{1,0:T(8,128)(2,1)S(1)}, bf16[2048,128]{1,0:T(8,128)(2,1)}, bf16[2048,128]{1,0:T(8,128)(2,1)}) fusion(bf16[8,2048,128]{2,1,0:T(8,128)(2,1)} %collective-permute-done.22, bf16[8,2048,128]{2,1,0:T(8,128)(2,1)} %weight_grads.4), kind=kLoop, calls=%fused_computation.18 | loop fusion | flops 4194304 | bytes 6291456 | tf_op jit(solution)/shard_map/convert_element_type | solution.py:255
  206.9 3.2 %collective-permute-start.25 = (bf16[2048,128]{1,0:T(8,128)(2,1)S(1)}, bf16[2048,128]{1,0:T(8,128)(2,1)S(1)}, u32[]{:S(2)}, u32[]{:S(2)}) collective-permute-start(bf16[2048,128]{1,0:T(8,128)(2,1)S(1)} %get-tuple-element.14), channel_id=1, source_target_pairs={{0,96},{8,104},{16,112},{24,120},{32,0},{40,8},{48,16},{56,24},{64... | collective-permute-start | bytes 1572872 | tf_op jit(solution)/shard_map/ppermute | solution.py:209
  210.1 14.0 %block_product.3 = bf16[8,384,512]{2,1,0:T(8,128)(2,1)} custom-call(s32[16]{0:T(128)} %stack.94.owners, s32[384]{0:T(512)} %convert_element_type.249.cols, bf16[3088,128]{1,0:T(8,128)(2,1)} %copy-done.9, bf16[3088,128]{1,0:T(8,128)(2,1)} %collective-permute-done.refs_9_.refs_1_, bf16[3088,128]{1,0:T(8,128)(2,1)} %collective-permute-done.1.refs_10_.refs_2_, ...), custom_call_target="tpu_custom_call" | custom-call | flops 6000000000 | bytes 14000000 | tf_op jit(solution)/shard_map/block_product/pallas_call | solution.py:190
  229.3 5.5 %all-to-all-start.1 = ((bf16[8,384,512]{2,1,0:T(8,128)(2,1)}), bf16[8,384,512]{2,1,0:T(8,128)(2,1)}, u32[]{:S(2)}, u32[]{:S(2)}) async-start(bf16[8,384,512]{2,1,0:T(8,128)(2,1)} %block_product.3), calls=%async_computation.1 | async-start | bytes 6291456 | tf_op jit(solution)/shard_map/all_to_all | solution.py:290
  240.6 30.6 %collective-permute-done.32 = bf16[2048,128]{1,0:T(8,128)(2,1)S(1)} collective-permute-done((bf16[2048,128]{1,0:T(8,128)(2,1)S(1)}, bf16[2048,128]{1,0:T(8,128)(2,1)S(1)}, u32[]{:S(2)}, u32[]{:S(2)}) %collective-permute-start.32) | collective-permute-done | bytes 524320 | tf_op jit(solution)/shard_map/ppermute | solution.py:209
  283.3 3.3 %reduce_sum.25 = bf16[384,512]{1,0:T(8,128)(2,1)} reduce(bf16[8,384,512]{2,1,0:T(8,128)(2,1)} %all-to-all-done.1, bf16[]{:T(256)} %constant.243.clone.1), dimensions={0}, to_apply=%region_1.2 | reduce | flops 1376256 | bytes 3538946 | tf_op jit(solution)/shard_map/reduce_sum | solution.py:291
  288.9 5.0 %collective-permute-done.27 = bf16[2048,128]{1,0:T(8,128)(2,1)} collective-permute-done((bf16[2048,128]{1,0:T(8,128)(2,1)}, bf16[2048,128]{1,0:T(8,128)(2,1)}, u32[]{:S(2)}, u32[]{:S(2)}) %collective-permute-start.27) | collective-permute-done | bytes 524320 | tf_op jit(solution)/shard_map/ppermute | solution.py:209
  (162 shorter events, 62.4 us)
Async XLA Ops:
  4.2 21.8 %collective-permute-start = (bf16[3088,128]{1,0:T(8,128)(2,1)S(1)}, bf16[3088,128]{1,0:T(8,128)(2,1)}, u32[]{:S(2)}, u32[]{:S(2)}) collective-permute-start(bf16[3088,128]{1,0:T(8,128)(2,1)S(1)} %pad_maximum_fusion.2.refs_8_.refs_0_), channel_id=1, source_target_pairs={{0,16},{8,24},{16,0},{24,8},{32,48},{40,56},{48,32},{56,40},{64,80... | collective-permute-start | bytes 2371592 | tf_op jit(solution)/shard_map/ppermute | solution.py:209
  8.3 21.0 %collective-permute-start.1 = (bf16[3088,128]{1,0:T(8,128)(2,1)S(1)}, bf16[3088,128]{1,0:T(8,128)(2,1)}, u32[]{:S(2)}, u32[]{:S(2)}) collective-permute-start(bf16[3088,128]{1,0:T(8,128)(2,1)S(1)} %pad_maximum_fusion.2.refs_8_.refs_0_), channel_id=1, source_target_pairs={{0,32},{8,40},{16,48},{24,56},{32,64},{40,72},{48,80},{56,88},{64,... | collective-permute-start | bytes 2371592 | tf_op jit(solution)/shard_map/ppermute | solution.py:209
  9.9 23.7 %collective-permute-start.2 = (bf16[3088,128]{1,0:T(8,128)(2,1)S(1)}, bf16[3088,128]{1,0:T(8,128)(2,1)S(1)}, u32[]{:S(2)}, u32[]{:S(2)}) collective-permute-start(bf16[3088,128]{1,0:T(8,128)(2,1)S(1)} %pad_maximum_fusion.2.refs_8_.refs_0_), channel_id=1, source_target_pairs={{0,96},{8,104},{16,112},{24,120},{32,0},{40,8},{48,16},{56,24},{64... | collective-permute-start | bytes 2371592 | tf_op jit(solution)/shard_map/ppermute | solution.py:209
  11.5 37.6 %collective-permute-start.7 = (bf16[3088,128]{1,0:T(8,128)(2,1)S(1)}, bf16[3088,128]{1,0:T(8,128)(2,1)}, u32[]{:S(2)}, u32[]{:S(2)}) collective-permute-start(bf16[3088,128]{1,0:T(8,128)(2,1)S(1)} %pad_maximum_fusion.2.refs_8_.refs_0_), channel_id=1, source_target_pairs={{0,8},{8,0},{16,24},{24,16},{32,40},{40,32},{48,56},{56,48},{64,72... | collective-permute-start | bytes 2371592 | tf_op jit(solution)/shard_map/ppermute | solution.py:209
  26.0 23.1 %collective-permute-start.3 = (bf16[3088,128]{1,0:T(8,128)(2,1)}, bf16[3088,128]{1,0:T(8,128)(2,1)}, u32[]{:S(2)}, u32[]{:S(2)}) collective-permute-start(bf16[3088,128]{1,0:T(8,128)(2,1)} %collective-permute-done.refs_9_.refs_1_), channel_id=1, source_target_pairs={{0,32},{8,40},{16,48},{24,56},{32,64},{40,72},{48,80},{56,88},{64,... | collective-permute-start | bytes 2371592 | tf_op jit(solution)/shard_map/ppermute | solution.py:209
  27.6 22.0 %collective-permute-start.4 = (bf16[3088,128]{1,0:T(8,128)(2,1)}, bf16[3088,128]{1,0:T(8,128)(2,1)}, u32[]{:S(2)}, u32[]{:S(2)}) collective-permute-start(bf16[3088,128]{1,0:T(8,128)(2,1)} %collective-permute-done.refs_9_.refs_1_), channel_id=1, source_target_pairs={{0,96},{8,104},{16,112},{24,120},{32,0},{40,8},{48,16},{56,24},{64... | collective-permute-start | bytes 2371592 | tf_op jit(solution)/shard_map/ppermute | solution.py:209
  33.6 29.7 %collective-permute-start.5 = (bf16[3088,128]{1,0:T(8,128)(2,1)}, bf16[3088,128]{1,0:T(8,128)(2,1)S(1)}, u32[]{:S(2)}, u32[]{:S(2)}) collective-permute-start(bf16[3088,128]{1,0:T(8,128)(2,1)} %collective-permute-done.1.refs_10_.refs_2_), channel_id=1, source_target_pairs={{0,32},{8,40},{16,48},{24,56},{32,64},{40,72},{48,80},{56,88},{64,... | collective-permute-start | bytes 2371592 | tf_op jit(solution)/shard_map/ppermute | solution.py:209
  67.8 18.8 %collective-permute-start.11 = (bf16[3088,128]{1,0:T(8,128)(2,1)}, bf16[3088,128]{1,0:T(8,128)(2,1)S(1)}, u32[]{:S(2)}, u32[]{:S(2)}) collective-permute-start(bf16[3088,128]{1,0:T(8,128)(2,1)} %collective-permute-done.3.refs_12_.refs_4_), channel_id=1, source_target_pairs={{0,8},{8,0},{16,24},{24,16},{32,40},{40,32},{48,56},{56,48},{64,72... | collective-permute-start | bytes 2371592 | tf_op jit(solution)/shard_map/ppermute | solution.py:209
  82.8 21.8 %collective-permute-start.17 = (bf16[768,512]{1,0:T(8,128)(2,1)S(1)}, bf16[768,512]{1,0:T(8,128)(2,1)}, u32[]{:S(2)}, u32[]{:S(2)}) collective-permute-start(bf16[768,512]{1,0:T(8,128)(2,1)S(1)} %constant_dynamic-update-slice_fusion.refs_0_), channel_id=1, source_target_pairs={{0,6},{1,7},{2,0},{3,1},{4,2},{5,3},{6,4},{7,5},{8,14},{9,15},{10,... | collective-permute-start | bytes 2359304 | tf_op jit(solution)/shard_map/ppermute | solution.py:209
  86.6 21.8 %collective-permute-start.18 = (bf16[768,512]{1,0:T(8,128)(2,1)S(1)}, bf16[768,512]{1,0:T(8,128)(2,1)}, u32[]{:S(2)}, u32[]{:S(2)}) collective-permute-start(bf16[768,512]{1,0:T(8,128)(2,1)S(1)} %collective-permute-done.15.refs_1_), channel_id=1, source_target_pairs={{0,2},{1,3},{2,4},{3,5},{4,6},{5,7},{6,0},{7,1},{8,10},{9,11},{10,... | collective-permute-start | bytes 2359304 | tf_op jit(solution)/shard_map/ppermute | solution.py:209
  86.7 35.4 %collective-permute-start.20 = (bf16[768,512]{1,0:T(8,128)(2,1)S(1)}, bf16[768,512]{1,0:T(8,128)(2,1)}, u32[]{:S(2)}, u32[]{:S(2)}) collective-permute-start(bf16[768,512]{1,0:T(8,128)(2,1)S(1)} %collective-permute-done.16.refs_2_), channel_id=1, source_target_pairs={{0,2},{1,3},{2,4},{3,5},{4,6},{5,7},{6,0},{7,1},{8,10},{9,11},{10,... | collective-permute-start | bytes 2359304 | tf_op jit(solution)/shard_map/ppermute | solution.py:209
  86.8 35.3 %collective-permute-start.21 = (bf16[768,512]{1,0:T(8,128)(2,1)}, bf16[768,512]{1,0:T(8,128)(2,1)}, u32[]{:S(2)}, u32[]{:S(2)}) collective-permute-start(bf16[768,512]{1,0:T(8,128)(2,1)} %collective-permute-done.19.refs_5_), channel_id=1, source_target_pairs={{0,6},{1,7},{2,0},{3,1},{4,2},{5,3},{6,4},{7,5},{8,14},{9,15},{10,... | collective-permute-start | bytes 2359304 | tf_op jit(solution)/shard_map/ppermute | solution.py:209
  158.7 44.6 %collective-permute-start.22 = (bf16[8,2048,128]{2,1,0:T(8,128)(2,1)}, bf16[8,2048,128]{2,1,0:T(8,128)(2,1)}, u32[]{:S(2)}, u32[]{:S(2)}) collective-permute-start(bf16[8,2048,128]{2,1,0:T(8,128)(2,1)} %weight_grads.5), channel_id=1, source_target_pairs={{0,8},{8,0},{16,24},{24,16},{32,40},{40,32},{48,56},{56,48},{64,72... | collective-permute-start | bytes 12582920 | tf_op jit(solution)/shard_map/ppermute | solution.py:209
  166.2 31.6 %collective-permute-start.28 = (bf16[8,1024,128]{2,1,0:T(8,128)(2,1)}, bf16[8,1024,128]{2,1,0:T(8,128)(2,1)}, u32[]{:S(2)}, u32[]{:S(2)}) collective-permute-start(bf16[8,1024,128]{2,1,0:T(8,128)(2,1)} %weight_grads.7), channel_id=1, source_target_pairs={{0,8},{8,0},{16,24},{24,16},{32,40},{40,32},{48,56},{56,48},{64,72... | collective-permute-start | bytes 6291464 | tf_op jit(solution)/shard_map/ppermute | solution.py:209
  176.9 52.4 %all-to-all-start = ((bf16[8,384,512]{2,1,0:T(8,128)(2,1)}), bf16[8,384,512]{2,1,0:T(8,128)(2,1)S(1)}, u32[]{:S(2)}, u32[]{:S(2)}) async-start(bf16[8,384,512]{2,1,0:T(8,128)(2,1)} %block_product.2), calls=%async_computation | async-start | bytes 6291456 | tf_op jit(solution)/shard_map/all_to_all | solution.py:290
  200.0 24.1 %collective-permute-start.29 = (bf16[1024,128]{1,0:T(8,128)(2,1)S(1)}, bf16[1024,128]{1,0:T(8,128)(2,1)}, u32[]{:S(2)}, u32[]{:S(2)}) collective-permute-start(bf16[1024,128]{1,0:T(8,128)(2,1)S(1)} %get-tuple-element.19), channel_id=1, source_target_pairs={{0,32},{8,40},{16,48},{24,56},{32,64},{40,72},{48,80},{56,88},{64,... | collective-permute-start | bytes 786440 | tf_op jit(solution)/shard_map/ppermute | solution.py:209
  200.2 23.9 %collective-permute-start.31 = (bf16[1024,128]{1,0:T(8,128)(2,1)S(1)}, bf16[1024,128]{1,0:T(8,128)(2,1)}, u32[]{:S(2)}, u32[]{:S(2)}) collective-permute-start(bf16[1024,128]{1,0:T(8,128)(2,1)S(1)} %get-tuple-element.20), channel_id=1, source_target_pairs={{0,96},{8,104},{16,112},{24,120},{32,0},{40,8},{48,16},{56,24},{64... | collective-permute-start | bytes 786440 | tf_op jit(solution)/shard_map/ppermute | solution.py:209
  206.9 19.5 %collective-permute-start.23 = (bf16[2048,128]{1,0:T(8,128)(2,1)S(1)}, bf16[2048,128]{1,0:T(8,128)(2,1)S(1)}, u32[]{:S(2)}, u32[]{:S(2)}) collective-permute-start(bf16[2048,128]{1,0:T(8,128)(2,1)S(1)} %get-tuple-element.13), channel_id=1, source_target_pairs={{0,32},{8,40},{16,48},{24,56},{32,64},{40,72},{48,80},{56,88},{64,... | collective-permute-start | bytes 1572872 | tf_op jit(solution)/shard_map/ppermute | solution.py:209
  206.9 19.5 %collective-permute-start.25 = (bf16[2048,128]{1,0:T(8,128)(2,1)S(1)}, bf16[2048,128]{1,0:T(8,128)(2,1)S(1)}, u32[]{:S(2)}, u32[]{:S(2)}) collective-permute-start(bf16[2048,128]{1,0:T(8,128)(2,1)S(1)} %get-tuple-element.14), channel_id=1, source_target_pairs={{0,96},{8,104},{16,112},{24,120},{32,0},{40,8},{48,16},{56,24},{64... | collective-permute-start | bytes 1572872 | tf_op jit(solution)/shard_map/ppermute | solution.py:209
  229.3 54.1 %all-to-all-start.1 = ((bf16[8,384,512]{2,1,0:T(8,128)(2,1)}), bf16[8,384,512]{2,1,0:T(8,128)(2,1)}, u32[]{:S(2)}, u32[]{:S(2)}) async-start(bf16[8,384,512]{2,1,0:T(8,128)(2,1)} %block_product.3), calls=%async_computation.1 | async-start | bytes 6291456 | tf_op jit(solution)/shard_map/all_to_all | solution.py:290
  236.2 41.0 %collective-permute-start.26 = (bf16[4096,128]{1,0:T(8,128)(2,1)S(1)}, bf16[4096,128]{1,0:T(8,128)(2,1)S(1)}, u32[]{:S(2)}, u32[]{:S(2)}) collective-permute-start(bf16[4096,128]{1,0:T(8,128)(2,1)S(1)} %pad_maximum_fusion.1), channel_id=1, source_target_pairs={{0,96},{8,104},{16,112},{24,120},{32,0},{40,8},{48,16},{56,24},{64... | collective-permute-start | bytes 3145736 | tf_op jit(solution)/shard_map/ppermute | solution.py:209
  236.8 40.5 %collective-permute-start.24 = (bf16[4096,128]{1,0:T(8,128)(2,1)S(1)}, bf16[4096,128]{1,0:T(8,128)(2,1)S(1)}, u32[]{:S(2)}, u32[]{:S(2)}) collective-permute-start(bf16[4096,128]{1,0:T(8,128)(2,1)S(1)} %pad_maximum_fusion), channel_id=1, source_target_pairs={{0,32},{8,40},{16,48},{24,56},{32,64},{40,72},{48,80},{56,88},{64,... | collective-permute-start | bytes 3145736 | tf_op jit(solution)/shard_map/ppermute | solution.py:209
  238.4 32.8 %collective-permute-start.32 = (bf16[2048,128]{1,0:T(8,128)(2,1)S(1)}, bf16[2048,128]{1,0:T(8,128)(2,1)S(1)}, u32[]{:S(2)}, u32[]{:S(2)}) collective-permute-start(bf16[2048,128]{1,0:T(8,128)(2,1)S(1)} %pad_maximum_fusion.4), channel_id=1, source_target_pairs={{0,96},{8,104},{16,112},{24,120},{32,0},{40,8},{48,16},{56,24},{64... | collective-permute-start | bytes 1572872 | tf_op jit(solution)/shard_map/ppermute | solution.py:209
  240.2 32.6 %collective-permute-start.30 = (bf16[2048,128]{1,0:T(8,128)(2,1)S(1)}, bf16[2048,128]{1,0:T(8,128)(2,1)S(1)}, u32[]{:S(2)}, u32[]{:S(2)}) collective-permute-start(bf16[2048,128]{1,0:T(8,128)(2,1)S(1)} %pad_maximum_fusion.3), channel_id=1, source_target_pairs={{0,32},{8,40},{16,48},{24,56},{32,64},{40,72},{48,80},{56,88},{64,... | collective-permute-start | bytes 1572872 | tf_op jit(solution)/shard_map/ppermute | solution.py:209
  (40 other events, 737.0 us)

commit v3 on v1

--- a/solution.py
+++ b/solution.py
@@ -10,8 +10,7 @@
 BLK = 128
 NZ = 4
 FB_DEV = 16
-X_SIZE = 4
-VMEM_BYTES = 56 * 1024 * 1024
+RING = 4
 NT = (((1,), (1,)), ((), ()))
 TN = (((0,), (0,)), ((), ()))
 
@@ -58,23 +57,42 @@
             gate_delta_ref[f] = (grad * up * sig * (1.0 + gate * (1.0 - sig))).astype(jnp.bfloat16)
 
 
-def weight_grads_kernel(scale, order, cols, x_ref, hidden_ref, gate_delta_ref, up_delta_ref, o_ref):
+def weight_grads_kernel(scale, count, at_x, owners, cols, x_ref, *refs):
+    hidden_ref, gate_delta_ref, up_delta_ref = refs[:3]
     step = pl.program_id(0)
+    owner = owners[step]
     tok_rows = hidden_ref.shape[1]
-    for i in range(4):
-        owner = order[step] * 2 + i // 2
-        feat = x_ref[0, :tok_rows, i * BLK : (i + 1) * BLK]
-        cot = x_ref[0, tok_rows:, i * BLK : (i + 1) * BLK]
+    for i in range(2):
+        at = pl.ds(pl.multiple_of((owner % 2) * 2 * BLK + i * BLK, BLK), BLK)
+        feat = x_ref[0, :tok_rows, at]
+        cot = x_ref[0, tok_rows:, at]
         for t, source in enumerate((gate_delta_ref, up_delta_ref, hidden_ref)):
             left = cot if t == 2 else feat
-            base = owner * 24 + t * 8 + (i % 2) * NZ
+            base = owner * 24 + t * 8 + i * NZ
             right = lanes([source[cols[base + s]] for s in range(NZ)])
             prod = lax.dot_general(left, right, TN, preferred_element_type=jnp.float32) * scale
-            row = (t * 2 + i % 2) * NZ * BLK
             for s in range(NZ):
-                o_ref[i // 2, row + s * BLK : row + (s + 1) * BLK, :] = prod[
-                    :, s * BLK : (s + 1) * BLK
-                ].astype(jnp.bfloat16)
+                row = (t * 2 + i) * NZ * BLK + s * BLK
+                value = prod[:, s * BLK : (s + 1) * BLK]
+                if count:
+                    got = refs[3][0, row : row + BLK, :].astype(jnp.float32)
+                    value = value + got
+                    held = refs[4 + count]
+                    held[step, row : row + BLK, :] = value.astype(jnp.bfloat16)
+                else:
+                    refs[-1][0, row : row + BLK, :] = value.astype(jnp.bfloat16)
+    if count:
+        outs, held, sems = refs[4 : 4 + count], refs[4 + count], refs[5 + count]
+        for n in range(count):
+
+            @pl.when(step == n)
+            def _():
+                pltpu.make_async_copy(held.at[n], outs[n], sems.at[n]).start()
+
+        @pl.when(step == count - 1)
+        def _():
+            for n in range(count):
+                pltpu.make_async_copy(held.at[n], outs[n], sems.at[n]).wait()
 
 
 def product_kernel(tensors, cols, w_ref, *refs):
@@ -97,9 +115,9 @@
     return pl.CostEstimate(flops=flops, bytes_accessed=moved, transcendentals=0)
 
 
-def params():
+def params(megabytes):
     return pltpu.CompilerParams(
-        dimension_semantics=("arbitrary",), vmem_limit_bytes=VMEM_BYTES
+        dimension_semantics=("arbitrary",), vmem_limit_bytes=megabytes * 1024 * 1024
     )
 
 
@@ -126,29 +144,45 @@
             out_specs=[whole(shape)] * 3,
             scratch_shapes=[pltpu.VMEM((3,) + shape, jnp.float32)],
         ),
-        compiler_params=params(),
+        compiler_params=params(56),
         cost_estimate=cost(10**10, 30 * 10**6),
         name="local_sums",
     )(order, cols, feats, weights)
 
 
-def weight_grads(order, cols, feats, hidden, gate_delta, up_delta, scale):
-    steps, rows2, width = feats.shape
+def weight_grads(at_x, owners, cols, feats, sources, scale, got=None):
+    _, rows2, width = feats.shape
+    count = owners.shape[0]
     rows = 3 * 2 * NZ * BLK
+    block = pl.BlockSpec((1, rows, BLK), lambda j, *_: (j, 0, 0))
+    in_specs = [pl.BlockSpec((1, rows2, width), lambda j, at_x, *_: (at_x[j], 0, 0))]
+    in_specs += [pl.BlockSpec(memory_space=pltpu.VMEM)] * 3
+    if got is None:
+        out_shape = jax.ShapeDtypeStruct((count, rows, BLK), jnp.bfloat16)
+        out_specs, scratch, extra = block, [], ()
+    else:
+        in_specs.append(block)
+        out_shape = (jax.ShapeDtypeStruct((rows, BLK), jnp.bfloat16),) * count
+        out_specs = (pl.BlockSpec(memory_space=pl.ANY),) * count
+        scratch = [
+            pltpu.VMEM((count, rows, BLK), jnp.bfloat16),
+            pltpu.SemaphoreType.DMA((count,)),
+        ]
+        extra = (got,)
     return pl.pallas_call(
-        functools.partial(weight_grads_kernel, scale),
-        out_shape=jax.ShapeDtypeStruct((2 * steps, rows, BLK), jnp.bfloat16),
+        functools.partial(weight_grads_kernel, scale, 0 if got is None else count),
+        out_shape=out_shape,
         grid_spec=pltpu.PrefetchScalarGridSpec(
-            num_scalar_prefetch=2,
-            grid=(steps,),
-            in_specs=[pl.BlockSpec((1, rows2, width), lambda j, order, cols: (j, 0, 0))]
-            + [whole(hidden.shape)] * 3,
-            out_specs=pl.BlockSpec((2, rows, BLK), lambda j, order, cols: (order[j], 0, 0)),
+            num_scalar_prefetch=3,
+            grid=(count,),
+            in_specs=in_specs,
+            out_specs=out_specs,
+            scratch_shapes=scratch,
         ),
-        compiler_params=params(),
-        cost_estimate=cost(10**10, 25 * 10**6),
+        compiler_params=params(28),
+        cost_estimate=cost(count * 10**9, count * 3 * 10**6),
         name="weight_grads",
-    )(order, cols, feats, hidden, gate_delta, up_delta)
+    )(at_x, owners, cols, feats, *sources, *extra)
 
 
 def block_product(tensors, cols, weights, sources):
@@ -166,32 +200,51 @@
             + [whole(sources[0].shape)] * len(sources),
             out_specs=pl.BlockSpec((1, tok_rows, 4 * BLK), lambda j, cols: (j, 0, 0)),
         ),
-        compiler_params=params(),
+        compiler_params=params(40),
         cost_estimate=cost(len(tensors) * 3 * 10**9, len(tensors) * 7 * 10**6),
         name="block_product",
     )(cols, weights, *sources)
 
 
-def over_x(value, shift, cols):
-    pairs = [(c, ((c // 2 + shift) % X_SIZE) * 2 + c % 2) for c in range(cols)]
-    return lax.ppermute(value, "col", pairs)
-
-
-def gather_features(own, cols):
-    me = lax.axis_index("col")
-    x, z = me // 2, me % 2
-    near = lax.ppermute(own, "col", [(c, c ^ 1) for c in range(cols)])
-    own_w, own_e = over_x(own, 1, cols), over_x(own, -1, cols)
-    near_w, near_e = over_x(near, 1, cols), over_x(near, -1, cols)
-    own_far, near_far = over_x(own_w, 1, cols), over_x(near_e, -1, cols)
-    pieces = [own, near, own_w, own_e, near_w, near_e, own_far, near_far]
-    shifts = [(0, 0), (0, 1), (-1, 0), (1, 0), (-1, 1), (1, 1), (2, 0), (2, 1)]
-    order = [((x + dx) % X_SIZE) * 2 + (z + dz) % 2 for dx, dz in shifts]
+def permute(value, axis, target):
+    return lax.ppermute(value, axis, [(i, target(i)) for i in range(lax.axis_size(axis))])
+
+
+def over_x(value, shift):
+    return permute(value, "col", lambda c: ((c // 2 + shift) % RING) * 2 + c % 2)
+
+
+def over_y(value, shift):
+    return permute(value, "row", lambda r: ((r // 4 + shift) % RING) * 4 + r % 4)
+
+
+def gather_features(own):
+    x, z = lax.axis_index("col") // 2, lax.axis_index("col") % 2
+    near = permute(own, "col", lambda c: c ^ 1)
+    own_m, own_p = over_x(own, 1), over_x(own, -1)
+    near_m, near_p = over_x(near, 1), over_x(near, -1)
+    own_far, near_far = over_x(own_m, 1), over_x(near_p, -1)
+    pieces = [own, near, own_p, near_p, own_far, near_far, own_m, near_m]
+    order = [((x + n // 2) % RING) * 2 + (z + n) % 2 for n in range(8)]
     return jnp.stack(pieces), jnp.stack(order).astype(jnp.int32)
 
 
+def slot_tables(shifts, half):
+    x, z = lax.axis_index("col") // 2, lax.axis_index("col") % 2
+    row = lax.axis_index("row")
+    chips = [((row // 4 + d) % RING, (row // 2 + e) % 2) for d, e in shifts]
+    at_x = [((y - x) % RING) * 2 + (h - z) % 2 for y, h in chips]
+    owners = [y * 4 + h * 2 + (row + half) % 2 for y, h in chips]
+    return jnp.stack(at_x).astype(jnp.int32), jnp.stack(owners).astype(jnp.int32)
+
+
+FAR = ((2, 0), (2, 1))
+NEAR = ((1, 1), (-1, 1), (1, 0), (-1, 0))
+OWN = ((0, 0), (0, 1))
+
+
 def body(tokens, cotangent, gate_blocks, up_blocks, down_blocks, gate_cols, up_cols, down_cols):
-    n_row, n_col = lax.axis_size("row"), lax.axis_size("col")
+    n_row = lax.axis_size("row")
     tok_rows = tokens.shape[0]
     tables = jnp.concatenate(
         [jnp.bitwise_and(t, FB_DEV - 1).reshape(1, -1) for t in (gate_cols, up_cols, down_cols)], 1
@@ -201,23 +254,53 @@
         [b.reshape(-1, BLK) for b in (gate_blocks, up_blocks, down_blocks)] + [tables], 0
     )
     weights = lax.all_gather(packed, "row", axis=0, tiled=True).reshape(n_row, -1, BLK)
-    feats, order = gather_features(jnp.concatenate([tokens, cotangent], 0), n_col)
+    feats, order = gather_features(jnp.concatenate([tokens, cotangent], 0))
     at = packed.shape[0] - 16
     cols = weights[:, at, : 3 * 2 * NZ].astype(jnp.int32).reshape(-1)
     hidden, gate_delta, up_delta = local_sums(order, cols, feats, weights)
+    sources = (hidden, gate_delta, up_delta)
     scale = float(tok_rows * n_row) ** (-0.5)
-    terms = weight_grads(order, cols, feats, hidden, gate_delta, up_delta, scale)
-    grads = lax.psum_scatter(terms.reshape(-1, BLK), "row", scatter_dimension=0, tiled=True)
+
+    def after(value):
+        return lax.optimization_barrier((cols, value))[0]
+
+    def theirs(shifts, cols):
+        return weight_grads(*slot_tables(shifts, 1), cols, feats, sources, scale)
+
+    def mine(shifts, cols, got):
+        return weight_grads(*slot_tables(shifts, 0), cols, feats, sources, scale, got)
+
+    def other_core(value):
+        return permute(value, "row", lambda r: r ^ 1)
+
+    def reduce_features(partial_value):
+        parts = lax.all_to_all(partial_value, "col", 0, 0, tiled=True)
+        return jnp.sum(parts.astype(jnp.float32), axis=0).astype(jnp.bfloat16)
+
+    def total(*values):
+        return sum(v.astype(jnp.float32) for v in values).astype(jnp.bfloat16)
+
+    out_parts = block_product((2,), cols, weights, (hidden,))
+    output = reduce_features(out_parts)
+    their_far = theirs(FAR, after(out_parts))
+    got_far = other_core(their_far)
+    their_near = theirs(NEAR, after(their_far))
+    got_near = other_core(their_near)
+    far0, far1 = mine(FAR, after(their_near), got_far)
+    far_p, far_m = over_y(far0, 1), over_y(far1, -1)
+    in_parts = block_product((0, 1), after(far0), weights, (gate_delta, up_delta))
+    tokens_grad = reduce_features(in_parts)
+    their_own = theirs(OWN, after(in_parts))
+    got_own = other_core(their_own)
+    p1, m1, p0, m0 = mine(NEAR, after(their_own), got_near)
+    from_m1, from_p1 = over_y(p1, 1), over_y(total(m1, far_m), -1)
+    from_m0, from_p0 = over_y(total(p0, far_p), 1), over_y(m0, -1)
+    own0, own1 = mine(OWN, after(p1), got_own)
+    last = permute(total(own1, from_m1, from_p1), "row", lambda r: r ^ 2)
+    grads = total(own0, from_m0, from_p0, last)
     gate_grad, up_grad, down_grad = (
         g.reshape(gate_blocks.shape) for g in jnp.split(grads, 3, axis=0)
     )
-
-    def reduce_features(partial_value):
-        parts = lax.all_to_all(partial_value, "col", 0, 0, tiled=True)
-        return jnp.sum(parts.astype(jnp.float32), axis=0).astype(jnp.bfloat16)
-
-    output = reduce_features(block_product((2,), cols, weights, (hidden,)))
-    tokens_grad = reduce_features(block_product((0, 1), cols, weights, (gate_delta, up_delta)))
     return (output, tokens_grad, gate_grad, up_grad, down_grad)
 
 

time: 314 us -> 273 us (0.87)
  waiting for transfers between devices: 196 us -> 122 us
  starting transfers between devices: 19.6 us -> 30.5 us
  other arithmetic: 9.5 us -> 19.3 us
  Pallas kernels: 59.5 us -> 68.3 us
  local copies, waits for them, and re-layouts: 13.2 us -> 16.8 us
    all_to_all x2, waiting for transfers between devices: 75.9 us -> 27.4 us  [reduce_features(): parts = lax.all_to_all(partial_value, 'col', 0, 0, tiled=True)]
    reduce_scatter x1 -> x0, waiting for transfers between devices: 40.2 us -> none  [body(): lax.psum_scatter(terms.reshape(-1, BLK), 'row', scatter_dimension=0, tile...]
    ppermute x7 -> x17, waiting for transfers between devices: 44.3 us -> 74.8 us  [permute(): lax.ppermute(value, axis, [(i, target(i)) for i in range(lax.axis_size(ax...]
    all_gather x1, waiting for transfers between devices: 35.9 us -> 20.4 us  [body(): lax.all_gather(packed, 'row', axis=0, tiled=True).reshape(n_row, -1, BLK)]
    pallas_call x1 -> x6, Pallas kernels: 14.9 us -> 28.7 us  [weight_grads(): pl.pallas_call(functools.partial(weight_grads_kernel, scale, 0 if got is...]
    ppermute x7 -> x17, starting transfers between devices: 10.7 us -> 21.5 us  [permute(): lax.ppermute(value, axis, [(i, target(i)) for i in range(lax.axis_size(ax...]
    convert_element_type x0 -> x4, other arithmetic: none -> 7.36 us  [total(): return sum((v.astype(jnp.float32) for v in values)).astype(jnp.bfloat16)]
    unnamed x8 -> x38, local copies, waits for them, and re-layouts: 7.72 us -> 13.4 us
  transfers between devices with their start and end apart: 11 -> 20, of which waited for: 8 -> 10; matrix products, arithmetic and copies ran while one was open for 5% -> 8% of each run, Pallas kernels for 8% -> 11%
where the time goes in v3:
time: 273 us; the launch traced here: 272 us
  waiting for transfers between devices  122 us (45%)
  Pallas kernels  68.3 us (25%)
  starting transfers between devices  30.5 us (11%)
  other arithmetic  19.3 us (7%)
  local copies, waits for them, and re-layouts  16.8 us (6%)
  between operations  14.3 us (5%)
    ppermute x17, waiting for transfers between devices, permute(): lax.ppermute(value, axis, [(i, target(i)) for i in range(lax.axis_size(ax...  74.8 us
    pallas_call x6, Pallas kernels, weight_grads(): pl.pallas_call(functools.partial(weight_grads_kernel, scale, 0 if got is...  28.7 us
    all_to_all x2, waiting for transfers between devices, reduce_features(): parts = lax.all_to_all(partial_value, 'col', 0, 0, tiled=True)  27.4 us
    ppermute x17, starting transfers between devices, permute(): lax.ppermute(value, axis, [(i, target(i)) for i in range(lax.axis_size(ax...  21.5 us
    pallas_call x1, Pallas kernels, local_sums(): pl.pallas_call(sums_kernel, out_shape=(out, out, out), grid_spec=pltpu.Pr...  21 us
    all_gather x1, waiting for transfers between devices, body(): lax.all_gather(packed, 'row', axis=0, tiled=True).reshape(n_row, -1, BLK)  20.4 us
    pallas_call x2, Pallas kernels, block_product(): pl.pallas_call(functools.partial(product_kernel, tensors), out_shape=jax....  18.6 us
    unnamed x38, local copies, waits for them, and re-layouts  13.4 us
  transfers between devices with their start and end apart: 20, of which 10 were waited for; matrix products, arithmetic and copies ran while one was open for 8% of the time, Pallas kernels for 11%

profile of v3, /device:TPU:0, one launch (start us, length us, event | category | flops | bytes accessed | tf_op | source)
XLA Modules:
  0.0 271.7 jit_solution(12855445375659833583)
XLA Ops:
  16.4 22.6 %collective-permute-done = bf16[768,512]{1,0:T(8,128)(2,1)S(1)} collective-permute-done((bf16[768,512]{1,0:T(8,128)(2,1)S(1)}, bf16[768,512]{1,0:T(8,128)(2,1)S(1)}, u32[]{:S(2)}, u32[]{:S(2)}) %collective-permute-start) | collective-permute-done | bytes 786464 | tf_op jit(solution)/shard_map/ppermute | solution.py:210
  46.3 13.3 %collective-permute-done.2 = bf16[768,512]{1,0:T(8,128)(2,1)S(1)} collective-permute-done((bf16[768,512]{1,0:T(8,128)(2,1)S(1)}, bf16[768,512]{1,0:T(8,128)(2,1)S(1)}, u32[]{:S(2)}, u32[]{:S(2)}) %collective-permute-start.2) | collective-permute-done | bytes 786464 | tf_op jit(solution)/shard_map/ppermute | solution.py:210
  59.5 3.7 %collective-permute-start.5 = (bf16[768,512]{1,0:T(8,128)(2,1)S(1)}, bf16[768,512]{1,0:T(8,128)(2,1)S(1)}, u32[]{:S(2)}, u32[]{:S(2)}) collective-permute-start(bf16[768,512]{1,0:T(8,128)(2,1)S(1)} %collective-permute-done.2), channel_id=1, source_target_pairs={{0,6},{1,7},{2,0},{3,1},{4,2},{5,3},{6,4},{7,5},{8,14},{9,15},{10,... | collective-permute-start | bytes 2359304 | tf_op jit(solution)/shard_map/ppermute | solution.py:210
  63.2 13.2 %collective-permute-done.1 = bf16[768,512]{1,0:T(8,128)(2,1)} collective-permute-done((bf16[768,512]{1,0:T(8,128)(2,1)S(1)}, bf16[768,512]{1,0:T(8,128)(2,1)}, u32[]{:S(2)}, u32[]{:S(2)}) %collective-permute-start.1) | collective-permute-done | bytes 786464 | tf_op jit(solution)/shard_map/ppermute | solution.py:210
  80.4 8.5 %collective-permute-done.5 = bf16[768,512]{1,0:T(8,128)(2,1)S(1)} collective-permute-done((bf16[768,512]{1,0:T(8,128)(2,1)S(1)}, bf16[768,512]{1,0:T(8,128)(2,1)S(1)}, u32[]{:S(2)}, u32[]{:S(2)}) %collective-permute-start.5) | collective-permute-done | bytes 786464 | tf_op jit(solution)/shard_map/ppermute | solution.py:210
  91.7 20.4 %all-gather.2.cloned.1.call-done = bf16[49408,128]{1,0:T(8,128)(2,1)} async-done(((bf16[3088,128]{1,0:T(8,128)(2,1)}), bf16[49408,128]{1,0:T(8,128)(2,1)}) %all-gather.2.cloned.1.call-update) | async-done | bytes 12648464 | tf_op jit(solution)/shard_map/all_gather | solution.py:256
  113.6 21.0 %local_sums.1 = (bf16[16,384,128]{2,1,0:T(8,128)(2,1)}, bf16[16,384,128]{2,1,0:T(8,128)(2,1)}, bf16[16,384,128]{2,1,0:T(8,128)(2,1)}) custom-call(s32[8]{0:T(128)} %stack.172.order, s32[384]{0:T(512)} %reshape.100.cols, bf16[8,768,512]{2,1,0:T(8,128)(2,1)} %bitcast_dynamic-update-slice_fusion.x_ref, bf16[16,3088,128]{2,1,0:T(8,128)(2,1)} %bitcast.56), custom_call_target="tpu_custom_call" | custom-call | flops 10000000000 | bytes 30000000 | tf_op jit(solution)/shard_map/local_sums/pallas_call | solution.py:134
  136.0 8.0 %block_product.2 = bf16[8,384,512]{2,1,0:T(8,128)(2,1)S(1)} custom-call(s32[384]{0:T(512)S(1)} %copy-done.13, bf16[16,3088,128]{2,1,0:T(8,128)(2,1)} %bitcast.57, bf16[16,384,128]{2,1,0:T(8,128)(2,1)S(1)} %copy-done), custom_call_target="tpu_custom_call" | custom-call | flops 3000000000 | bytes 7000000 | tf_op jit(solution)/shard_map/block_product/pallas_call | solution.py:193
  144.1 4.4 %weight_grads.6 = bf16[2,3072,128]{2,1,0:T(8,128)(2,1)} custom-call(s32[2]{0:T(128)S(1)} %get-tuple-element.44.at_x, s32[2]{0:T(128)S(1)} %get-tuple-element.45.owners, s32[384]{0:T(512)S(1)} %copy-done.13, bf16[8,768,512]{2,1,0:T(8,128)(2,1)} %bitcast_dynamic-update-slice_fusion.x_ref, bf16[16,384,128]{2,1,0:T(8,128)(2,1)S(1)} %copy-done.1, ...), custom_call_target="tpu_custom_call" | custom-call | flops 2000000000 | bytes 6000000 | tf_op jit(solution)/shard_map/weight_grads/pallas_call | solution.py:172
  148.5 6.0 %weight_grads.7 = bf16[4,3072,128]{2,1,0:T(8,128)(2,1)} custom-call(s32[4]{0:T(128)S(1)} %get-tuple-element.46.at_x, s32[4]{0:T(128)S(1)} %get-tuple-element.47.owners, s32[384]{0:T(512)S(1)} %copy-done.13, bf16[8,768,512]{2,1,0:T(8,128)(2,1)} %bitcast_dynamic-update-slice_fusion.x_ref, bf16[16,384,128]{2,1,0:T(8,128)(2,1)S(1)} %copy-done.1, ...), custom_call_target="tpu_custom_call" | custom-call | flops 4000000000 | bytes 12000000 | tf_op jit(solution)/shard_map/weight_grads/pallas_call | solution.py:172
  155.0 4.5 %all-to-all-start = ((bf16[8,384,512]{2,1,0:T(8,128)(2,1)}), bf16[8,384,512]{2,1,0:T(8,128)(2,1)}, u32[]{:S(2)}, u32[]{:S(2)}) async-start(bf16[8,384,512]{2,1,0:T(8,128)(2,1)} %copy-done.7), calls=%async_computation | async-start | bytes 6291456 | tf_op jit(solution)/shard_map/all_to_all | solution.py:277
  164.1 4.2 %weight_grads.8 = (bf16[3072,128]{1,0:T(8,128)(2,1)}, bf16[3072,128]{1,0:T(8,128)(2,1)}) custom-call(s32[2]{0:T(128)S(1)} %get-tuple-element.44.at_x, s32[2]{0:T(128)S(1)} %pad_add_fusion.1.owners, s32[384]{0:T(512)S(1)} %copy-done.13, bf16[8,768,512]{2,1,0:T(8,128)(2,1)} %bitcast_dynamic-update-slice_fusion.x_ref, bf16[16,384,128]{2,1,0:T(8,128)(2,1)S(1)} %copy-done.1, ...), custom_call_target="tpu_custom_call" | custom-call | flops 2000000000 | bytes 6000000 | tf_op jit(solution)/shard_map/weight_grads/pallas_call | solution.py:172
  168.5 3.1 %collective-permute-start.14 = (bf16[3072,128]{1,0:T(8,128)(2,1)}, bf16[3072,128]{1,0:T(8,128)(2,1)}, u32[]{:S(2)}, u32[]{:S(2)}) collective-permute-start(bf16[3072,128]{1,0:T(8,128)(2,1)} %get-tuple-element.40), channel_id=1, source_target_pairs={{0,96},{8,104},{16,112},{24,120},{32,0},{40,8},{48,16},{56,24},{64... | collective-permute-start | bytes 2359304 | tf_op jit(solution)/shard_map/ppermute | solution.py:210
  171.6 10.5 %block_product.3 = bf16[8,384,512]{2,1,0:T(8,128)(2,1)S(1)} custom-call(s32[384]{0:T(512)S(1)} %copy-done.13, bf16[16,3088,128]{2,1,0:T(8,128)(2,1)} %bitcast.58, bf16[16,384,128]{2,1,0:T(8,128)(2,1)S(1)} %copy-done.2, bf16[16,384,128]{2,1,0:T(8,128)(2,1)S(1)} %copy-done.5), custom_call_target="tpu_custom_call" | custom-call | flops 6000000000 | bytes 14000000 | tf_op jit(solution)/shard_map/block_product/pallas_call | solution.py:193
  182.2 4.4 %weight_grads.9 = bf16[2,3072,128]{2,1,0:T(8,128)(2,1)} custom-call(s32[2]{0:T(128)S(1)} %get-tuple-element.48.at_x, s32[2]{0:T(128)S(1)} %get-tuple-element.49.owners, s32[384]{0:T(512)S(1)} %copy-done.13, bf16[8,768,512]{2,1,0:T(8,128)(2,1)} %bitcast_dynamic-update-slice_fusion.x_ref, bf16[16,384,128]{2,1,0:T(8,128)(2,1)S(1)} %copy-done.1, ...), custom_call_target="tpu_custom_call" | custom-call | flops 2000000000 | bytes 6000000 | tf_op jit(solution)/shard_map/weight_grads/pallas_call | solution.py:172
  186.6 6.5 %weight_grads.10 = (bf16[3072,128]{1,0:T(8,128)(2,1)}, bf16[3072,128]{1,0:T(8,128)(2,1)S(1)}, bf16[3072,128]{1,0:T(8,128)(2,1)S(1)}, bf16[3072,128]{1,0:T(8,128)(2,1)}) custom-call(s32[4]{0:T(128)S(1)} %get-tuple-element.46.at_x, s32[4]{0:T(128)S(1)} %pad_add_fusion.7.owners, s32[384]{0:T(512)S(1)} %copy-done.13, ...), custom_call_target="tpu_custom_call" | custom-call | flops 4000000000 | bytes 12000000 | tf_op jit(solution)/shard_map/weight_grads/pallas_call | solution.py:172
  194.8 10.7 %all-to-all-done = bf16[8,384,512]{2,1,0:T(8,128)(2,1)} async-done(((bf16[8,384,512]{2,1,0:T(8,128)(2,1)}), bf16[8,384,512]{2,1,0:T(8,128)(2,1)}, u32[]{:S(2)}, u32[]{:S(2)}) %all-to-all-start) | async-done | bytes 3145760 | tf_op jit(solution)/shard_map/all_to_all | solution.py:277
  205.5 4.5 %all-to-all-start.1 = ((bf16[8,384,512]{2,1,0:T(8,128)(2,1)}), bf16[8,384,512]{2,1,0:T(8,128)(2,1)}, u32[]{:S(2)}, u32[]{:S(2)}) async-start(bf16[8,384,512]{2,1,0:T(8,128)(2,1)} %copy-done.8), calls=%async_computation.1 | async-start | bytes 6291456 | tf_op jit(solution)/shard_map/all_to_all | solution.py:277
  218.3 3.3 %weight_grads.11 = (bf16[3072,128]{1,0:T(8,128)(2,1)S(1)}, bf16[3072,128]{1,0:T(8,128)(2,1)S(1)}) custom-call(s32[2]{0:T(128)S(1)} %get-tuple-element.48.at_x, s32[2]{0:T(128)S(1)} %pad_add_fusion.6.owners, s32[384]{0:T(512)S(1)} %copy-done.13, bf16[8,768,512]{2,1,0:T(8,128)(2,1)} %bitcast_dynamic-update-slice_fusion.x_ref, ...), custom_call_target="tpu_custom_call" | custom-call | flops 2000000000 | bytes 6000000 | tf_op jit(solution)/shard_map/weight_grads/pallas_call | solution.py:172
  221.6 10.6 %collective-permute-done.15 = bf16[3072,128]{1,0:T(8,128)(2,1)S(1)} collective-permute-done((bf16[3072,128]{1,0:T(8,128)(2,1)S(1)}, bf16[3072,128]{1,0:T(8,128)(2,1)S(1)}, u32[]{:S(2)}, u32[]{:S(2)}) %collective-permute-start.15) | collective-permute-done | bytes 786464 | tf_op jit(solution)/shard_map/ppermute | solution.py:210
  235.3 3.3 %reduce_sum.24 = bf16[384,512]{1,0:T(8,128)(2,1)} reduce(bf16[8,384,512]{2,1,0:T(8,128)(2,1)} %all-to-all-done, bf16[]{:T(256)} %constant.386.clone.1), dimensions={0}, to_apply=%region_0.1 | reduce | flops 1376256 | bytes 3538946 | tf_op jit(solution)/shard_map/reduce_sum | solution.py:278
  238.6 16.6 %all-to-all-done.1 = bf16[8,384,512]{2,1,0:T(8,128)(2,1)} async-done(((bf16[8,384,512]{2,1,0:T(8,128)(2,1)}), bf16[8,384,512]{2,1,0:T(8,128)(2,1)}, u32[]{:S(2)}, u32[]{:S(2)}) %all-to-all-start.1) | async-done | bytes 3145760 | tf_op jit(solution)/shard_map/all_to_all | solution.py:277
  255.2 3.2 %reduce_sum.25 = bf16[384,512]{1,0:T(8,128)(2,1)} reduce(bf16[8,384,512]{2,1,0:T(8,128)(2,1)} %all-to-all-done.1, bf16[]{:T(256)} %constant.386.clone.1), dimensions={0}, to_apply=%region_1.2 | reduce | flops 1376256 | bytes 3538946 | tf_op jit(solution)/shard_map/reduce_sum | solution.py:278
  258.4 3.7 %collective-permute-done.16 = bf16[3072,128]{1,0:T(8,128)(2,1)S(1)} collective-permute-done((bf16[3072,128]{1,0:T(8,128)(2,1)S(1)}, bf16[3072,128]{1,0:T(8,128)(2,1)S(1)}, u32[]{:S(2)}, u32[]{:S(2)}) %collective-permute-start.16) | collective-permute-done | bytes 786464 | tf_op jit(solution)/shard_map/ppermute | solution.py:210
  (90 shorter events, 47.4 us)
Async XLA Ops:
  7.2 104.9 %all-gather.2.cloned.1.call-start = ((), (), s32[]{:S(2)}) async-start(), calls=%async_computation.2 | async-start | bytes 13438976 | tf_op jit(solution)/shard_map/all_gather | solution.py:256
  12.8 26.1 %collective-permute-start = (bf16[768,512]{1,0:T(8,128)(2,1)S(1)}, bf16[768,512]{1,0:T(8,128)(2,1)S(1)}, u32[]{:S(2)}, u32[]{:S(2)}) collective-permute-start(bf16[768,512]{1,0:T(8,128)(2,1)S(1)} %constant_dynamic-update-slice_fusion), channel_id=1, source_target_pairs={{0,1},{1,0},{2,3},{3,2},{4,5},{5,4},{6,7},{7,6},{8,9},{9,8},{10,11... | collective-permute-start | bytes 2359304 | tf_op jit(solution)/shard_map/ppermute | solution.py:210
  14.9 30.4 %collective-permute-start.3 = (bf16[768,512]{1,0:T(8,128)(2,1)S(1)}, bf16[768,512]{1,0:T(8,128)(2,1)S(1)}, u32[]{:S(2)}, u32[]{:S(2)}) collective-permute-start(bf16[768,512]{1,0:T(8,128)(2,1)S(1)} %constant_dynamic-update-slice_fusion), channel_id=1, source_target_pairs={{0,2},{1,3},{2,4},{3,5},{4,6},{5,7},{6,0},{7,1},{8,10},{9,11},{10,... | collective-permute-start | bytes 2359304 | tf_op jit(solution)/shard_map/ppermute | solution.py:210
  38.9 20.6 %collective-permute-start.2 = (bf16[768,512]{1,0:T(8,128)(2,1)S(1)}, bf16[768,512]{1,0:T(8,128)(2,1)S(1)}, u32[]{:S(2)}, u32[]{:S(2)}) collective-permute-start(bf16[768,512]{1,0:T(8,128)(2,1)S(1)} %collective-permute-done), channel_id=1, source_target_pairs={{0,6},{1,7},{2,0},{3,1},{4,2},{5,3},{6,4},{7,5},{8,14},{9,15},{10,... | collective-permute-start | bytes 2359304 | tf_op jit(solution)/shard_map/ppermute | solution.py:210
  41.5 34.9 %collective-permute-start.1 = (bf16[768,512]{1,0:T(8,128)(2,1)S(1)}, bf16[768,512]{1,0:T(8,128)(2,1)}, u32[]{:S(2)}, u32[]{:S(2)}) collective-permute-start(bf16[768,512]{1,0:T(8,128)(2,1)S(1)} %constant_dynamic-update-slice_fusion), channel_id=1, source_target_pairs={{0,6},{1,7},{2,0},{3,1},{4,2},{5,3},{6,4},{7,5},{8,14},{9,15},{10,... | collective-permute-start | bytes 2359304 | tf_op jit(solution)/shard_map/ppermute | solution.py:210
  44.1 46.7 %collective-permute-start.6 = (bf16[768,512]{1,0:T(8,128)(2,1)S(1)}, bf16[768,512]{1,0:T(8,128)(2,1)S(1)}, u32[]{:S(2)}, u32[]{:S(2)}) collective-permute-start(bf16[768,512]{1,0:T(8,128)(2,1)S(1)} %collective-permute-done), channel_id=1, source_target_pairs={{0,2},{1,3},{2,4},{3,5},{4,6},{5,7},{6,0},{7,1},{8,10},{9,11},{10,... | collective-permute-start | bytes 2359304 | tf_op jit(solution)/shard_map/ppermute | solution.py:210
  45.3 34.1 %collective-permute-start.4 = (bf16[768,512]{1,0:T(8,128)(2,1)S(1)}, bf16[768,512]{1,0:T(8,128)(2,1)S(1)}, u32[]{:S(2)}, u32[]{:S(2)}) collective-permute-start(bf16[768,512]{1,0:T(8,128)(2,1)S(1)} %collective-permute-done.3), channel_id=1, source_target_pairs={{0,2},{1,3},{2,4},{3,5},{4,6},{5,7},{6,0},{7,1},{8,10},{9,11},{10,... | collective-permute-start | bytes 2359304 | tf_op jit(solution)/shard_map/ppermute | solution.py:210
  59.5 29.3 %collective-permute-start.5 = (bf16[768,512]{1,0:T(8,128)(2,1)S(1)}, bf16[768,512]{1,0:T(8,128)(2,1)S(1)}, u32[]{:S(2)}, u32[]{:S(2)}) collective-permute-start(bf16[768,512]{1,0:T(8,128)(2,1)S(1)} %collective-permute-done.2), channel_id=1, source_target_pairs={{0,6},{1,7},{2,0},{3,1},{4,2},{5,3},{6,4},{7,5},{8,14},{9,15},{10,... | collective-permute-start | bytes 2359304 | tf_op jit(solution)/shard_map/ppermute | solution.py:210
  113.6 21.0 %copy-start.13 = (s32[384]{0:T(512)S(1)}, s32[384]{0:T(512)}, u32[]{:S(2)}) copy-start(s32[384]{0:T(512)} %reshape.100.cols) | copy-start | bytes 4612
  154.5 32.1 %collective-permute-start.8 = (bf16[4,3072,128]{2,1,0:T(8,128)(2,1)}, bf16[4,3072,128]{2,1,0:T(8,128)(2,1)}, u32[]{:S(2)}, u32[]{:S(2)}) collective-permute-start(bf16[4,3072,128]{2,1,0:T(8,128)(2,1)} %weight_grads.7), channel_id=1, source_target_pairs={{0,8},{8,0},{16,24},{24,16},{32,40},{40,32},{48,56},{56,48},{64,72... | collective-permute-start | bytes 9437192 | tf_op jit(solution)/shard_map/ppermute | solution.py:210
  154.6 8.1 %collective-permute-start.7 = (bf16[2,3072,128]{2,1,0:T(8,128)(2,1)}, bf16[2,3072,128]{2,1,0:T(8,128)(2,1)}, u32[]{:S(2)}, u32[]{:S(2)}) collective-permute-start(bf16[2,3072,128]{2,1,0:T(8,128)(2,1)} %weight_grads.6), channel_id=1, source_target_pairs={{0,8},{8,0},{16,24},{24,16},{32,40},{40,32},{48,56},{56,48},{64,72... | collective-permute-start | bytes 4718600 | tf_op jit(solution)/shard_map/ppermute | solution.py:210
  155.0 50.5 %all-to-all-start = ((bf16[8,384,512]{2,1,0:T(8,128)(2,1)}), bf16[8,384,512]{2,1,0:T(8,128)(2,1)}, u32[]{:S(2)}, u32[]{:S(2)}) async-start(bf16[8,384,512]{2,1,0:T(8,128)(2,1)} %copy-done.7), calls=%async_computation | async-start | bytes 6291456 | tf_op jit(solution)/shard_map/all_to_all | solution.py:277
  168.3 44.3 %collective-permute-start.10 = (bf16[3072,128]{1,0:T(8,128)(2,1)}, bf16[3072,128]{1,0:T(8,128)(2,1)}, u32[]{:S(2)}, u32[]{:S(2)}) collective-permute-start(bf16[3072,128]{1,0:T(8,128)(2,1)} %get-tuple-element.29), channel_id=1, source_target_pairs={{0,32},{8,40},{16,48},{24,56},{32,64},{40,72},{48,80},{56,88},{64,... | collective-permute-start | bytes 2359304 | tf_op jit(solution)/shard_map/ppermute | solution.py:210
  168.5 41.4 %collective-permute-start.14 = (bf16[3072,128]{1,0:T(8,128)(2,1)}, bf16[3072,128]{1,0:T(8,128)(2,1)}, u32[]{:S(2)}, u32[]{:S(2)}) collective-permute-start(bf16[3072,128]{1,0:T(8,128)(2,1)} %get-tuple-element.40), channel_id=1, source_target_pairs={{0,96},{8,104},{16,112},{24,120},{32,0},{40,8},{48,16},{56,24},{64... | collective-permute-start | bytes 2359304 | tf_op jit(solution)/shard_map/ppermute | solution.py:210
  186.6 31.7 %collective-permute-start.9 = (bf16[2,3072,128]{2,1,0:T(8,128)(2,1)}, bf16[2,3072,128]{2,1,0:T(8,128)(2,1)}, u32[]{:S(2)}, u32[]{:S(2)}) collective-permute-start(bf16[2,3072,128]{2,1,0:T(8,128)(2,1)} %weight_grads.9), channel_id=1, source_target_pairs={{0,8},{8,0},{16,24},{24,16},{32,40},{40,32},{48,56},{56,48},{64,72... | collective-permute-start | bytes 4718600 | tf_op jit(solution)/shard_map/ppermute | solution.py:210
  194.8 37.5 %collective-permute-start.13 = (bf16[3072,128]{1,0:T(8,128)(2,1)}, bf16[3072,128]{1,0:T(8,128)(2,1)}, u32[]{:S(2)}, u32[]{:S(2)}) collective-permute-start(bf16[3072,128]{1,0:T(8,128)(2,1)} %get-tuple-element.33), channel_id=1, source_target_pairs={{0,32},{8,40},{16,48},{24,56},{32,64},{40,72},{48,80},{56,88},{64,... | collective-permute-start | bytes 2359304 | tf_op jit(solution)/shard_map/ppermute | solution.py:210
  205.5 49.7 %all-to-all-start.1 = ((bf16[8,384,512]{2,1,0:T(8,128)(2,1)}), bf16[8,384,512]{2,1,0:T(8,128)(2,1)}, u32[]{:S(2)}, u32[]{:S(2)}) async-start(bf16[8,384,512]{2,1,0:T(8,128)(2,1)} %copy-done.8), calls=%async_computation.1 | async-start | bytes 6291456 | tf_op jit(solution)/shard_map/all_to_all | solution.py:277
  210.0 8.3 %copy-start.6 = (bf16[16,384,128]{2,1,0:T(8,128)(2,1)S(1)}, bf16[16,384,128]{2,1,0:T(8,128)(2,1)}, u32[]{:S(2)}) copy-start(bf16[16,384,128]{2,1,0:T(8,128)(2,1)} %get-tuple-element.26.refs_2_.refs_1_) | copy-start | bytes 4718596
  211.7 20.5 %collective-permute-start.15 = (bf16[3072,128]{1,0:T(8,128)(2,1)S(1)}, bf16[3072,128]{1,0:T(8,128)(2,1)S(1)}, u32[]{:S(2)}, u32[]{:S(2)}) collective-permute-start(bf16[3072,128]{1,0:T(8,128)(2,1)S(1)} %add_convert_fusion.2), channel_id=1, source_target_pairs={{0,96},{8,104},{16,112},{24,120},{32,0},{40,8},{48,16},{56,24},{64... | collective-permute-start | bytes 2359304 | tf_op jit(solution)/shard_map/ppermute | solution.py:210
  215.0 43.4 %collective-permute-start.11 = (bf16[3072,128]{1,0:T(8,128)(2,1)}, bf16[3072,128]{1,0:T(8,128)(2,1)}, u32[]{:S(2)}, u32[]{:S(2)}) collective-permute-start(bf16[3072,128]{1,0:T(8,128)(2,1)} %add_convert_fusion.3), channel_id=1, source_target_pairs={{0,32},{8,40},{16,48},{24,56},{32,64},{40,72},{48,80},{56,88},{64,... | collective-permute-start | bytes 2359304 | tf_op jit(solution)/shard_map/ppermute | solution.py:210
  216.2 42.2 %collective-permute-start.12 = (bf16[3072,128]{1,0:T(8,128)(2,1)}, bf16[3072,128]{1,0:T(8,128)(2,1)}, u32[]{:S(2)}, u32[]{:S(2)}) collective-permute-start(bf16[3072,128]{1,0:T(8,128)(2,1)} %get-tuple-element.37), channel_id=1, source_target_pairs={{0,96},{8,104},{16,112},{24,120},{32,0},{40,8},{48,16},{56,24},{64... | collective-permute-start | bytes 2359304 | tf_op jit(solution)/shard_map/ppermute | solution.py:210
  221.6 12.0 %copy-start.11 = (bf16[3072,128]{1,0:T(8,128)(2,1)}, bf16[3072,128]{1,0:T(8,128)(2,1)S(1)}, u32[]{:S(2)}) copy-start(bf16[3072,128]{1,0:T(8,128)(2,1)S(1)} %get-tuple-element.35) | copy-start | bytes 2359300
  233.7 28.5 %collective-permute-start.16 = (bf16[3072,128]{1,0:T(8,128)(2,1)S(1)}, bf16[3072,128]{1,0:T(8,128)(2,1)S(1)}, u32[]{:S(2)}, u32[]{:S(2)}) collective-permute-start(bf16[3072,128]{1,0:T(8,128)(2,1)S(1)} %add_convert_fusion.1), channel_id=1, source_target_pairs={{0,16},{8,24},{16,0},{24,8},{32,48},{40,56},{48,32},{56,40},{64,80... | collective-permute-start | bytes 2359304 | tf_op jit(solution)/shard_map/ppermute | solution.py:210
  235.3 26.9 %copy-start.12 = (bf16[3072,128]{1,0:T(8,128)(2,1)S(1)}, bf16[3072,128]{1,0:T(8,128)(2,1)}, u32[]{:S(2)}) copy-start(bf16[3072,128]{1,0:T(8,128)(2,1)} %copy-done.11) | copy-start | bytes 2359300
  (11 other events, 50.7 us)
Sparse Core Ops, SparseCore 0:
  11.8 100.2 all-gather.1

commit v4 on v3

--- a/solution.py
+++ b/solution.py
@@ -95,7 +95,7 @@
                 pltpu.make_async_copy(held.at[n], outs[n], sems.at[n]).wait()
 
 
-def product_kernel(tensors, cols, w_ref, *refs):
+def product_kernel(tensors, flip, cols, w_ref, *refs):
     step = pl.program_id(0)
     sources, o_ref = refs[:-1], refs[-1]
     for i in range(4):
@@ -185,7 +185,7 @@
     )(at_x, owners, cols, feats, *sources, *extra)
 
 
-def block_product(tensors, cols, weights, sources):
+def block_product(tensors, flip, cols, weights, sources):
     tok_rows = sources[0].shape[1]
     steps = weights.shape[0] // 2
     rows = len(tensors) * 2 * NZ * BLK
@@ -194,16 +194,18 @@
         functools.partial(product_kernel, tensors),
         out_shape=jax.ShapeDtypeStruct((steps, tok_rows, 4 * BLK), jnp.bfloat16),
         grid_spec=pltpu.PrefetchScalarGridSpec(
-            num_scalar_prefetch=1,
+            num_scalar_prefetch=2,
             grid=(steps,),
-            in_specs=[pl.BlockSpec((2, rows, BLK), lambda j, cols: (j, at, 0))]
+            in_specs=[pl.BlockSpec((2, rows, BLK), lambda j, flip, cols: (j, at, 0))]
             + [whole(sources[0].shape)] * len(sources),
-            out_specs=pl.BlockSpec((1, tok_rows, 4 * BLK), lambda j, cols: (j, 0, 0)),
+            out_specs=pl.BlockSpec(
+                (1, tok_rows, 4 * BLK), lambda j, flip, cols: (j // 2 * 2 + (j + flip[0]) % 2, 0, 0)
+            ),
         ),
         compiler_params=params(40),
         cost_estimate=cost(len(tensors) * 3 * 10**9, len(tensors) * 7 * 10**6),
         name="block_product",
-    )(cols, weights, *sources)
+    )(flip, cols, weights, *sources)
 
 
 def permute(value, axis, target):
@@ -246,9 +248,8 @@
 def body(tokens, cotangent, gate_blocks, up_blocks, down_blocks, gate_cols, up_cols, down_cols):
     n_row = lax.axis_size("row")
     tok_rows = tokens.shape[0]
-    tables = jnp.concatenate(
-        [jnp.bitwise_and(t, FB_DEV - 1).reshape(1, -1) for t in (gate_cols, up_cols, down_cols)], 1
-    ).astype(jnp.bfloat16)
+    tables = jnp.concatenate([t.reshape(1, -1) for t in (gate_cols, up_cols, down_cols)], 1)
+    tables = jnp.bitwise_and(tables, FB_DEV - 1).astype(jnp.bfloat16)
     tables = jnp.pad(tables, ((0, 15), (0, BLK - tables.shape[1])))
     packed = jnp.concatenate(
         [b.reshape(-1, BLK) for b in (gate_blocks, up_blocks, down_blocks)] + [tables], 0
@@ -273,14 +274,21 @@
     def other_core(value):
         return permute(value, "row", lambda r: r ^ 1)
 
-    def reduce_features(partial_value):
-        parts = lax.all_to_all(partial_value, "col", 0, 0, tiled=True)
-        return jnp.sum(parts.astype(jnp.float32), axis=0).astype(jnp.bfloat16)
-
     def total(*values):
         return sum(v.astype(jnp.float32) for v in values).astype(jnp.bfloat16)
 
-    out_parts = block_product((2,), cols, weights, (hidden,))
+    rings = [[2 * x + z for x in range(RING)] for z in range(2)]
+
+    def reduce_features(parts):
+        ring_sum = lax.psum_scatter(
+            parts.reshape(-1, parts.shape[2]), "col", scatter_dimension=0, tiled=True,
+            axis_index_groups=rings,
+        )
+        got = permute(ring_sum[tok_rows:], "col", lambda c: c ^ 1)
+        return total(ring_sum[:tok_rows], got)
+
+    flip = (lax.axis_index("col") % 2).astype(jnp.int32).reshape(1)
+    out_parts = block_product((2,), flip, cols, weights, (hidden,))
     output = reduce_features(out_parts)
     their_far = theirs(FAR, after(out_parts))
     got_far = other_core(their_far)
@@ -288,7 +296,7 @@
     got_near = other_core(their_near)
     far0, far1 = mine(FAR, after(their_near), got_far)
     far_p, far_m = over_y(far0, 1), over_y(far1, -1)
-    in_parts = block_product((0, 1), after(far0), weights, (gate_delta, up_delta))
+    in_parts = block_product((0, 1), flip, after(far0), weights, (gate_delta, up_delta))
     tokens_grad = reduce_features(in_parts)
     their_own = theirs(OWN, after(in_parts))
     got_own = other_core(their_own)

time: 273 us -> 264 us (0.967)
  local copies, waits for them, and re-layouts: 16.8 us -> 29.3 us
  other arithmetic: 19.3 us -> 8.74 us
  starting transfers between devices: 30.5 us -> 24.5 us
    all_to_all x2 -> x0, waiting for transfers between devices: 27.4 us -> none  [reduce_features(): parts = lax.all_to_all(partial_value, 'col', 0, 0, tiled=True)]
    ppermute x17 -> x19, waiting for transfers between devices: 74.8 us -> 98.3 us  [permute(): lax.ppermute(value, axis, [(i, target(i)) for i in range(lax.axis_size(ax...]
    all_to_all x2 -> x0, starting transfers between devices: 8.93 us -> none  [reduce_features(): parts = lax.all_to_all(partial_value, 'col', 0, 0, tiled=True)]
    unnamed x38 -> x44, local copies, waits for them, and re-layouts: 13.4 us -> 21.6 us
    reduce_sum x2 -> x0, other arithmetic: 6.44 us -> none  [reduce_features(): return jnp.sum(parts.astype(jnp.float32), axis=0).astype(jnp.bfloat16)]
    pallas_call x6, Pallas kernels: 28.7 us -> 25.8 us  [weight_grads(): pl.pallas_call(functools.partial(weight_grads_kernel, scale, 0 if got is...]
    ppermute x17 -> x19, starting transfers between devices: 21.5 us -> 24.4 us  [permute(): lax.ppermute(value, axis, [(i, target(i)) for i in range(lax.axis_size(ax...]
    convert_element_type x4 -> x6, other arithmetic: 7.36 us -> 5.33 us  [total(): return sum((v.astype(jnp.float32) for v in values)).astype(jnp.bfloat16)]
  transfers between devices with their start and end apart: 20 -> 22, of which waited for: 10 -> 13; matrix products, arithmetic and copies ran while one was open for 8% -> 7% of each run, Pallas kernels for 11% -> 14%
where the time goes in v4:
time: 264 us; the launch traced here: 263 us
  waiting for transfers between devices  120 us (45%)
  Pallas kernels  67 us (25%)
  local copies, waits for them, and re-layouts  29.3 us (11%)
  starting transfers between devices  24.5 us (9%)
  between operations  14.2 us (5%)
  other arithmetic  8.74 us (3%)
    ppermute x19, waiting for transfers between devices, permute(): lax.ppermute(value, axis, [(i, target(i)) for i in range(lax.axis_size(ax...  98.3 us
    pallas_call x6, Pallas kernels, weight_grads(): pl.pallas_call(functools.partial(weight_grads_kernel, scale, 0 if got is...  25.8 us
    ppermute x19, starting transfers between devices, permute(): lax.ppermute(value, axis, [(i, target(i)) for i in range(lax.axis_size(ax...  24.4 us
    pallas_call x1, Pallas kernels, local_sums(): pl.pallas_call(sums_kernel, out_shape=(out, out, out), grid_spec=pltpu.Pr...  22.9 us
    unnamed x44, local copies, waits for them, and re-layouts  21.6 us
    all_gather x1, waiting for transfers between devices, body(): lax.all_gather(packed, 'row', axis=0, tiled=True).reshape(n_row, -1, BLK)  21.2 us
    pallas_call x2, Pallas kernels, block_product(): pl.pallas_call(functools.partial(product_kernel, tensors), out_shape=jax....  18.4 us
    convert_element_type x6, other arithmetic, total(): return sum((v.astype(jnp.float32) for v in values)).astype(jnp.bfloat16)  5.33 us
  transfers between devices with their start and end apart: 22, of which 13 were waited for; matrix products, arithmetic and copies ran while one was open for 7% of the time, Pallas kernels for 14%

profile of v4, /device:TPU:0, one launch (start us, length us, event | category | flops | bytes accessed | tf_op | source)
XLA Modules:
  0.0 263.4 jit_solution(3637783347248509164)
XLA Ops:
  15.4 21.6 %collective-permute-done = bf16[768,512]{1,0:T(8,128)(2,1)S(1)} collective-permute-done((bf16[768,512]{1,0:T(8,128)(2,1)S(1)}, bf16[768,512]{1,0:T(8,128)(2,1)S(1)}, u32[]{:S(2)}, u32[]{:S(2)}) %collective-permute-start) | collective-permute-done | bytes 786464 | tf_op jit(solution)/shard_map/ppermute | solution.py:212
  37.1 2.6 collective-permute-start.2
  44.3 13.4 %collective-permute-done.2 = bf16[768,512]{1,0:T(8,128)(2,1)S(1)} collective-permute-done((bf16[768,512]{1,0:T(8,128)(2,1)S(1)}, bf16[768,512]{1,0:T(8,128)(2,1)S(1)}, u32[]{:S(2)}, u32[]{:S(2)}) %collective-permute-start.2) | collective-permute-done | bytes 786464 | tf_op jit(solution)/shard_map/ppermute | solution.py:212
  57.7 3.7 %collective-permute-start.5 = (bf16[768,512]{1,0:T(8,128)(2,1)S(1)}, bf16[768,512]{1,0:T(8,128)(2,1)S(1)}, u32[]{:S(2)}, u32[]{:S(2)}) collective-permute-start(bf16[768,512]{1,0:T(8,128)(2,1)S(1)} %collective-permute-done.2), channel_id=1, source_target_pairs={{0,6},{1,7},{2,0},{3,1},{4,2},{5,3},{6,4},{7,5},{8,14},{9,15},{10,... | collective-permute-start | bytes 2359304 | tf_op jit(solution)/shard_map/ppermute | solution.py:212
  61.4 13.2 %collective-permute-done.1 = bf16[768,512]{1,0:T(8,128)(2,1)} collective-permute-done((bf16[768,512]{1,0:T(8,128)(2,1)S(1)}, bf16[768,512]{1,0:T(8,128)(2,1)}, u32[]{:S(2)}, u32[]{:S(2)}) %collective-permute-start.1) | collective-permute-done | bytes 786464 | tf_op jit(solution)/shard_map/ppermute | solution.py:212
  78.5 8.5 %collective-permute-done.5 = bf16[768,512]{1,0:T(8,128)(2,1)S(1)} collective-permute-done((bf16[768,512]{1,0:T(8,128)(2,1)S(1)}, bf16[768,512]{1,0:T(8,128)(2,1)S(1)}, u32[]{:S(2)}, u32[]{:S(2)}) %collective-permute-start.5) | collective-permute-done | bytes 786464 | tf_op jit(solution)/shard_map/ppermute | solution.py:212
  89.9 21.2 %all-gather.2.cloned.1.call-done = bf16[49408,128]{1,0:T(8,128)(2,1)} async-done(((bf16[3088,128]{1,0:T(8,128)(2,1)}), bf16[49408,128]{1,0:T(8,128)(2,1)}) %all-gather.2.cloned.1.call-update) | async-done | bytes 12648464 | tf_op jit(solution)/shard_map/all_gather | solution.py:257
  112.6 22.9 %local_sums.1 = (bf16[16,384,128]{2,1,0:T(8,128)(2,1)}, bf16[16,384,128]{2,1,0:T(8,128)(2,1)}, bf16[16,384,128]{2,1,0:T(8,128)(2,1)}) custom-call(s32[8]{0:T(128)} %stack.172.order, s32[384]{0:T(512)} %reshape.113.cols, bf16[8,768,512]{2,1,0:T(8,128)(2,1)} %bitcast_dynamic-update-slice_fusion.x_ref, bf16[16,3088,128]{2,1,0:T(8,128)(2,1)} %bitcast.61), custom_call_target="tpu_custom_call" | custom-call | flops 10000000000 | bytes 30000000 | tf_op jit(solution)/shard_map/local_sums/pallas_call | solution.py:134
  136.9 7.8 %block_product.2 = bf16[8,384,512]{2,1,0:T(8,128)(2,1)S(1)} custom-call(s32[1]{0:T(128)} %bitcast.flip, s32[384]{0:T(512)S(1)} %copy-done.11, bf16[16,3088,128]{2,1,0:T(8,128)(2,1)} %bitcast.62, bf16[16,384,128]{2,1,0:T(8,128)(2,1)S(1)} %copy-done), custom_call_target="tpu_custom_call" | custom-call | flops 3000000000 | bytes 7000000 | tf_op jit(solution)/shard_map/block_product/pallas_call | solution.py:193
  149.7 3.9 %weight_grads.6 = bf16[2,3072,128]{2,1,0:T(8,128)(2,1)} custom-call(s32[2]{0:T(128)S(1)} %get-tuple-element.44.at_x, s32[2]{0:T(128)S(1)} %get-tuple-element.45.owners, s32[384]{0:T(512)S(1)} %copy-done.11, bf16[8,768,512]{2,1,0:T(8,128)(2,1)} %bitcast_dynamic-update-slice_fusion.x_ref, bf16[16,384,128]{2,1,0:T(8,128)(2,1)S(1)} %copy-done.1, ...), custom_call_target="tpu_custom_call" | custom-call | flops 2000000000 | bytes 6000000 | tf_op jit(solution)/shard_map/weight_grads/pallas_call | solution.py:172
  155.4 6.0 %weight_grads.7 = bf16[4,3072,128]{2,1,0:T(8,128)(2,1)} custom-call(s32[4]{0:T(128)S(1)} %get-tuple-element.46.at_x, s32[4]{0:T(128)S(1)} %get-tuple-element.47.owners, s32[384]{0:T(512)S(1)} %copy-done.11, bf16[8,768,512]{2,1,0:T(8,128)(2,1)} %bitcast_dynamic-update-slice_fusion.x_ref, bf16[16,384,128]{2,1,0:T(8,128)(2,1)S(1)} %copy-done.1, ...), custom_call_target="tpu_custom_call" | custom-call | flops 4000000000 | bytes 12000000 | tf_op jit(solution)/shard_map/weight_grads/pallas_call | solution.py:172
  163.1 3.4 %weight_grads.8 = (bf16[3072,128]{1,0:T(8,128)(2,1)S(1)}, bf16[3072,128]{1,0:T(8,128)(2,1)S(1)}) custom-call(s32[2]{0:T(128)S(1)} %get-tuple-element.44.at_x, s32[2]{0:T(128)S(1)} %pad_add_fusion.1.owners, s32[384]{0:T(512)S(1)} %copy-done.11, bf16[8,768,512]{2,1,0:T(8,128)(2,1)} %bitcast_dynamic-update-slice_fusion.x_ref, ...), custom_call_target="tpu_custom_call" | custom-call | flops 2000000000 | bytes 6000000 | tf_op jit(solution)/shard_map/weight_grads/pallas_call | solution.py:172
  168.3 10.6 %block_product.3 = bf16[8,384,512]{2,1,0:T(8,128)(2,1)S(1)} custom-call(s32[1]{0:T(128)} %bitcast.flip, s32[384]{0:T(512)S(1)} %copy-done.11, bf16[16,3088,128]{2,1,0:T(8,128)(2,1)} %bitcast.63, bf16[16,384,128]{2,1,0:T(8,128)(2,1)S(1)} %copy-done.2, bf16[16,384,128]{2,1,0:T(8,128)(2,1)S(1)} %copy-done.6), custom_call_target="tpu_custom_call" | custom-call | flops 6000000000 | bytes 14000000 | tf_op jit(solution)/shard_map/block_product/pallas_call | solution.py:193
  184.3 3.0 %weight_grads.9 = bf16[2,3072,128]{2,1,0:T(8,128)(2,1)S(1)} custom-call(s32[2]{0:T(128)S(1)} %get-tuple-element.48.at_x, s32[2]{0:T(128)S(1)} %get-tuple-element.49.owners, s32[384]{0:T(512)S(1)} %copy-done.11, bf16[8,768,512]{2,1,0:T(8,128)(2,1)} %bitcast_dynamic-update-slice_fusion.x_ref, bf16[16,384,128]{2,1,0:T(8,128)(2,1)S(1)} %copy-done.1, ...), custom_call_target="tpu_custom_call" | custom-call | flops 2000000000 | bytes 6000000 | tf_op jit(solution)/shard_map/weight_grads/pallas_call | solution.py:172
  187.6 6.4 %weight_grads.10 = (bf16[3072,128]{1,0:T(8,128)(2,1)S(1)}, bf16[3072,128]{1,0:T(8,128)(2,1)S(1)}, bf16[3072,128]{1,0:T(8,128)(2,1)S(1)}, bf16[3072,128]{1,0:T(8,128)(2,1)}) custom-call(s32[4]{0:T(128)S(1)} %get-tuple-element.46.at_x, s32[4]{0:T(128)S(1)} %pad_add_fusion.7.owners, s32[384]{0:T(512)S(1)} %copy-done.11, ...), custom_call_target="tpu_custom_call" | custom-call | flops 4000000000 | bytes 12000000 | tf_op jit(solution)/shard_map/weight_grads/pallas_call | solution.py:172
  194.6 6.0 %collective-permute-done.16 = bf16[3072,128]{1,0:T(8,128)(2,1)S(1)} collective-permute-done((bf16[3072,128]{1,0:T(8,128)(2,1)}, bf16[3072,128]{1,0:T(8,128)(2,1)S(1)}, u32[]{:S(2)}, u32[]{:S(2)}) %collective-permute-start.16) | collective-permute-done | bytes 786464 | tf_op jit(solution)/shard_map/ppermute | solution.py:212
  200.9 2.5 collective-permute-start.17
  205.0 3.2 %collective-permute-start.14 = (bf16[3072,128]{1,0:T(8,128)(2,1)}, bf16[3072,128]{1,0:T(8,128)(2,1)}, u32[]{:S(2)}, u32[]{:S(2)}) collective-permute-start(bf16[3072,128]{1,0:T(8,128)(2,1)} %get-tuple-element.37), channel_id=1, source_target_pairs={{0,96},{8,104},{16,112},{24,120},{32,0},{40,8},{48,16},{56,24},{64... | collective-permute-start | bytes 2359304 | tf_op jit(solution)/shard_map/ppermute | solution.py:212
  208.3 3.1 %weight_grads.11 = (bf16[3072,128]{1,0:T(8,128)(2,1)S(1)}, bf16[3072,128]{1,0:T(8,128)(2,1)S(1)}) custom-call(s32[2]{0:T(128)S(1)} %get-tuple-element.48.at_x, s32[2]{0:T(128)S(1)} %pad_add_fusion.6.owners, s32[384]{0:T(512)S(1)} %copy-done.11, bf16[8,768,512]{2,1,0:T(8,128)(2,1)} %bitcast_dynamic-update-slice_fusion.x_ref, ...), custom_call_target="tpu_custom_call" | custom-call | flops 2000000000 | bytes 6000000 | tf_op jit(solution)/shard_map/weight_grads/pallas_call | solution.py:172
  211.4 10.1 %collective-permute-done.17 = bf16[3072,128]{1,0:T(8,128)(2,1)S(1)} collective-permute-done((bf16[3072,128]{1,0:T(8,128)(2,1)S(1)}, bf16[3072,128]{1,0:T(8,128)(2,1)S(1)}, u32[]{:S(2)}, u32[]{:S(2)}) %collective-permute-start.17) | collective-permute-done | bytes 786464 | tf_op jit(solution)/shard_map/ppermute | solution.py:212
  225.3 11.5 %collective-permute-done.13 = bf16[3072,128]{1,0:T(8,128)(2,1)} collective-permute-done((bf16[3072,128]{1,0:T(8,128)(2,1)}, bf16[3072,128]{1,0:T(8,128)(2,1)}, u32[]{:S(2)}, u32[]{:S(2)}) %collective-permute-start.13) | collective-permute-done | bytes 786464 | tf_op jit(solution)/shard_map/ppermute | solution.py:212
  237.0 6.9 %collective-permute-done.18 = bf16[3072,128]{1,0:T(8,128)(2,1)S(1)} collective-permute-done((bf16[3072,128]{1,0:T(8,128)(2,1)S(1)}, bf16[3072,128]{1,0:T(8,128)(2,1)S(1)}, u32[]{:S(2)}, u32[]{:S(2)}) %collective-permute-start.18) | collective-permute-done | bytes 786464 | tf_op jit(solution)/shard_map/ppermute | solution.py:212
  248.7 2.3 collective-permute-done.7
  251.9 4.1 %collective-permute-done.9 = bf16[384,512]{1,0:T(8,128)(2,1)S(1)} collective-permute-done((bf16[384,512]{1,0:T(8,128)(2,1)S(1)}, bf16[384,512]{1,0:T(8,128)(2,1)S(1)}, u32[]{:S(2)}, u32[]{:S(2)}) %collective-permute-start.9) | collective-permute-done | bytes 393248 | tf_op jit(solution)/shard_map/ppermute | solution.py:212
  (101 shorter events, 51.3 us)
Async XLA Ops:
  7.2 104.0 %all-gather.2.cloned.1.call-start = ((), (), s32[]{:S(2)}) async-start(), calls=%async_computation.2 | async-start | bytes 13438976 | tf_op jit(solution)/shard_map/all_gather | solution.py:257
  11.7 210.5 %reduce-scatter.3.cloned.1.call-start = ((), (), s32[]{:S(2)}) async-start(), calls=%async_computation.3 | async-start | bytes 3932160 | tf_op jit(solution)/shard_map/reduce_scatter | solution.py:283
  11.9 25.2 %collective-permute-start = (bf16[768,512]{1,0:T(8,128)(2,1)S(1)}, bf16[768,512]{1,0:T(8,128)(2,1)S(1)}, u32[]{:S(2)}, u32[]{:S(2)}) collective-permute-start(bf16[768,512]{1,0:T(8,128)(2,1)S(1)} %constant_dynamic-update-slice_fusion), channel_id=1, source_target_pairs={{0,1},{1,0},{2,3},{3,2},{4,5},{5,4},{6,7},{7,6},{8,9},{9,8},{10,11... | collective-permute-start | bytes 2359304 | tf_op jit(solution)/shard_map/ppermute | solution.py:212
  14.0 29.4 %collective-permute-start.3 = (bf16[768,512]{1,0:T(8,128)(2,1)S(1)}, bf16[768,512]{1,0:T(8,128)(2,1)S(1)}, u32[]{:S(2)}, u32[]{:S(2)}) collective-permute-start(bf16[768,512]{1,0:T(8,128)(2,1)S(1)} %constant_dynamic-update-slice_fusion), channel_id=1, source_target_pairs={{0,2},{1,3},{2,4},{3,5},{4,6},{5,7},{6,0},{7,1},{8,10},{9,11},{10,... | collective-permute-start | bytes 2359304 | tf_op jit(solution)/shard_map/ppermute | solution.py:212
  37.1 20.6 %collective-permute-start.2 = (bf16[768,512]{1,0:T(8,128)(2,1)S(1)}, bf16[768,512]{1,0:T(8,128)(2,1)S(1)}, u32[]{:S(2)}, u32[]{:S(2)}) collective-permute-start(bf16[768,512]{1,0:T(8,128)(2,1)S(1)} %collective-permute-done), channel_id=1, source_target_pairs={{0,6},{1,7},{2,0},{3,1},{4,2},{5,3},{6,4},{7,5},{8,14},{9,15},{10,... | collective-permute-start | bytes 2359304 | tf_op jit(solution)/shard_map/ppermute | solution.py:212
  39.7 34.9 %collective-permute-start.1 = (bf16[768,512]{1,0:T(8,128)(2,1)S(1)}, bf16[768,512]{1,0:T(8,128)(2,1)}, u32[]{:S(2)}, u32[]{:S(2)}) collective-permute-start(bf16[768,512]{1,0:T(8,128)(2,1)S(1)} %constant_dynamic-update-slice_fusion), channel_id=1, source_target_pairs={{0,6},{1,7},{2,0},{3,1},{4,2},{5,3},{6,4},{7,5},{8,14},{9,15},{10,... | collective-permute-start | bytes 2359304 | tf_op jit(solution)/shard_map/ppermute | solution.py:212
  42.1 46.9 %collective-permute-start.6 = (bf16[768,512]{1,0:T(8,128)(2,1)S(1)}, bf16[768,512]{1,0:T(8,128)(2,1)S(1)}, u32[]{:S(2)}, u32[]{:S(2)}) collective-permute-start(bf16[768,512]{1,0:T(8,128)(2,1)S(1)} %collective-permute-done), channel_id=1, source_target_pairs={{0,2},{1,3},{2,4},{3,5},{4,6},{5,7},{6,0},{7,1},{8,10},{9,11},{10,... | collective-permute-start | bytes 2359304 | tf_op jit(solution)/shard_map/ppermute | solution.py:212
  43.3 34.3 %collective-permute-start.4 = (bf16[768,512]{1,0:T(8,128)(2,1)S(1)}, bf16[768,512]{1,0:T(8,128)(2,1)S(1)}, u32[]{:S(2)}, u32[]{:S(2)}) collective-permute-start(bf16[768,512]{1,0:T(8,128)(2,1)S(1)} %collective-permute-done.3), channel_id=1, source_target_pairs={{0,2},{1,3},{2,4},{3,5},{4,6},{5,7},{6,0},{7,1},{8,10},{9,11},{10,... | collective-permute-start | bytes 2359304 | tf_op jit(solution)/shard_map/ppermute | solution.py:212
  57.7 29.3 %collective-permute-start.5 = (bf16[768,512]{1,0:T(8,128)(2,1)S(1)}, bf16[768,512]{1,0:T(8,128)(2,1)S(1)}, u32[]{:S(2)}, u32[]{:S(2)}) collective-permute-start(bf16[768,512]{1,0:T(8,128)(2,1)S(1)} %collective-permute-done.2), channel_id=1, source_target_pairs={{0,6},{1,7},{2,0},{3,1},{4,2},{5,3},{6,4},{7,5},{8,14},{9,15},{10,... | collective-permute-start | bytes 2359304 | tf_op jit(solution)/shard_map/ppermute | solution.py:212
  112.6 22.9 %copy-start.11 = (s32[384]{0:T(512)S(1)}, s32[384]{0:T(512)}, u32[]{:S(2)}) copy-start(s32[384]{0:T(512)} %reshape.113.cols) | copy-start | bytes 4612
  146.5 99.4 %reduce-scatter.5.cloned.1.call-start = ((), (), s32[]{:S(2)}) async-start(), calls=%async_computation.4 | async-start | bytes 3932160 | tf_op jit(solution)/shard_map/reduce_scatter | solution.py:283
  153.6 8.1 %collective-permute-start.8 = (bf16[2,3072,128]{2,1,0:T(8,128)(2,1)}, bf16[2,3072,128]{2,1,0:T(8,128)(2,1)}, u32[]{:S(2)}, u32[]{:S(2)}) collective-permute-start(bf16[2,3072,128]{2,1,0:T(8,128)(2,1)} %weight_grads.6), channel_id=1, source_target_pairs={{0,8},{8,0},{16,24},{24,16},{32,40},{40,32},{48,56},{56,48},{64,72... | collective-permute-start | bytes 4718600 | tf_op jit(solution)/shard_map/ppermute | solution.py:212
  161.4 26.2 %collective-permute-start.10 = (bf16[4,3072,128]{2,1,0:T(8,128)(2,1)}, bf16[4,3072,128]{2,1,0:T(8,128)(2,1)}, u32[]{:S(2)}, u32[]{:S(2)}) collective-permute-start(bf16[4,3072,128]{2,1,0:T(8,128)(2,1)} %weight_grads.7), channel_id=1, source_target_pairs={{0,8},{8,0},{16,24},{24,16},{32,40},{40,32},{48,56},{56,48},{64,72... | collective-permute-start | bytes 9437192 | tf_op jit(solution)/shard_map/ppermute | solution.py:212
  180.7 20.0 %collective-permute-start.16 = (bf16[3072,128]{1,0:T(8,128)(2,1)}, bf16[3072,128]{1,0:T(8,128)(2,1)S(1)}, u32[]{:S(2)}, u32[]{:S(2)}) collective-permute-start(bf16[3072,128]{1,0:T(8,128)(2,1)} %copy-done.13), channel_id=1, source_target_pairs={{0,96},{8,104},{16,112},{24,120},{32,0},{40,8},{48,16},{56,24},{64... | collective-permute-start | bytes 2359304 | tf_op jit(solution)/shard_map/ppermute | solution.py:212
  182.1 21.8 %collective-permute-start.12 = (bf16[3072,128]{1,0:T(8,128)(2,1)}, bf16[3072,128]{1,0:T(8,128)(2,1)S(1)}, u32[]{:S(2)}, u32[]{:S(2)}) collective-permute-start(bf16[3072,128]{1,0:T(8,128)(2,1)} %copy-done.12), channel_id=1, source_target_pairs={{0,32},{8,40},{16,48},{24,56},{32,64},{40,72},{48,80},{56,88},{64,... | collective-permute-start | bytes 2359304 | tf_op jit(solution)/shard_map/ppermute | solution.py:212
  187.3 20.9 %collective-permute-start.11 = (bf16[2,3072,128]{2,1,0:T(8,128)(2,1)S(1)}, bf16[2,3072,128]{2,1,0:T(8,128)(2,1)S(1)}, u32[]{:S(2)}, u32[]{:S(2)}) collective-permute-start(bf16[2,3072,128]{2,1,0:T(8,128)(2,1)S(1)} %weight_grads.9), channel_id=1, source_target_pairs={{0,8},{8,0},{16,24},{24,16},{32,40},{40,32},{48,56},{56,48},{64,72... | collective-permute-start | bytes 4718600 | tf_op jit(solution)/shard_map/ppermute | solution.py:212
  194.0 27.4 %collective-permute-start.15 = (bf16[3072,128]{1,0:T(8,128)(2,1)S(1)}, bf16[3072,128]{1,0:T(8,128)(2,1)S(1)}, u32[]{:S(2)}, u32[]{:S(2)}) collective-permute-start(bf16[3072,128]{1,0:T(8,128)(2,1)S(1)} %get-tuple-element.33), channel_id=1, source_target_pairs={{0,32},{8,40},{16,48},{24,56},{32,64},{40,72},{48,80},{56,88},{64,... | collective-permute-start | bytes 2359304 | tf_op jit(solution)/shard_map/ppermute | solution.py:212
  200.9 20.5 %collective-permute-start.17 = (bf16[3072,128]{1,0:T(8,128)(2,1)S(1)}, bf16[3072,128]{1,0:T(8,128)(2,1)S(1)}, u32[]{:S(2)}, u32[]{:S(2)}) collective-permute-start(bf16[3072,128]{1,0:T(8,128)(2,1)S(1)} %add_convert_fusion.2), channel_id=1, source_target_pairs={{0,96},{8,104},{16,112},{24,120},{32,0},{40,8},{48,16},{56,24},{64... | collective-permute-start | bytes 2359304 | tf_op jit(solution)/shard_map/ppermute | solution.py:212
  205.0 31.8 %collective-permute-start.13 = (bf16[3072,128]{1,0:T(8,128)(2,1)}, bf16[3072,128]{1,0:T(8,128)(2,1)}, u32[]{:S(2)}, u32[]{:S(2)}) collective-permute-start(bf16[3072,128]{1,0:T(8,128)(2,1)} %add_convert_fusion.3), channel_id=1, source_target_pairs={{0,32},{8,40},{16,48},{24,56},{32,64},{40,72},{48,80},{56,88},{64,... | collective-permute-start | bytes 2359304 | tf_op jit(solution)/shard_map/ppermute | solution.py:212
  205.0 31.9 %collective-permute-start.14 = (bf16[3072,128]{1,0:T(8,128)(2,1)}, bf16[3072,128]{1,0:T(8,128)(2,1)}, u32[]{:S(2)}, u32[]{:S(2)}) collective-permute-start(bf16[3072,128]{1,0:T(8,128)(2,1)} %get-tuple-element.37), channel_id=1, source_target_pairs={{0,96},{8,104},{16,112},{24,120},{32,0},{40,8},{48,16},{56,24},{64... | collective-permute-start | bytes 2359304 | tf_op jit(solution)/shard_map/ppermute | solution.py:212
  211.4 10.4 %copy-start.10 = (bf16[3072,128]{1,0:T(8,128)(2,1)}, bf16[3072,128]{1,0:T(8,128)(2,1)S(1)}, u32[]{:S(2)}) copy-start(bf16[3072,128]{1,0:T(8,128)(2,1)S(1)} %get-tuple-element.35) | copy-start | bytes 2359300
  221.8 22.1 %collective-permute-start.18 = (bf16[3072,128]{1,0:T(8,128)(2,1)S(1)}, bf16[3072,128]{1,0:T(8,128)(2,1)S(1)}, u32[]{:S(2)}, u32[]{:S(2)}) collective-permute-start(bf16[3072,128]{1,0:T(8,128)(2,1)S(1)} %add_convert_fusion.1), channel_id=1, source_target_pairs={{0,16},{8,24},{16,0},{24,8},{32,48},{40,56},{48,32},{56,40},{64,80... | collective-permute-start | bytes 2359304 | tf_op jit(solution)/shard_map/ppermute | solution.py:212
  223.3 27.8 %collective-permute-start.7 = (bf16[384,512]{1,0:T(8,128)(2,1)S(1)}, bf16[384,512]{1,0:T(8,128)(2,1)S(1)}, u32[]{:S(2)}, u32[]{:S(2)}) collective-permute-start(bf16[384,512]{1,0:T(8,128)(2,1)S(1)} %slice.22), channel_id=1, source_target_pairs={{0,1},{1,0},{2,3},{3,2},{4,5},{5,4},{6,7},{7,6},{8,9},{9,8},{10,11... | collective-permute-start | bytes 1179656 | tf_op jit(solution)/shard_map/ppermute | solution.py:212
  247.0 9.0 %collective-permute-start.9 = (bf16[384,512]{1,0:T(8,128)(2,1)S(1)}, bf16[384,512]{1,0:T(8,128)(2,1)S(1)}, u32[]{:S(2)}, u32[]{:S(2)}) collective-permute-start(bf16[384,512]{1,0:T(8,128)(2,1)S(1)} %slice.24), channel_id=1, source_target_pairs={{0,1},{1,0},{2,3},{3,2},{4,5},{5,4},{6,7},{7,6},{8,9},{9,8},{10,11... | collective-permute-start | bytes 1179656 | tf_op jit(solution)/shard_map/ppermute | solution.py:212
  (16 other events, 42.8 us)
Sparse Core Ops, SparseCore 0:
  11.9 99.2 all-gather.1
  146.6 35.7 reduce-scatter.2
  184.9 37.9 reduce-scatter.4

commit v5 on v4

--- a/solution.py
+++ b/solution.py
@@ -288,22 +288,24 @@
         return total(ring_sum[:tok_rows], got)
 
     flip = (lax.axis_index("col") % 2).astype(jnp.int32).reshape(1)
-    out_parts = block_product((2,), flip, cols, weights, (hidden,))
+    their_far = theirs(FAR, cols)
+    got_far = other_core(their_far)
+    out_parts = block_product((2,), flip, after(their_far), weights, (hidden,))
     output = reduce_features(out_parts)
-    their_far = theirs(FAR, after(out_parts))
-    got_far = other_core(their_far)
-    their_near = theirs(NEAR, after(their_far))
+    far0, far1 = mine(FAR, after(out_parts), got_far)
+    far_p, far_m = over_y(far0, 1), over_y(far1, -1)
+    their_near = theirs(NEAR, after(far0))
     got_near = other_core(their_near)
-    far0, far1 = mine(FAR, after(their_near), got_far)
-    far_p, far_m = over_y(far0, 1), over_y(far1, -1)
-    in_parts = block_product((0, 1), flip, after(far0), weights, (gate_delta, up_delta))
-    tokens_grad = reduce_features(in_parts)
-    their_own = theirs(OWN, after(in_parts))
+    their_own = theirs(OWN, after(their_near))
     got_own = other_core(their_own)
     p1, m1, p0, m0 = mine(NEAR, after(their_own), got_near)
-    from_m1, from_p1 = over_y(p1, 1), over_y(total(m1, far_m), -1)
-    from_m0, from_p0 = over_y(total(p0, far_p), 1), over_y(m0, -1)
-    own0, own1 = mine(OWN, after(p1), got_own)
+    m1, p0 = total(m1, far_m), total(p0, far_p)
+    from_m1, from_p1 = over_y(p1, 1), over_y(m1, -1)
+    from_m0, from_p0 = over_y(p0, 1), over_y(m0, -1)
+    ready = lax.optimization_barrier((cols, p1, m1, p0))[0]
+    in_parts = block_product((0, 1), flip, ready, weights, (gate_delta, up_delta))
+    tokens_grad = reduce_features(in_parts)
+    own0, own1 = mine(OWN, lax.optimization_barrier((cols, in_parts, output))[0], got_own)
     last = permute(total(own1, from_m1, from_p1), "row", lambda r: r ^ 2)
     grads = total(own0, from_m0, from_p0, last)
     gate_grad, up_grad, down_grad = (

time: 264 us -> 263 us (level)
  waiting for transfers between devices: 120 us -> 115 us
  local copies, waits for them, and re-layouts: 29.3 us -> 33.1 us
  other arithmetic: 8.74 us -> 12.1 us
    ppermute x19, waiting for transfers between devices: 98.3 us -> 86.5 us  [permute(): lax.ppermute(value, axis, [(i, target(i)) for i in range(lax.axis_size(ax...]
    reduce_scatter x2, waiting for transfers between devices: 0.02 us -> 7.05 us  [reduce_features(): lax.psum_scatter(parts.reshape(-1, parts.shape[2]), 'col', scatter_dimens...]
    unnamed x44 -> x50, local copies, waits for them, and re-layouts: 21.6 us -> 25.6 us
    convert_element_type x6, other arithmetic: 5.33 us -> 8.73 us  [total(): return sum((v.astype(jnp.float32) for v in values)).astype(jnp.bfloat16)]
  transfers between devices with their start and end apart: 22 -> 22, of which waited for: 13 -> 14; matrix products, arithmetic and copies ran while one was open for 7% -> 8% of each run, Pallas kernels for 14% -> 15%
where the time goes in v5:
time: 263 us; the launch traced here: 262 us
  waiting for transfers between devices  115 us (44%)
  Pallas kernels  64.8 us (25%)
  local copies, waits for them, and re-layouts  33.1 us (13%)
  starting transfers between devices  22.7 us (9%)
  between operations  14 us (5%)
  other arithmetic  12.1 us (5%)
    ppermute x19, waiting for transfers between devices, permute(): lax.ppermute(value, axis, [(i, target(i)) for i in range(lax.axis_size(ax...  86.5 us
    unnamed x50, local copies, waits for them, and re-layouts  25.6 us
    pallas_call x6, Pallas kernels, weight_grads(): pl.pallas_call(functools.partial(weight_grads_kernel, scale, 0 if got is...  25.3 us
    ppermute x19, starting transfers between devices, permute(): lax.ppermute(value, axis, [(i, target(i)) for i in range(lax.axis_size(ax...  22.6 us
    all_gather x1, waiting for transfers between devices, body(): lax.all_gather(packed, 'row', axis=0, tiled=True).reshape(n_row, -1, BLK)  21.3 us
    pallas_call x1, Pallas kernels, local_sums(): pl.pallas_call(sums_kernel, out_shape=(out, out, out), grid_spec=pltpu.Pr...  21.1 us
    pallas_call x2, Pallas kernels, block_product(): pl.pallas_call(functools.partial(product_kernel, tensors), out_shape=jax....  18.4 us
    convert_element_type x6, other arithmetic, total(): return sum((v.astype(jnp.float32) for v in values)).astype(jnp.bfloat16)  8.73 us
  transfers between devices with their start and end apart: 22, of which 14 were waited for; matrix products, arithmetic and copies ran while one was open for 8% of the time, Pallas kernels for 15%

profile of v5, /device:TPU:0, one launch (start us, length us, event | category | flops | bytes accessed | tf_op | source)
XLA Modules:
  0.0 261.6 jit_solution(17389368917866991030)
XLA Ops:
  9.6 2.1 fusion.1
  15.4 21.6 %collective-permute-done = bf16[768,512]{1,0:T(8,128)(2,1)S(1)} collective-permute-done((bf16[768,512]{1,0:T(8,128)(2,1)S(1)}, bf16[768,512]{1,0:T(8,128)(2,1)S(1)}, u32[]{:S(2)}, u32[]{:S(2)}) %collective-permute-start) | collective-permute-done | bytes 786464 | tf_op jit(solution)/shard_map/ppermute | solution.py:212
  37.1 2.6 collective-permute-start.2
  44.3 13.4 %collective-permute-done.2 = bf16[768,512]{1,0:T(8,128)(2,1)S(1)} collective-permute-done((bf16[768,512]{1,0:T(8,128)(2,1)S(1)}, bf16[768,512]{1,0:T(8,128)(2,1)S(1)}, u32[]{:S(2)}, u32[]{:S(2)}) %collective-permute-start.2) | collective-permute-done | bytes 786464 | tf_op jit(solution)/shard_map/ppermute | solution.py:212
  57.7 3.7 %collective-permute-start.5 = (bf16[768,512]{1,0:T(8,128)(2,1)S(1)}, bf16[768,512]{1,0:T(8,128)(2,1)S(1)}, u32[]{:S(2)}, u32[]{:S(2)}) collective-permute-start(bf16[768,512]{1,0:T(8,128)(2,1)S(1)} %collective-permute-done.2), channel_id=1, source_target_pairs={{0,6},{1,7},{2,0},{3,1},{4,2},{5,3},{6,4},{7,5},{8,14},{9,15},{10,... | collective-permute-start | bytes 2359304 | tf_op jit(solution)/shard_map/ppermute | solution.py:212
  61.4 13.2 %collective-permute-done.1 = bf16[768,512]{1,0:T(8,128)(2,1)} collective-permute-done((bf16[768,512]{1,0:T(8,128)(2,1)S(1)}, bf16[768,512]{1,0:T(8,128)(2,1)}, u32[]{:S(2)}, u32[]{:S(2)}) %collective-permute-start.1) | collective-permute-done | bytes 786464 | tf_op jit(solution)/shard_map/ppermute | solution.py:212
  74.5 2.1 bitcast_dynamic-update-slice_fusion.5
  78.5 8.5 %collective-permute-done.5 = bf16[768,512]{1,0:T(8,128)(2,1)S(1)} collective-permute-done((bf16[768,512]{1,0:T(8,128)(2,1)S(1)}, bf16[768,512]{1,0:T(8,128)(2,1)S(1)}, u32[]{:S(2)}, u32[]{:S(2)}) %collective-permute-start.5) | collective-permute-done | bytes 786464 | tf_op jit(solution)/shard_map/ppermute | solution.py:212
  89.9 21.3 %all-gather.2.cloned.1.call-done = bf16[49408,128]{1,0:T(8,128)(2,1)} async-done(((bf16[3088,128]{1,0:T(8,128)(2,1)}), bf16[49408,128]{1,0:T(8,128)(2,1)}) %all-gather.2.cloned.1.call-update) | async-done | bytes 12648464 | tf_op jit(solution)/shard_map/all_gather | solution.py:257
  112.6 21.1 %local_sums.1 = (bf16[16,384,128]{2,1,0:T(8,128)(2,1)}, bf16[16,384,128]{2,1,0:T(8,128)(2,1)}, bf16[16,384,128]{2,1,0:T(8,128)(2,1)}) custom-call(s32[8]{0:T(128)} %stack.187.order, s32[384]{0:T(512)} %reshape.113.cols, bf16[8,768,512]{2,1,0:T(8,128)(2,1)} %bitcast_dynamic-update-slice_fusion.x_ref, bf16[16,3088,128]{2,1,0:T(8,128)(2,1)} %bitcast.61), custom_call_target="tpu_custom_call" | custom-call | flops 10000000000 | bytes 30000000 | tf_op jit(solution)/shard_map/local_sums/pallas_call | solution.py:134
  137.9 3.9 %weight_grads.6 = bf16[2,3072,128]{2,1,0:T(8,128)(2,1)} custom-call(s32[2]{0:T(128)S(1)} %get-tuple-element.44.at_x, s32[2]{0:T(128)S(1)} %get-tuple-element.45.owners, s32[384]{0:T(512)S(1)} %copy-done.13, bf16[8,768,512]{2,1,0:T(8,128)(2,1)} %bitcast_dynamic-update-slice_fusion.x_ref, bf16[16,384,128]{2,1,0:T(8,128)(2,1)S(1)} %copy-done, ...), custom_call_target="tpu_custom_call" | custom-call | flops 2000000000 | bytes 6000000 | tf_op jit(solution)/shard_map/weight_grads/pallas_call | solution.py:172
  142.0 7.8 %block_product.2 = bf16[8,384,512]{2,1,0:T(8,128)(2,1)S(1)} custom-call(s32[1]{0:T(128)} %bitcast.flip, s32[384]{0:T(512)S(1)} %copy-done.13, bf16[16,3088,128]{2,1,0:T(8,128)(2,1)} %bitcast.62, bf16[16,384,128]{2,1,0:T(8,128)(2,1)S(1)} %copy-done.1), custom_call_target="tpu_custom_call" | custom-call | flops 3000000000 | bytes 7000000 | tf_op jit(solution)/shard_map/block_product/pallas_call | solution.py:193
  154.4 3.4 %weight_grads.7 = (bf16[3072,128]{1,0:T(8,128)(2,1)S(1)}, bf16[3072,128]{1,0:T(8,128)(2,1)S(1)}) custom-call(s32[2]{0:T(128)S(1)} %get-tuple-element.44.at_x, s32[2]{0:T(128)S(1)} %pad_add_fusion.7.owners, s32[384]{0:T(512)S(1)} %copy-done.13, bf16[8,768,512]{2,1,0:T(8,128)(2,1)} %bitcast_dynamic-update-slice_fusion.x_ref, ...), custom_call_target="tpu_custom_call" | custom-call | flops 2000000000 | bytes 6000000 | tf_op jit(solution)/shard_map/weight_grads/pallas_call | solution.py:172
  159.5 6.0 %weight_grads.8 = bf16[4,3072,128]{2,1,0:T(8,128)(2,1)} custom-call(s32[4]{0:T(128)S(1)} %get-tuple-element.46.at_x, s32[4]{0:T(128)S(1)} %get-tuple-element.47.owners, s32[384]{0:T(512)S(1)} %copy-done.13, bf16[8,768,512]{2,1,0:T(8,128)(2,1)} %bitcast_dynamic-update-slice_fusion.x_ref, bf16[16,384,128]{2,1,0:T(8,128)(2,1)S(1)} %copy-done.1, ...), custom_call_target="tpu_custom_call" | custom-call | flops 4000000000 | bytes 12000000 | tf_op jit(solution)/shard_map/weight_grads/pallas_call | solution.py:172
  169.7 3.0 %weight_grads.9 = bf16[2,3072,128]{2,1,0:T(8,128)(2,1)S(1)} custom-call(s32[2]{0:T(128)S(1)} %get-tuple-element.48.at_x, s32[2]{0:T(128)S(1)} %get-tuple-element.49.owners, s32[384]{0:T(512)S(1)} %copy-done.13, bf16[8,768,512]{2,1,0:T(8,128)(2,1)} %bitcast_dynamic-update-slice_fusion.x_ref, bf16[16,384,128]{2,1,0:T(8,128)(2,1)S(1)} %copy-done.1, ...), custom_call_target="tpu_custom_call" | custom-call | flops 2000000000 | bytes 6000000 | tf_op jit(solution)/shard_map/weight_grads/pallas_call | solution.py:172
  173.8 5.7 %weight_grads.10 = (bf16[3072,128]{1,0:T(8,128)(2,1)S(1)}, bf16[3072,128]{1,0:T(8,128)(2,1)S(1)}, bf16[3072,128]{1,0:T(8,128)(2,1)S(1)}, bf16[3072,128]{1,0:T(8,128)(2,1)S(1)}) custom-call(s32[4]{0:T(128)S(1)} %get-tuple-element.46.at_x, s32[4]{0:T(128)S(1)} %pad_add_fusion.3.owners, s32[384]{0:T(512)S(1)} %copy-done.13, ...), custom_call_target="tpu_custom_call" | custom-call | flops 4000000000 | bytes 12000000 | tf_op jit(solution)/shard_map/weight_grads/pallas_call | solution.py:172
  181.3 4.4 %collective-permute-done.10 = bf16[3072,128]{1,0:T(8,128)(2,1)S(1)} collective-permute-done((bf16[3072,128]{1,0:T(8,128)(2,1)}, bf16[3072,128]{1,0:T(8,128)(2,1)S(1)}, u32[]{:S(2)}, u32[]{:S(2)}) %collective-permute-start.10) | collective-permute-done | bytes 786464 | tf_op jit(solution)/shard_map/ppermute | solution.py:212
  189.0 10.6 %block_product.3 = bf16[8,384,512]{2,1,0:T(8,128)(2,1)S(1)} custom-call(s32[1]{0:T(128)} %bitcast.flip, s32[384]{0:T(512)S(1)} %copy-done.13, bf16[16,3088,128]{2,1,0:T(8,128)(2,1)} %bitcast.63, bf16[16,384,128]{2,1,0:T(8,128)(2,1)S(1)} %copy-done.3, bf16[16,384,128]{2,1,0:T(8,128)(2,1)S(1)} %copy-done.7), custom_call_target="tpu_custom_call" | custom-call | flops 6000000000 | bytes 14000000 | tf_op jit(solution)/shard_map/block_product/pallas_call | solution.py:193
  205.4 8.7 %collective-permute-done.7 = bf16[384,512]{1,0:T(8,128)(2,1)} collective-permute-done((bf16[384,512]{1,0:T(8,128)(2,1)S(1)}, bf16[384,512]{1,0:T(8,128)(2,1)}, u32[]{:S(2)}, u32[]{:S(2)}) %collective-permute-start.7) | collective-permute-done | bytes 393248 | tf_op jit(solution)/shard_map/ppermute | solution.py:212
  219.1 3.4 %weight_grads.11 = (bf16[3072,128]{1,0:T(8,128)(2,1)S(1)}, bf16[3072,128]{1,0:T(8,128)(2,1)S(1)}) custom-call(s32[2]{0:T(128)S(1)} %get-tuple-element.48.at_x, s32[2]{0:T(128)S(1)} %pad_add_fusion.8.owners, s32[384]{0:T(512)S(1)} %copy-done.13, bf16[8,768,512]{2,1,0:T(8,128)(2,1)} %bitcast_dynamic-update-slice_fusion.x_ref, ...), custom_call_target="tpu_custom_call" | custom-call | flops 2000000000 | bytes 6000000 | tf_op jit(solution)/shard_map/weight_grads/pallas_call | solution.py:172
  224.0 2.9 %collective-permute-done.16 = bf16[3072,128]{1,0:T(8,128)(2,1)} collective-permute-done((bf16[3072,128]{1,0:T(8,128)(2,1)}, bf16[3072,128]{1,0:T(8,128)(2,1)}, u32[]{:S(2)}, u32[]{:S(2)}) %collective-permute-start.16) | collective-permute-done | bytes 786464 | tf_op jit(solution)/shard_map/ppermute | solution.py:212
  230.3 7.0 %reduce-scatter.5.cloned.1.call-done = bf16[768,512]{1,0:T(8,128)(2,1)} async-done(((bf16[3072,512]{1,0:T(8,128)(2,1)}), bf16[768,512]{1,0:T(8,128)(2,1)}) %reduce-scatter.5.cloned.1.call-update) | async-done | bytes 786448 | tf_op jit(solution)/shard_map/reduce_scatter | solution.py:283
  240.0 2.6 collective-permute-done.14
  242.6 8.0 %collective-permute-done.18 = bf16[3072,128]{1,0:T(8,128)(2,1)S(1)} collective-permute-done((bf16[3072,128]{1,0:T(8,128)(2,1)S(1)}, bf16[3072,128]{1,0:T(8,128)(2,1)S(1)}, u32[]{:S(2)}, u32[]{:S(2)}) %collective-permute-start.18) | collective-permute-done | bytes 786464 | tf_op jit(solution)/shard_map/ppermute | solution.py:212
  (107 shorter events, 60.8 us)
Async XLA Ops:
  7.2 104.0 %all-gather.2.cloned.1.call-start = ((), (), s32[]{:S(2)}) async-start(), calls=%async_computation.2 | async-start | bytes 13438976 | tf_op jit(solution)/shard_map/all_gather | solution.py:257
  11.7 189.7 %reduce-scatter.3.cloned.1.call-start = ((), (), s32[]{:S(2)}) async-start(), calls=%async_computation.3 | async-start | bytes 3932160 | tf_op jit(solution)/shard_map/reduce_scatter | solution.py:283
  11.9 25.2 %collective-permute-start = (bf16[768,512]{1,0:T(8,128)(2,1)S(1)}, bf16[768,512]{1,0:T(8,128)(2,1)S(1)}, u32[]{:S(2)}, u32[]{:S(2)}) collective-permute-start(bf16[768,512]{1,0:T(8,128)(2,1)S(1)} %constant_dynamic-update-slice_fusion), channel_id=1, source_target_pairs={{0,1},{1,0},{2,3},{3,2},{4,5},{5,4},{6,7},{7,6},{8,9},{9,8},{10,11... | collective-permute-start | bytes 2359304 | tf_op jit(solution)/shard_map/ppermute | solution.py:212
  14.0 29.3 %collective-permute-start.3 = (bf16[768,512]{1,0:T(8,128)(2,1)S(1)}, bf16[768,512]{1,0:T(8,128)(2,1)S(1)}, u32[]{:S(2)}, u32[]{:S(2)}) collective-permute-start(bf16[768,512]{1,0:T(8,128)(2,1)S(1)} %constant_dynamic-update-slice_fusion), channel_id=1, source_target_pairs={{0,2},{1,3},{2,4},{3,5},{4,6},{5,7},{6,0},{7,1},{8,10},{9,11},{10,... | collective-permute-start | bytes 2359304 | tf_op jit(solution)/shard_map/ppermute | solution.py:212
  37.1 20.6 %collective-permute-start.2 = (bf16[768,512]{1,0:T(8,128)(2,1)S(1)}, bf16[768,512]{1,0:T(8,128)(2,1)S(1)}, u32[]{:S(2)}, u32[]{:S(2)}) collective-permute-start(bf16[768,512]{1,0:T(8,128)(2,1)S(1)} %collective-permute-done), channel_id=1, source_target_pairs={{0,6},{1,7},{2,0},{3,1},{4,2},{5,3},{6,4},{7,5},{8,14},{9,15},{10,... | collective-permute-start | bytes 2359304 | tf_op jit(solution)/shard_map/ppermute | solution.py:212
  39.7 34.9 %collective-permute-start.1 = (bf16[768,512]{1,0:T(8,128)(2,1)S(1)}, bf16[768,512]{1,0:T(8,128)(2,1)}, u32[]{:S(2)}, u32[]{:S(2)}) collective-permute-start(bf16[768,512]{1,0:T(8,128)(2,1)S(1)} %constant_dynamic-update-slice_fusion), channel_id=1, source_target_pairs={{0,6},{1,7},{2,0},{3,1},{4,2},{5,3},{6,4},{7,5},{8,14},{9,15},{10,... | collective-permute-start | bytes 2359304 | tf_op jit(solution)/shard_map/ppermute | solution.py:212
  42.1 46.8 %collective-permute-start.6 = (bf16[768,512]{1,0:T(8,128)(2,1)S(1)}, bf16[768,512]{1,0:T(8,128)(2,1)S(1)}, u32[]{:S(2)}, u32[]{:S(2)}) collective-permute-start(bf16[768,512]{1,0:T(8,128)(2,1)S(1)} %collective-permute-done), channel_id=1, source_target_pairs={{0,2},{1,3},{2,4},{3,5},{4,6},{5,7},{6,0},{7,1},{8,10},{9,11},{10,... | collective-permute-start | bytes 2359304 | tf_op jit(solution)/shard_map/ppermute | solution.py:212
  43.3 34.3 %collective-permute-start.4 = (bf16[768,512]{1,0:T(8,128)(2,1)S(1)}, bf16[768,512]{1,0:T(8,128)(2,1)S(1)}, u32[]{:S(2)}, u32[]{:S(2)}) collective-permute-start(bf16[768,512]{1,0:T(8,128)(2,1)S(1)} %collective-permute-done.3), channel_id=1, source_target_pairs={{0,2},{1,3},{2,4},{3,5},{4,6},{5,7},{6,0},{7,1},{8,10},{9,11},{10,... | collective-permute-start | bytes 2359304 | tf_op jit(solution)/shard_map/ppermute | solution.py:212
  57.7 29.3 %collective-permute-start.5 = (bf16[768,512]{1,0:T(8,128)(2,1)S(1)}, bf16[768,512]{1,0:T(8,128)(2,1)S(1)}, u32[]{:S(2)}, u32[]{:S(2)}) collective-permute-start(bf16[768,512]{1,0:T(8,128)(2,1)S(1)} %collective-permute-done.2), channel_id=1, source_target_pairs={{0,6},{1,7},{2,0},{3,1},{4,2},{5,3},{6,4},{7,5},{8,14},{9,15},{10,... | collective-permute-start | bytes 2359304 | tf_op jit(solution)/shard_map/ppermute | solution.py:212
  112.6 21.1 %copy-start.13 = (s32[384]{0:T(512)S(1)}, s32[384]{0:T(512)}, u32[]{:S(2)}) copy-start(s32[384]{0:T(512)} %reshape.113.cols) | copy-start | bytes 4612
  141.8 9.9 %collective-permute-start.8 = (bf16[2,3072,128]{2,1,0:T(8,128)(2,1)}, bf16[2,3072,128]{2,1,0:T(8,128)(2,1)}, u32[]{:S(2)}, u32[]{:S(2)}) collective-permute-start(bf16[2,3072,128]{2,1,0:T(8,128)(2,1)} %weight_grads.6), channel_id=1, source_target_pairs={{0,8},{8,0},{16,24},{24,16},{32,40},{40,32},{48,56},{56,48},{64,72... | collective-permute-start | bytes 4718600 | tf_op jit(solution)/shard_map/ppermute | solution.py:212
  151.6 85.8 %reduce-scatter.5.cloned.1.call-start = ((), (), s32[]{:S(2)}) async-start(), calls=%async_computation.4 | async-start | bytes 3932160 | tf_op jit(solution)/shard_map/reduce_scatter | solution.py:283
  165.5 8.3 %collective-permute-start.9 = (bf16[4,3072,128]{2,1,0:T(8,128)(2,1)}, bf16[4,3072,128]{2,1,0:T(8,128)(2,1)}, u32[]{:S(2)}, u32[]{:S(2)}) collective-permute-start(bf16[4,3072,128]{2,1,0:T(8,128)(2,1)} %weight_grads.8), channel_id=1, source_target_pairs={{0,8},{8,0},{16,24},{24,16},{32,40},{40,32},{48,56},{56,48},{64,72... | collective-permute-start | bytes 9437192 | tf_op jit(solution)/shard_map/ppermute | solution.py:212
  165.8 19.9 %collective-permute-start.10 = (bf16[3072,128]{1,0:T(8,128)(2,1)}, bf16[3072,128]{1,0:T(8,128)(2,1)S(1)}, u32[]{:S(2)}, u32[]{:S(2)}) collective-permute-start(bf16[3072,128]{1,0:T(8,128)(2,1)} %copy-done.15), channel_id=1, source_target_pairs={{0,96},{8,104},{16,112},{24,120},{32,0},{40,8},{48,16},{56,24},{64... | collective-permute-start | bytes 2359304 | tf_op jit(solution)/shard_map/ppermute | solution.py:212
  166.9 21.0 %collective-permute-start.11 = (bf16[3072,128]{1,0:T(8,128)(2,1)}, bf16[3072,128]{1,0:T(8,128)(2,1)S(1)}, u32[]{:S(2)}, u32[]{:S(2)}) collective-permute-start(bf16[3072,128]{1,0:T(8,128)(2,1)} %copy-done.14), channel_id=1, source_target_pairs={{0,32},{8,40},{16,48},{24,56},{32,64},{40,72},{48,80},{56,88},{64,... | collective-permute-start | bytes 2359304 | tf_op jit(solution)/shard_map/ppermute | solution.py:212
  201.3 16.4 %collective-permute-start.13 = (bf16[2,3072,128]{2,1,0:T(8,128)(2,1)}, bf16[2,3072,128]{2,1,0:T(8,128)(2,1)}, u32[]{:S(2)}, u32[]{:S(2)}) collective-permute-start(bf16[2,3072,128]{2,1,0:T(8,128)(2,1)} %copy-done.11), channel_id=1, source_target_pairs={{0,8},{8,0},{16,24},{24,16},{32,40},{40,32},{48,56},{56,48},{64,72... | collective-permute-start | bytes 4718600 | tf_op jit(solution)/shard_map/ppermute | solution.py:212
  202.4 11.7 %collective-permute-start.7 = (bf16[384,512]{1,0:T(8,128)(2,1)S(1)}, bf16[384,512]{1,0:T(8,128)(2,1)}, u32[]{:S(2)}, u32[]{:S(2)}) collective-permute-start(bf16[384,512]{1,0:T(8,128)(2,1)S(1)} %slice.22), channel_id=1, source_target_pairs={{0,1},{1,0},{2,3},{3,2},{4,5},{5,4},{6,7},{7,6},{8,9},{9,8},{10,11... | collective-permute-start | bytes 1179656 | tf_op jit(solution)/shard_map/ppermute | solution.py:212
  203.3 20.7 %collective-permute-start.17 = (bf16[3072,128]{1,0:T(8,128)(2,1)}, bf16[3072,128]{1,0:T(8,128)(2,1)}, u32[]{:S(2)}, u32[]{:S(2)}) collective-permute-start(bf16[3072,128]{1,0:T(8,128)(2,1)} %add_convert_fusion.3), channel_id=1, source_target_pairs={{0,96},{8,104},{16,112},{24,120},{32,0},{40,8},{48,16},{56,24},{64... | collective-permute-start | bytes 2359304 | tf_op jit(solution)/shard_map/ppermute | solution.py:212
  204.9 21.9 %collective-permute-start.16 = (bf16[3072,128]{1,0:T(8,128)(2,1)}, bf16[3072,128]{1,0:T(8,128)(2,1)}, u32[]{:S(2)}, u32[]{:S(2)}) collective-permute-start(bf16[3072,128]{1,0:T(8,128)(2,1)} %copy-done.17), channel_id=1, source_target_pairs={{0,32},{8,40},{16,48},{24,56},{32,64},{40,72},{48,80},{56,88},{64,... | collective-permute-start | bytes 2359304 | tf_op jit(solution)/shard_map/ppermute | solution.py:212
  205.4 37.2 %collective-permute-start.14 = (bf16[3072,128]{1,0:T(8,128)(2,1)}, bf16[3072,128]{1,0:T(8,128)(2,1)}, u32[]{:S(2)}, u32[]{:S(2)}) collective-permute-start(bf16[3072,128]{1,0:T(8,128)(2,1)} %add_convert_fusion.2), channel_id=1, source_target_pairs={{0,32},{8,40},{16,48},{24,56},{32,64},{40,72},{48,80},{56,88},{64,... | collective-permute-start | bytes 2359304 | tf_op jit(solution)/shard_map/ppermute | solution.py:212
  214.1 28.5 %collective-permute-start.15 = (bf16[3072,128]{1,0:T(8,128)(2,1)}, bf16[3072,128]{1,0:T(8,128)(2,1)}, u32[]{:S(2)}, u32[]{:S(2)}) collective-permute-start(bf16[3072,128]{1,0:T(8,128)(2,1)} %copy-done.16), channel_id=1, source_target_pairs={{0,96},{8,104},{16,112},{24,120},{32,0},{40,8},{48,16},{56,24},{64... | collective-permute-start | bytes 2359304 | tf_op jit(solution)/shard_map/ppermute | solution.py:212
  222.6 6.0 %copy-start.12 = (bf16[3072,128]{1,0:T(8,128)(2,1)}, bf16[3072,128]{1,0:T(8,128)(2,1)S(1)}, u32[]{:S(2)}) copy-start(bf16[3072,128]{1,0:T(8,128)(2,1)S(1)} %get-tuple-element.38) | copy-start | bytes 2359300
  228.6 22.1 %collective-permute-start.18 = (bf16[3072,128]{1,0:T(8,128)(2,1)S(1)}, bf16[3072,128]{1,0:T(8,128)(2,1)S(1)}, u32[]{:S(2)}, u32[]{:S(2)}) collective-permute-start(bf16[3072,128]{1,0:T(8,128)(2,1)S(1)} %add_convert_fusion.1), channel_id=1, source_target_pairs={{0,16},{8,24},{16,0},{24,8},{32,48},{40,56},{48,32},{56,40},{64,80... | collective-permute-start | bytes 2359304 | tf_op jit(solution)/shard_map/ppermute | solution.py:212
  238.4 15.8 %collective-permute-start.12 = (bf16[384,512]{1,0:T(8,128)(2,1)S(1)}, bf16[384,512]{1,0:T(8,128)(2,1)S(1)}, u32[]{:S(2)}, u32[]{:S(2)}) collective-permute-start(bf16[384,512]{1,0:T(8,128)(2,1)S(1)} %slice.24), channel_id=1, source_target_pairs={{0,1},{1,0},{2,3},{3,2},{4,5},{5,4},{6,7},{7,6},{8,9},{9,8},{10,11... | collective-permute-start | bytes 1179656 | tf_op jit(solution)/shard_map/ppermute | solution.py:212
  (19 other events, 32.8 us)
Sparse Core Ops, SparseCore 0:
  11.9 99.2 all-gather.1
  151.7 35.7 reduce-scatter.2
  201.4 35.9 reduce-scatter.4
